TPU v7x, 32 devices: a whole 2x2x4 slice. The times are simulated.
32 devices in a mesh: frame: 4 (over y, core), slab: 8 (over z, x).
Axes of the slice: x: 2, y: 2, z: 4, core: 2. Of those that a mesh axis runs over, the one named last changes fastest.
Arguments:
- element_data: bfloat16 [1024, 4, 512], P('slab', 'frame'), may hold values from -6 to 6
- migration: bfloat16 [2048, 1024], replicated, may hold values from -0.1875 to 0.1875
- column_gain: float32 [2048], replicated, may hold values from 0.3 to 3
- depth_gain: float32 [512], P('slab'), may hold values from 0.3 to 3
- coarse_shift: int32 [3, 4, 4, 8, 32], P(None, 'frame', None, None, 'slab'), may hold values from -8 to 8
- reference_frame: int32 [4], replicated, may hold values from 0 to 3, each once
Outputs:
- scores: float32 [7, 4, 4, 8, 32], P(None, 'frame', None, None, 'slab')
- displacement: float32 [3, 4, 4, 8, 32], P(None, 'frame', None, None, 'slab')
Inputs may be any that keep to these rules, and one draw needn't show every extreme that they name: `reference_frame`: each frame index appears exactly once; the first entry names the reference frame, which serves all blocks.
All inputs are finite; a program needn't handle non-finite values.
Results may differ from a plain program's by a relative error of at most 0.0039.
Values may be sent and summed in bfloat16 or wider, within the bound.
No kernel may reach another device: no remote copies, remote signals or barrier semaphores. Data moves between devices by JAX's collectives and lax.ppermute only.
A program may use at most 64 MiB of HBM per device.

v0:
```python
import math

import jax
import jax.numpy as jnp
from jax import lax
from jax.sharding import PartitionSpec as P

LX = 32
LY = 64
KX = 8
KY = 8
KZ = 16
CMAX = 8


epsilon = 1e-05
shift_table = ((0, 0, 0), (-1, 0, 0), (1, 0, 0), (0, -1, 0), (0, 1, 0), (0, 0, -1), (0, 0, 1))


def spread(value, axis, source):
    kept = jnp.where(lax.axis_index(axis) == source, value, 0).astype(value.dtype)
    return lax.psum(kept, axis)


def padded_2(array, sides, width):
    for axis, dim in sides:
        devices, length = (lax.axis_size(axis), array.shape[dim])
        up = [(i, (i + 1) % devices) for i in range(devices - 1)]
        down = [(j, i) for i, j in up]
        last = lax.slice_in_dim(array, length - width, length, axis=dim)
        initial = lax.slice_in_dim(array, 0, width, axis=dim)
        before = lax.ppermute(last, axis, up)
        after = lax.ppermute(initial, axis, down)
        array = jnp.concatenate([before, array, after], axis=dim)
    return array


def migrate(pieces, migration, column_gain, depth_gain):
    elements, items, depth_count = pieces.shape
    flattened = pieces.reshape(elements, items * depth_count)
    raw_image = jnp.dot(migration, flattened, preferred_element_type=jnp.float32)
    raw_image = raw_image.reshape(migration.shape[0], items, depth_count)
    scaled = raw_image * column_gain[:, None, None] * depth_gain[None, None, :]
    return scaled.astype(jnp.bfloat16)


def block_scores(kernels, padded, starts):
    kernel_shape = kernels.shape[1:]
    box_shape = (kernel_shape[0] + 2, kernel_shape[1] + 2, kernel_shape[2] + 2)

    def take_box(first, second, third):
        return lax.dynamic_slice(padded, (first - 1, second - 1, third - 1), box_shape)

    boxes = jax.vmap(take_box)(starts[0], starts[1], starts[2])
    cell_count = kernel_shape[0] * kernel_shape[1] * kernel_shape[2]
    kernel_float = kernels.astype(jnp.float32)
    kernel_power = jnp.mean(kernel_float * kernel_float, axis=(1, 2, 3))
    results = []
    for shift_step in shift_table:
        low = [1 + shift_step[dimension] for dimension in range(3)]
        window = boxes[
            :,
            low[0] : low[0] + kernel_shape[0],
            low[1] : low[1] + kernel_shape[1],
            low[2] : low[2] + kernel_shape[2],
        ].astype(jnp.float32)
        cross_mean = jnp.mean(kernel_float * window, axis=(1, 2, 3))
        window_power = jnp.mean(window * window, axis=(1, 2, 3))
        results.append(
            math.sqrt(cell_count)
            * cross_mean
            / jnp.sqrt((kernel_power + epsilon) * (window_power + epsilon))
        )
    return jnp.stack(results)


def refine(scores, shifts):
    refined = []
    for dimension in range(3):
        lower_score = scores[1 + 2 * dimension]
        upper_score = scores[2 + 2 * dimension]
        curvature = jnp.maximum(2.0 * scores[0] - lower_score - upper_score, 1.0)
        refined.append(
            shifts[dimension].astype(jnp.float32) + (upper_score - lower_score) / (2.0 * curvature)
        )
    return jnp.stack(refined)


def per_device(element_data, migration, column_gain, depth_gain, coarse_shift, reference_frame):
    frames_here = element_data.shape[1]
    depth_here = depth_gain.shape[0]
    margin = CMAX + 1
    chosen = reference_frame[0]
    owner_index = chosen // frames_here
    position = chosen % frames_here
    images = migrate(
        lax.all_to_all(element_data, "slab", split_axis=2, concat_axis=0, tiled=True),
        migration,
        column_gain,
        depth_gain,
    )
    candidate = lax.dynamic_index_in_dim(images, position, 1, keepdims=False)
    volume = spread(candidate, "frame", owner_index)
    lattice = volume.reshape(LX, LY, depth_here)
    extended = padded_2(lattice, (("slab", 2),), margin)
    padded = jnp.pad(extended, ((margin, margin), (margin, margin), (0, 0)))
    kernel_shape = (KX, KY, KZ)
    block_counts = (LX // KX, LY // KY, depth_here // KZ)
    arranged = images.reshape(
        block_counts[0], KX, block_counts[1], KY, frames_here, block_counts[2], KZ
    )
    kernels = arranged.transpose(4, 0, 2, 5, 1, 3, 6).reshape(frames_here, -1, KX, KY, KZ)
    layout = (frames_here, block_counts[0], block_counts[1], block_counts[2])
    block_index = [
        lax.broadcasted_iota(jnp.int32, layout, dimension + 1).reshape(frames_here, -1)
        for dimension in range(3)
    ]
    shifts = coarse_shift.reshape(3, frames_here, -1)
    starts = jnp.stack(
        [
            block_index[dimension] * kernel_shape[dimension] + shifts[dimension] + margin
            for dimension in range(3)
        ]
    )
    frame_starts = starts.transpose(1, 0, 2)

    def per_frame(inputs):
        frame_kernels, frame_start = inputs
        return block_scores(frame_kernels, padded, [frame_start[0], frame_start[1], frame_start[2]])

    framed = lax.map(per_frame, (kernels, frame_starts))
    scores = framed.transpose(1, 0, 2).reshape(7, -1)
    displacement = refine(scores, shifts.reshape(3, -1))
    return (scores.reshape((7,) + layout), displacement.reshape((3,) + layout))


def solution(mesh):
    placed = (
        P("slab", "frame", None),
        P(),
        P(),
        P("slab"),
        P(None, "frame", None, None, "slab"),
        P(),
    )
    return jax.shard_map(
        per_device,
        mesh=mesh,
        in_specs=placed,
        out_specs=(P(None, "frame", None, None, "slab"), P(None, "frame", None, None, "slab")),
        check_vma=False,
    )
```

profile of v0, /device:TPU:0, one launch (start us, length us, event | category | flops | bytes accessed | tf_op | source)
XLA Modules:
  0.0 548.9 jit_solution(10297995893335371396)
XLA Ops:
  10.8 7.3 %all-to-all-start = ((bf16[8,2,4096]{2,1,0:T(2,128)(2,1)}), bf16[8,2,4096]{2,1,0:T(2,128)(2,1)S(1)}, u32[]{:S(2)}, u32[]{:S(2)}) async-start(bf16[8,2,4096]{2,1,0:T(2,128)(2,1)} %reshape.756), calls=%async_computation | async-start | bytes 262144 | tf_op jit(solution)/shard_map/all_to_all | solution.py:97
  20.6 4.9 all-to-all-done
  25.7 3.6 broadcast_select_fusion
  30.7 3.3 mul.491
  34.0 3.1 reduce_sum.151
  37.1 24.6 %all-reduce.3.cloned.1.call-done = bf16[32,64,64]{2,1,0:T(8,128)(2,1)} async-done(((bf16[32,64,64]{2,1,0:T(8,128)(2,1)}), bf16[32,64,64]{2,1,0:T(8,128)(2,1)}) %all-reduce.3.cloned.1.call-update) | async-done | bytes 262160 | tf_op jit(solution)/shard_map/psum | solution.py:22
  64.0 3.4 collective-permute-start
  69.1 3.3 reshape.755
  72.4 4.9 copy.60
  77.5 11.6 %collective-permute-done = bf16[32,64,9]{2,1,0:T(8,128)(2,1)S(1)} collective-permute-done((bf16[32,64,9]{2,1,0:T(8,128)(2,1)}, bf16[32,64,9]{2,1,0:T(8,128)(2,1)S(1)}, u32[]{:S(2)}, u32[]{:S(2)}) %collective-permute-start) | collective-permute-done | bytes 36896 | tf_op jit(solution)/shard_map/ppermute | solution.py:32
  90.1 425.3 %while.1 = (s32[]{:T(128)}, bf16[50,82,82]{2,1,0:T(8,128)(2,1)S(1)}, s32[128,3]{0,1:T(4,128)S(1)}, bf16[128,10,10,18]{3,2,1,0:T(8,128)(2,1)}, s32[]{:T(128)}) while((s32[]{:T(128)}, bf16[50,82,82]{2,1,0:T(8,128)(2,1)S(1)}, s32[128,3]{0,1:T(4,128)S(1)}, bf16[128,10,10,18]{3,2,1,0:T(8,128)(2,1)}, s32[]{:T(128)}) %tuple.57), condition=%wide.while_cond, body=%wide.while_body.sunk | while | flops 2 | bytes 46721 | solution.py:52
  124.0 2.7 bitcast_dynamic-update-slice_fusion.2
  250.2 2.7 bitcast_dynamic-update-slice_fusion.2
  253.5 2.7 bitcast_dynamic-update-slice_fusion.2
  263.5 2.7 bitcast_dynamic-update-slice_fusion.2
  286.8 2.7 bitcast_dynamic-update-slice_fusion.2
  320.0 2.7 bitcast_dynamic-update-slice_fusion.2
  389.8 2.7 bitcast_dynamic-update-slice_fusion.2
  433.0 2.7 bitcast_dynamic-update-slice_fusion.2
  466.2 2.7 bitcast_dynamic-update-slice_fusion.2
  476.2 2.7 bitcast_dynamic-update-slice_fusion.2
  492.8 2.7 bitcast_dynamic-update-slice_fusion.2
  506.1 2.7 bitcast_dynamic-update-slice_fusion.2
  515.4 23.2 %fusion.13 = (f32[128]{0:T(128)S(1)}, f32[128]{0:T(128)S(1)}, f32[128]{0:T(128)S(1)}, f32[128]{0:T(128)S(1)}, f32[128]{0:T(128)S(1)}, /*index=5*/f32[128]{0:T(12...) fusion(bf16[128,10,10,18]{3,2,1,0:T(8,128)(2,1)} %get-tuple-ele, ...), kind=kLoop, calls=%fused_computation.29 | loop fusion | flops 4585728 | bytes 2366464 | tf_op jit(solution)/shard_map/while/body/eval_jaxpr/reduce_sum | solution.py:68
  (450 shorter events, 408.3 us)
Async XLA Ops:
  10.8 14.6 %all-to-all-start = ((bf16[8,2,4096]{2,1,0:T(2,128)(2,1)}), bf16[8,2,4096]{2,1,0:T(2,128)(2,1)S(1)}, u32[]{:S(2)}, u32[]{:S(2)}) async-start(bf16[8,2,4096]{2,1,0:T(2,128)(2,1)} %reshape.756), calls=%async_computation | async-start | bytes 262144 | tf_op jit(solution)/shard_map/all_to_all | solution.py:97
  18.1 43.6 %all-reduce.3.cloned.1.call-start = ((), (), s32[]{:S(2)}) async-start(), calls=%async_computation.1 | async-start | bytes 1048576 | tf_op jit(solution)/shard_map/psum | solution.py:22
  64.0 25.1 %collective-permute-start = (bf16[32,64,9]{2,1,0:T(8,128)(2,1)}, bf16[32,64,9]{2,1,0:T(8,128)(2,1)S(1)}, u32[]{:S(2)}, u32[]{:S(2)}) collective-permute-start(bf16[32,64,9]{2,1,0:T(8,128)(2,1)} %get-tuple-element.67), channel_id=1, source_target_pairs={{0,1},{1,2},{2,3},{3,4},{4,5},{5,6},{6,7},{8,9},{9,10},{10,11},{11... | collective-permute-start | bytes 110600 | tf_op jit(solution)/shard_map/ppermute | solution.py:32
  67.4 21.7 %collective-permute-start.1 = (bf16[32,64,9]{2,1,0:T(8,128)(2,1)S(1)}, bf16[32,64,9]{2,1,0:T(8,128)(2,1)S(1)}, u32[]{:S(2)}, u32[]{:S(2)}) collective-permute-start(bf16[32,64,9]{2,1,0:T(8,128)(2,1)S(1)} %get-tuple-element.68), channel_id=1, source_target_pairs={{1,0},{2,1},{3,2},{4,3},{5,4},{6,5},{7,6},{9,8},{10,9},{11,10},{12... | collective-permute-start | bytes 110600 | tf_op jit(solution)/shard_map/ppermute | solution.py:33
  72.4 16.7 %copy-start = (bf16[32,64,64]{2,1,0:T(8,128)(2,1)S(1)}, bf16[32,64,64]{2,1,0:T(8,128)(2,1)}, u32[]{:S(2)}) copy-start(bf16[32,64,64]{2,1,0:T(8,128)(2,1)} %all-reduce.3.cloned.1.call-done) | copy-start | bytes 786436
Sparse Core Ops, SparseCore 0:
  30.5 31.2 all-reduce.2
where the time goes:
time: 553 us; the launch traced here: 549 us
  local copies, waits for them, and re-layouts  448 us (81%)
  waiting for transfers between devices  41.2 us (7%)
  other arithmetic  28.9 us (5%)
  between operations  15.1 us (3%)
  starting transfers between devices  12.2 us (2%)
    gather x384, local copies, waits for them, and re-layouts  425 us
    psum x1, waiting for transfers between devices, spread(): return lax.psum(kept, axis)  24.6 us
    reduce_sum x1, other arithmetic, block_scores(): window_power = jnp.mean(window * window, axis=(1, 2, 3))  23.2 us
    ppermute x1, waiting for transfers between devices, padded_2(): before = lax.ppermute(last, axis, up)  11.6 us
  transfers between devices with their start and end apart: 4, of which 3 were waited for; matrix products, arithmetic and copies ran while one was open for 3% of the time, Pallas kernels for 0%

commit v1 on v0

v1 whole, which is shorter than its diff:
```python
import functools
import math

import jax
import jax.numpy as jnp
from jax import lax
from jax.experimental import pallas as pl
from jax.experimental.pallas import tpu as pltpu
from jax.sharding import PartitionSpec as P

LX = 32
LY = 64
KX = 8
KY = 8
KZ = 16
CMAX = 8
MARGIN = CMAX + 1
EPSILON = 1e-05

LANES = 128
STEP = 64
EDGE = 16
WINDOW = STEP + 2 * EDGE
SEGMENT = 32
PACKED = STEP // KZ
BX = LX // KX
BY = LY // KY
GROUPS = BX * BY
NX = LX + 2 * MARGIN
NY = LY + 2 * EDGE
KROWS = 8 + 2 * LY + 8
CELLS = KX * KY * KZ
CHUNK = 256


def pieces_of(value):
    high = lax.reduce_precision(value, 8, 7)
    middle = lax.reduce_precision(value - high, 8, 7)
    low = value - high - middle
    return [part.astype(jnp.bfloat16) for part in (high, middle, low)]


def track(
    choice,
    shift,
    own,
    kept,
    received,
    migration,
    column_gain,
    depth_gain,
    shift_cells,
    scores,
    displacement,
    samples,
    volume,
    kernels,
    sums,
):
    part = pl.program_id(0)
    blocks = own.shape[0]

    samples[...] = jnp.zeros(samples.shape, jnp.bfloat16)
    keep = choice[0] == 1
    for block in range(blocks):
        lanes = slice(block * LANES, (block + 1) * LANES)
        for j in range(PACKED):
            samples[j * SEGMENT : j * SEGMENT + KZ, lanes] = own[
                block, EDGE + j * KZ : EDGE + (j + 1) * KZ, :
            ]

    @pl.when(keep)
    def _():
        for block in range(blocks):
            lanes = slice(block * LANES, (block + 1) * LANES)
            samples[LANES : LANES + WINDOW, lanes] = kept[block]

    @pl.when(jnp.logical_not(keep))
    def _():
        for block in range(blocks):
            lanes = slice(block * LANES, (block + 1) * LANES)
            samples[LANES : LANES + WINDOW, lanes] = received[block]

    lane = lax.broadcasted_iota(jnp.int32, (8, LANES), 1)
    depth_row = jnp.broadcast_to(depth_gain[0], (8, LANES))
    own_row = pltpu.roll(depth_row, LANES - EDGE, 1)
    for j in range(1, PACKED):
        moved = pltpu.roll(depth_row, (j * KZ - EDGE) % LANES, 1)
        own_row = jnp.where(lane >= j * SEGMENT, moved, own_row)
    columns = jnp.transpose(column_gain[...])

    zero = jnp.zeros((NY, LANES), jnp.float32)
    for x in list(range(MARGIN)) + list(range(LX + MARGIN, NX)):
        volume[x * NY : (x + 1) * NY, :] = zero
    for x in range(LX):
        base = (x + MARGIN) * NY
        volume[base : base + EDGE, :] = zero[:EDGE]
        volume[base + EDGE + LY : base + NY, :] = zero[:EDGE]
        for by in range(BY + 1):
            kernels[x * KROWS + by * 16 : x * KROWS + by * 16 + 8, :] = zero[:8]

    right = samples[...]
    for chunk in range(LX * LY // CHUNK):
        raw = lax.dot_general(
            migration[chunk * CHUNK : (chunk + 1) * CHUNK, :],
            right,
            (((1,), (1,)), ((), ())),
            preferred_element_type=jnp.float32,
        )
        for piece in range(CHUNK // LY):
            x = chunk * (CHUNK // LY) + piece
            row = x * LY
            gain = columns[row % LANES : row % LANES + LY, row // LANES : row // LANES + 1]
            gain = jnp.broadcast_to(gain, (LY, LANES))
            mine = raw[piece * LY : (piece + 1) * LY, :LANES]
            reference = raw[piece * LY : (piece + 1) * LY, LANES:]
            mine = (mine * gain) * own_row[:1]
            reference = (reference * gain) * depth_row[:1]
            mine = mine.astype(jnp.bfloat16).astype(jnp.float32)
            reference = reference.astype(jnp.bfloat16).astype(jnp.float32)
            base = (x + MARGIN) * NY + EDGE
            volume[base : base + LY, :] = reference
            for by in range(BY):
                row = x * KROWS + 8 + by * 16
                kernels[row : row + 8, :] = mine[by * KY : (by + 1) * KY]

    place = lax.broadcasted_iota(jnp.int32, (8, LANES), 1)
    place = (place + 8) % LANES // SEGMENT
    segment = [place == j for j in range(PACKED)]
    row_number = lax.broadcasted_iota(jnp.int32, (8, LANES), 0)

    def group(g, carry):
        bx = g // BY
        by = g % BY
        starts = []
        turns = []
        for j in range(PACKED):
            bz = part * PACKED + j
            first = bx * KX + MARGIN + shift[0, 0, bx, by, bz]
            second = by * KY + EDGE + shift[1, 0, bx, by, bz]
            starts.append(first * NY + second)
            turns.append((j * KZ - EDGE + 2 * LANES - shift[2, 0, bx, by, bz]) % LANES)

        def gather(offset, stride):
            value = None
            for j in range(PACKED):
                start = starts[j] + offset
                if stride == 1:
                    rows = volume[pl.ds(start, 8), :]
                else:
                    rows = volume[pl.ds(start, 8, stride=stride), :]
                rows = pltpu.roll(rows, turns[j], 1)
                value = rows if value is None else jnp.where(segment[j], rows, value)
            return value

        base = bx * KX * KROWS + by * 16 + 8
        window = [gather((x - 1) * NY, 1) for x in range(KX + 2)]
        square = [value * value for value in window]
        middle = square[2]
        for x in range(3, KX):
            middle = middle + square[x]
        pair_low = square[0] + square[1]
        pair_high = square[KX] + square[KX + 1]
        center = middle + (square[1] + square[KX])
        cross = [None] * 7
        power = None

        def add(index, value):
            cross[index] = value if cross[index] is None else cross[index] + value

        for x in range(KX):
            row = base + x * KROWS
            kernel = kernels[pl.ds(row, 8), :]
            add(0, kernel * window[x + 1])
            add(1, kernel * window[x])
            add(2, kernel * window[x + 2])
            add(3, kernels[pl.ds(row + 1, 8), :] * window[x + 1])
            add(4, kernels[pl.ds(row - 1, 8), :] * window[x + 1])
            add(5, pltpu.roll(kernel, LANES - 1, 1) * window[x + 1])
            add(6, pltpu.roll(kernel, 1, 1) * window[x + 1])
            power = kernel * kernel if power is None else power + kernel * kernel
        before = gather(-1, NY)
        after = gather(KY, NY)
        add(3, kernels[pl.ds(base, 8, stride=KROWS), :] * before)
        add(4, kernels[pl.ds(base + KY - 1, 8, stride=KROWS), :] * after)
        low = jnp.where(row_number < KY - 1, center, 0.0) + before * before
        high = jnp.where(row_number > 0, center, 0.0) + after * after
        held = cross + [center, middle + pair_low, middle + pair_high, low, high, power]
        for index, value in enumerate(held):
            sums[index, pl.ds(g * 8, 8), :] = value
        return carry

    lax.fori_loop(0, GROUPS, group, 0)

    def total(index, bx):
        value = None
        for y in range(KY):
            rows = sums[index, pl.ds(bx * BY * 8 + y, BY, stride=8), :]
            value = rows if value is None else value + rows
        for width in (1, 2, 4, 8):
            value = value + pltpu.roll(value, LANES - width, 1)
        return value

    def compress(value):
        result = value
        for j in range(1, PACKED):
            result = jnp.where(lane == j, pltpu.roll(value, LANES - j * (SEGMENT - 1), 1), result)
        return result[:, :PACKED]

    for bx in range(BX):
        cross = [total(index, bx) for index in range(7)]
        cross[5] = pltpu.roll(cross[5], 1, 1)
        cross[6] = pltpu.roll(cross[6], LANES - 1, 1)
        center = total(7, bx)
        powers = [center] + [total(index, bx) for index in range(8, 12)]
        powers += [pltpu.roll(center, 1, 1), pltpu.roll(center, LANES - 1, 1)]
        kernel_power = total(12, bx) * (1.0 / CELLS) + EPSILON
        result = []
        for index in range(7):
            mean = cross[index] * (1.0 / CELLS)
            window_power = powers[index] * (1.0 / CELLS) + EPSILON
            result.append(
                compress(math.sqrt(CELLS) * mean / jnp.sqrt(kernel_power * window_power))
            )
            scores[index, 0, bx] = result[index]
        for axis in range(3):
            lower = result[1 + 2 * axis]
            upper = result[2 + 2 * axis]
            curvature = jnp.maximum(2.0 * result[0] - lower - upper, 1.0)
            cells = shift_cells[axis, 0, bx].astype(jnp.float32)
            displacement[axis, 0, bx] = cells + (upper - lower) / (2.0 * curvature)


def per_device(element_data, migration, column_gain, depth_gain, coarse_shift, reference_frame):
    elements_here, _, depth = element_data.shape
    depth_here = depth_gain.shape[0]
    slabs = lax.axis_size("slab")
    frames = lax.axis_size("frame")
    parts = depth_here // STEP
    chosen = reference_frame[0]
    frame = lax.axis_index("frame")
    slab = lax.axis_index("slab")

    turned = jnp.pad(element_data[:, 0, :].T, ((EDGE, EDGE), (0, 0)))
    ends = jnp.concatenate([depth_gain[:MARGIN], depth_gain[depth_here - MARGIN :]])
    note = jnp.concatenate(pieces_of(ends))
    note_rows = -(-note.shape[0] // elements_here)
    note = jnp.pad(note, (0, note_rows * elements_here - note.shape[0]))
    note = note.reshape(note_rows, elements_here)
    windows = []
    for number in range(depth // STEP):
        window = turned[number * STEP : number * STEP + WINDOW]
        if number % parts == 0:
            window = jnp.concatenate([note, window[note_rows:]])
        windows.append(window)
    windows = jnp.stack(windows).reshape(slabs, parts * WINDOW, elements_here)
    own = lax.all_to_all(windows, "slab", split_axis=0, concat_axis=0, tiled=True)

    notes = own[:, :note_rows, :].reshape(slabs, -1)[:, : 6 * MARGIN].astype(jnp.float32)
    notes = notes.reshape(slabs, 3, 2 * MARGIN)
    notes = notes[:, 0] + notes[:, 1] + notes[:, 2]
    before = lax.dynamic_index_in_dim(notes, (slab - 1) % slabs, 0, keepdims=False)[MARGIN:]
    after = lax.dynamic_index_in_dim(notes, (slab + 1) % slabs, 0, keepdims=False)[:MARGIN]
    spare = jnp.ones((EDGE - MARGIN,), jnp.float32)
    extended = jnp.concatenate([spare, before, depth_gain, after, spare])
    gains = jnp.stack(
        [jnp.pad(extended[i * STEP : i * STEP + WINDOW], (0, LANES - WINDOW)) for i in range(parts)]
    ).reshape(parts, 1, LANES)

    if elements_here != LANES:
        own = own.transpose(1, 0, 2).reshape(parts * WINDOW, -1, LANES).transpose(1, 0, 2)

    kept = own
    received = own
    bit = 1
    while bit < frames:
        if bit > 1:
            mine = (chosen ^ frame) & (bit - 1 & ~(bit // 2 - 1)) == 0
            kept = jnp.where(mine, kept, received)
        received = lax.ppermute(kept, "frame", [(i, i ^ bit) for i in range(frames)])
        bit *= 2
    choice = ((chosen ^ frame) & (frames // 2) == 0).astype(jnp.int32).reshape(1)

    blocks = own.shape[0]
    piece = pl.BlockSpec((blocks, WINDOW, LANES), lambda i: (0, i, 0))
    cells = coarse_shift.shape[:4] + (PACKED,)
    if parts == 1:
        shift_vector = coarse_shift
        vector = lambda n: pl.BlockSpec((n,) + coarse_shift.shape[1:], lambda i: (0, 0, 0, 0, 0))
        shapes = [(n,) + coarse_shift.shape[1:] for n in (7, 3)]
    else:
        shift_vector = coarse_shift.reshape(coarse_shift.shape[:4] + (parts, PACKED))
        shift_vector = jnp.moveaxis(shift_vector, 4, 0).reshape((parts * 3,) + cells[1:])
        vector = lambda n: pl.BlockSpec((n,) + cells[1:], lambda i: (i, 0, 0, 0, 0))
        shapes = [(parts * n,) + cells[1:] for n in (7, 3)]
    whole = lambda array: pl.BlockSpec(array.shape, lambda i: (0,) * array.ndim)
    gain_table = column_gain.reshape(-1, LANES)
    scores, displacement = pl.pallas_call(
        track,
        grid=(parts,),
        in_specs=[
            pl.BlockSpec(memory_space=pltpu.SMEM),
            pl.BlockSpec(memory_space=pltpu.SMEM),
            piece,
            piece,
            piece,
            whole(migration),
            whole(gain_table),
            pl.BlockSpec((1, 1, LANES), lambda i: (i, 0, 0)),
            vector(3),
        ],
        out_specs=[vector(7), vector(3)],
        out_shape=[jax.ShapeDtypeStruct(shape, jnp.float32) for shape in shapes],
        scratch_shapes=[
            pltpu.VMEM((2 * LANES, blocks * LANES), jnp.bfloat16),
            pltpu.VMEM((NX * NY, LANES), jnp.float32),
            pltpu.VMEM((LX * KROWS, LANES), jnp.float32),
            pltpu.VMEM((13, GROUPS * 8, LANES), jnp.float32),
        ],
        name="track",
    )(
        choice,
        coarse_shift,
        own,
        kept,
        received,
        migration,
        gain_table,
        gains,
        shift_vector,
    )
    if parts > 1:
        scores, displacement = (
            jnp.moveaxis(array.reshape((parts, -1) + cells[1:]), 0, 4).reshape(
                (array.shape[0] // parts,) + coarse_shift.shape[1:]
            )
            for array in (scores, displacement)
        )
    return scores, displacement


def solution(mesh):
    blocks = P(None, "frame", None, None, "slab")
    placed = (P("slab", "frame", None), P(), P(), P("slab"), blocks, P())
    return jax.shard_map(
        per_device, mesh=mesh, in_specs=placed, out_specs=(blocks, blocks), check_vma=False
    )
```

time: 553 us -> 46.3 us (0.08)
  local copies, waits for them, and re-layouts: 448 us -> 8.81 us
  waiting for transfers between devices: 41.2 us -> 11.2 us
  other arithmetic: 28.9 us -> 5.14 us
  between operations: 15.1 us -> 1.37 us
  Pallas kernels: 0 us -> 10.5 us
    gather x384 -> x0, local copies, waits for them, and re-layouts: 425 us -> none
    reduce_sum x2 -> x0, other arithmetic: 26.3 us -> none  [the longest x1 23.2 us: block_scores(): window_power = jnp.mean(window * window, axis=(1, 2, 3))]
    psum x1 -> x0, waiting for transfers between devices: 24.6 us -> none  [spread(): return lax.psum(kept, axis)]
    pallas_call x0 -> x1, Pallas kernels: none -> 10.5 us  [per_device(): pl.pallas_call(track, grid=(parts,), in_specs=[pl.BlockSpec(memory_space=...]
    convert_element_type x3 -> x0, local copies, waits for them, and re-layouts: 8.38 us -> none  [block_scores(): kernel_float = kernels.astype(jnp.float32)]
    ppermute x2, waiting for transfers between devices: 11.6 us -> 5.43 us  [per_device(): lax.ppermute(kept, 'frame', [(i, i ^ bit) for i in range(frames)])]
  transfers between devices with their start and end apart: 4 -> 3, of which waited for: 3 -> 3; matrix products, arithmetic and copies ran while one was open for 3% -> 6% of each run, Pallas kernels for 0% -> 0%
where the time goes in v1:
time: 46.3 us; the launch traced here: 45.9 us
  waiting for transfers between devices  11.2 us (24%)
  Pallas kernels  10.5 us (23%)
  starting transfers between devices  8.87 us (19%)
  local copies, waits for them, and re-layouts  8.81 us (19%)
  other arithmetic  5.14 us (11%)
  between operations  1.37 us (3%)
    pallas_call x1, Pallas kernels, per_device(): pl.pallas_call(track, grid=(parts,), in_specs=[pl.BlockSpec(memory_space=...  10.5 us
    all_to_all x1, starting transfers between devices, per_device(): lax.all_to_all(windows, 'slab', split_axis=0, concat_axis=0, tiled=True)  7.28 us
    all_to_all x1, waiting for transfers between devices, per_device(): lax.all_to_all(windows, 'slab', split_axis=0, concat_axis=0, tiled=True)  5.8 us
    ppermute x2, waiting for transfers between devices, per_device(): lax.ppermute(kept, 'frame', [(i, i ^ bit) for i in range(frames)])  5.43 us
    unnamed x7, other arithmetic  4.32 us
    pallas_call x2, local copies, waits for them, and re-layouts, per_device(): pl.pallas_call(track, grid=(parts,), in_specs=[pl.BlockSpec(memory_space=...  3.29 us
    unnamed x9, local copies, waits for them, and re-layouts  3.19 us
    ppermute x2, starting transfers between devices, per_device(): lax.ppermute(kept, 'frame', [(i, i ^ bit) for i in range(frames)])  1.59 us
  transfers between devices with their start and end apart: 3, of which 3 were waited for; matrix products, arithmetic and copies ran while one was open for 6% of the time, Pallas kernels for 0%

profile of v1, /device:TPU:0, one launch (start us, length us, event | category | flops | bytes accessed | tf_op | source)
XLA Modules:
  0.0 45.9 jit_solution(14496326663666070017)
XLA Ops:
  0.6 0.8 %fusion.18 = (f32[9]{0:T(128)S(1)}, f32[9]{0:T(128)S(1)}) fusion(f32[64]{0:T(128)} %param.9), kind=kLoop, calls=%fused_computation.46 | loop fusion | bytes 144 | tf_op jit(solution)/shard_map/slice | solution.py:245
  1.5 1.0 %copy.13 = bf16[128,1,512]{0,2,1:T(8,128)(2,1)S(1)} copy(bf16[128,1,512]{2,0,1:T(8,128)(2,1)} %param.6) | data formatting | bytes 262144 | tf_op args[0]
  2.6 0.1 fusion.17
  2.7 0.6 %fusion.1 = bf16[8,96,128]{2,1,0:T(8,128)(2,1)} fusion(bf16[1,128]{1,0:T(2,128)(2,1)S(1)} %fusion.17, bf16[95,128]{1,0:T(8,128)(2,1)S(1)} %get-tuple-element.15), kind=kLoop, calls=%fused_computation.12 | loop fusion | flops 49151 | bytes 49152
  3.3 0.6 %fusion.3 = bf16[8,96,128]{2,1,0:T(8,128)(2,1)} fusion(bf16[8,96,128]{2,1,0:T(8,128)(2,1)} %fusion.1, bf16[1,128]{1,0:T(2,128)(2,1)S(1)} %fusion.17, bf16[95,128]{1,0:T(8,128)(2,1)S(1)} %get-tuple-element.14), kind=kLoop, calls=%fused_computation.14 | loop fusion | flops 49152 | bytes 49152
  3.9 0.6 %fusion.5 = bf16[8,96,128]{2,1,0:T(8,128)(2,1)} fusion(bf16[8,96,128]{2,1,0:T(8,128)(2,1)} %fusion.3, bf16[1,128]{1,0:T(2,128)(2,1)S(1)} %fusion.17, bf16[95,128]{1,0:T(8,128)(2,1)S(1)} %get-tuple-element.13), kind=kLoop, calls=%fused_computation.16 | loop fusion | flops 49152 | bytes 49152
  4.5 0.6 %fusion.7 = bf16[8,96,128]{2,1,0:T(8,128)(2,1)} fusion(bf16[8,96,128]{2,1,0:T(8,128)(2,1)} %fusion.5, bf16[1,128]{1,0:T(2,128)(2,1)S(1)} %fusion.17, bf16[95,128]{1,0:T(8,128)(2,1)S(1)} %get-tuple-element.12), kind=kLoop, calls=%fused_computation.18 | loop fusion | flops 49152 | bytes 49152
  5.2 0.6 %fusion.9 = bf16[8,96,128]{2,1,0:T(8,128)(2,1)} fusion(bf16[8,96,128]{2,1,0:T(8,128)(2,1)} %fusion.7, bf16[1,128]{1,0:T(2,128)(2,1)S(1)} %fusion.17, bf16[95,128]{1,0:T(8,128)(2,1)S(1)} %get-tuple-element.11), kind=kLoop, calls=%fused_computation.20 | loop fusion | flops 49152 | bytes 49152
  5.8 0.6 %fusion.11 = bf16[8,96,128]{2,1,0:T(8,128)(2,1)} fusion(bf16[8,96,128]{2,1,0:T(8,128)(2,1)} %fusion.9, bf16[1,128]{1,0:T(2,128)(2,1)S(1)} %fusion.17, bf16[95,128]{1,0:T(8,128)(2,1)S(1)} %get-tuple-element.10), kind=kLoop, calls=%fused_computation.22 | loop fusion | flops 49152 | bytes 49152
  6.4 0.6 %fusion.13 = bf16[8,96,128]{2,1,0:T(8,128)(2,1)} fusion(bf16[8,96,128]{2,1,0:T(8,128)(2,1)} %fusion.11, bf16[1,128]{1,0:T(2,128)(2,1)S(1)} %fusion.17, bf16[95,128]{1,0:T(8,128)(2,1)S(1)} %get-tuple-element.9), kind=kLoop, calls=%fused_computation.24 | loop fusion | flops 49152 | bytes 49152
  7.0 0.6 %fusion.15 = bf16[8,96,128]{2,1,0:T(8,128)(2,1)} fusion(bf16[8,96,128]{2,1,0:T(8,128)(2,1)} %fusion.13, bf16[1,128]{1,0:T(2,128)(2,1)S(1)} %fusion.17, bf16[95,128]{1,0:T(8,128)(2,1)S(1)} %get-tuple-element.8), kind=kLoop, calls=%fused_computation.26 | loop fusion | flops 49152 | bytes 49152 | tf_op jit(solution)/shard_map/stack | solution.py:256
  7.6 7.3 %all-to-all-start = ((bf16[8,96,128]{2,1,0:T(8,128)(2,1)}), bf16[8,96,128]{2,1,0:T(8,128)(2,1)S(1)}, u32[]{:S(2)}, u32[]{:S(2)}) async-start(bf16[8,96,128]{2,1,0:T(8,128)(2,1)} %fusion.15), calls=%async_computation | async-start | bytes 393216 | tf_op jit(solution)/shard_map/all_to_all | solution.py:257
  15.6 1.5 %copy.14.shift.shift_cells = s32[3,1,4,8,4]{4,3,2,1,0:T(8,128)} copy(s32[3,1,4,8,4]{3,4,2,1,0:T(4,128)} %param.10) | data formatting | bytes 3072 | tf_op args[4]
  17.1 5.8 %all-to-all-done.own = bf16[8,96,128]{2,1,0:T(8,128)(2,1)S(1)} async-done(((bf16[8,96,128]{2,1,0:T(8,128)(2,1)}), bf16[8,96,128]{2,1,0:T(8,128)(2,1)S(1)}, u32[]{:S(2)}, u32[]{:S(2)}) %all-to-all-start) | async-done | bytes 196640 | tf_op jit(solution)/shard_map/all_to_all | solution.py:257
  22.9 0.1 reshape.40
  23.0 1.4 %collective-permute-done = bf16[8,96,128]{2,1,0:T(8,128)(2,1)S(1)} collective-permute-done((bf16[8,96,128]{2,1,0:T(8,128)(2,1)S(1)}, bf16[8,96,128]{2,1,0:T(8,128)(2,1)S(1)}, u32[]{:S(2)}, u32[]{:S(2)}) %collective-permute-start) | collective-permute-done | bytes 196640 | tf_op jit(solution)/shard_map/ppermute | solution.py:280
  24.5 1.6 %collective-permute-start.1 = (bf16[8,96,128]{2,1,0:T(8,128)(2,1)S(1)}, bf16[8,96,128]{2,1,0:T(8,128)(2,1)S(1)}, u32[]{:S(2)}, u32[]{:S(2)}) collective-permute-start(bf16[8,96,128]{2,1,0:T(8,128)(2,1)S(1)} %broadcast_select_fusion.kept), channel_id=1, source_target_pairs={{0,16},{8,24},{16,0},{24,8},{1,17},{9,25},{17,1},{25,9},{2,18},{10... | collective-permute-start | bytes 589832 | tf_op jit(solution)/shard_map/ppermute | solution.py:280
  26.1 0.7 %concatenate.43 = f32[96]{0:T(128)S(1)} concatenate(f32[7]{0:T(128)S(1)} %broadcast.11, f32[9]{0:T(128)S(1)} %get-tuple-element.23, f32[64]{0:T(128)} %param.9, f32[9]{0:T(128)S(1)} %get-tuple-element.22, f32[7]{0:T(128)S(1)} %broadcast.11), dimensions={0} | concatenate | bytes 768 | tf_op jit(solution)/shard_map/concatenate | solution.py:265
  26.8 0.6 %pad_bitcast_fusion.depth_gain = f32[1,1,128]{2,1,0:T(1,128)} fusion(f32[96]{0:T(128)S(1)} %concatenate.43), kind=kLoop, calls=%fused_computation.41 | loop fusion | bytes 896 | tf_op jit(solution)/shard_map/reshape;stack | solution.py:268
  27.4 4.0 %collective-permute-done.1.received = bf16[8,96,128]{2,1,0:T(8,128)(2,1)S(1)} collective-permute-done((bf16[8,96,128]{2,1,0:T(8,128)(2,1)S(1)}, bf16[8,96,128]{2,1,0:T(8,128)(2,1)S(1)}, u32[]{:S(2)}, u32[]{:S(2)}) %collective-permute-start.1) | collective-permute-done | bytes 196640 | tf_op jit(solution)/shard_map/ppermute | solution.py:280
  31.5 0.7 %copy-done.2 = bf16[8,96,128]{2,1,0:T(8,128)(2,1)} copy-done((bf16[8,96,128]{2,1,0:T(8,128)(2,1)}, bf16[8,96,128]{2,1,0:T(8,128)(2,1)S(1)}, u32[]{:S(2)}) %copy-start.2) | copy-done | bytes 196632
  32.1 10.5 %track.1 = (f32[7,1,4,8,4]{4,3,2,1,0:T(8,128)}, f32[3,1,4,8,4]{4,3,2,1,0:T(8,128)}) custom-call(s32[1]{0:T(128)} %bitcast.1.choice, s32[3,1,4,8,4]{4,3,2,1,0:T(8,128)} %copy.14.shift.shift_cells, bf16[8,96,128]{2,1,0:T(8,128)(2,1)} %copy-done, bf16[8,96,128]{2,1,0:T(8,128)(2,1)} %copy-done.1, bf16[8,96,128]{2,1,0:T(8,128)(2,1)} %copy-done.2, ...), custom_call_target="tpu_custom_call" | custom-call | tf_op jit(solution)/shard_map/track/pallas_call | solution.py:298
  42.6 1.8 %copy.16 = f32[7,1,4,8,4]{3,4,2,1,0:T(4,128)} copy(f32[7,1,4,8,4]{4,3,2,1,0:T(8,128)} %get-tuple-element.4) | data formatting | bytes 7168 | tf_op jit(solution)/shard_map/track/pallas_call | solution.py:298
  44.4 1.5 %copy.17 = f32[3,1,4,8,4]{3,4,2,1,0:T(4,128)} copy(f32[3,1,4,8,4]{4,3,2,1,0:T(8,128)} %get-tuple-element.5) | data formatting | bytes 3072 | tf_op jit(solution)/shard_map/track/pallas_call | solution.py:298
  (17 shorter events, 0.3 us)
Async XLA Ops:
  7.6 15.2 %all-to-all-start = ((bf16[8,96,128]{2,1,0:T(8,128)(2,1)}), bf16[8,96,128]{2,1,0:T(8,128)(2,1)S(1)}, u32[]{:S(2)}, u32[]{:S(2)}) async-start(bf16[8,96,128]{2,1,0:T(8,128)(2,1)} %fusion.15), calls=%async_computation | async-start | bytes 393216 | tf_op jit(solution)/shard_map/all_to_all | solution.py:257
  22.9 8.6 %copy-start = (bf16[8,96,128]{2,1,0:T(8,128)(2,1)}, bf16[8,96,128]{2,1,0:T(8,128)(2,1)S(1)}, u32[]{:S(2)}) copy-start(bf16[8,96,128]{2,1,0:T(8,128)(2,1)S(1)} %all-to-all-done.own) | copy-start | bytes 589828
  23.0 1.4 %collective-permute-start = (bf16[8,96,128]{2,1,0:T(8,128)(2,1)S(1)}, bf16[8,96,128]{2,1,0:T(8,128)(2,1)S(1)}, u32[]{:S(2)}, u32[]{:S(2)}) collective-permute-start(bf16[8,96,128]{2,1,0:T(8,128)(2,1)S(1)} %all-to-all-done.own), channel_id=1, source_target_pairs={{0,8},{8,0},{16,24},{24,16},{1,9},{9,1},{17,25},{25,17},{2,10},{10... | collective-permute-start | bytes 589832 | tf_op jit(solution)/shard_map/ppermute | solution.py:280
  24.4 7.0 %copy-start.1 = (bf16[8,96,128]{2,1,0:T(8,128)(2,1)}, bf16[8,96,128]{2,1,0:T(8,128)(2,1)S(1)}, u32[]{:S(2)}) copy-start(bf16[8,96,128]{2,1,0:T(8,128)(2,1)S(1)} %broadcast_select_fusion.kept) | copy-start | bytes 589828
  24.5 7.0 %collective-permute-start.1 = (bf16[8,96,128]{2,1,0:T(8,128)(2,1)S(1)}, bf16[8,96,128]{2,1,0:T(8,128)(2,1)S(1)}, u32[]{:S(2)}, u32[]{:S(2)}) collective-permute-start(bf16[8,96,128]{2,1,0:T(8,128)(2,1)S(1)} %broadcast_select_fusion.kept), channel_id=1, source_target_pairs={{0,16},{8,24},{16,0},{24,8},{1,17},{9,25},{17,1},{25,9},{2,18},{10... | collective-permute-start | bytes 589832 | tf_op jit(solution)/shard_map/ppermute | solution.py:280
  31.5 0.7 %copy-start.2 = (bf16[8,96,128]{2,1,0:T(8,128)(2,1)}, bf16[8,96,128]{2,1,0:T(8,128)(2,1)S(1)}, u32[]{:S(2)}) copy-start(bf16[8,96,128]{2,1,0:T(8,128)(2,1)S(1)} %collective-permute-done.1.received) | copy-start | bytes 589828

commit v2 on v1

v2 whole, which is shorter than its diff:
```python
import functools
import math

import jax
import jax.numpy as jnp
from jax import lax
from jax.experimental import pallas as pl
from jax.experimental.pallas import tpu as pltpu
from jax.sharding import PartitionSpec as P

LX = 32
LY = 64
KX = 8
KY = 8
KZ = 16
CMAX = 8
MARGIN = CMAX + 1
EPSILON = 1e-05

LANES = 128
STEP = 64
EDGE = 16
WINDOW = STEP + 2 * EDGE
SEGMENT = 32
PACKED = STEP // KZ
BX = LX // KX
BY = LY // KY
GROUPS = BX * BY
NX = LX + 2 * MARGIN
NY = LY + 2 * EDGE
KROWS = 8 + 2 * LY + 8
CELLS = KX * KY * KZ
CHUNK = 256


def pieces_of(value):
    high = value.astype(jnp.bfloat16).astype(jnp.float32)
    middle = (value - high).astype(jnp.bfloat16).astype(jnp.float32)
    return high, middle, value - high - middle


def window_rows(element_data, depth_gain, windows, row):
    row[...] = jnp.zeros(row.shape, jnp.float32)
    for index, piece in enumerate(pieces_of(depth_gain[...])):
        row[index : index + 1, :STEP] = piece
    note = row[...].astype(jnp.bfloat16)
    slabs = windows.shape[0]
    empty = jnp.zeros((EDGE, LANES), jnp.bfloat16)
    spare = lax.broadcasted_iota(jnp.int32, (EDGE, LANES), 0) < 3

    def put(slab, first, rows):
        if 0 <= slab < slabs:
            if first == 0:
                rows = jnp.where(spare, note, rows)
            windows[slab, first : first + EDGE, :] = rows

    put(0, 0, empty)
    put(slabs - 1, EDGE + STEP, empty)
    for column in range(element_data.shape[1] // LANES):
        turned = jnp.transpose(element_data[:, column * LANES : (column + 1) * LANES])
        for unit in range(LANES // EDGE):
            slab, place = divmod(column * LANES + unit * EDGE, STEP)
            rows = turned[unit * EDGE : (unit + 1) * EDGE]
            put(slab, place + EDGE, rows)
            if place == STEP - EDGE:
                put(slab + 1, 0, rows)
            if place == 0:
                put(slab - 1, EDGE + STEP, rows)


def depth_row(choice, samples):
    lane = lax.broadcasted_iota(jnp.int32, (8, LANES), 1)

    def of(which):
        note = samples[choice[which], :EDGE, :].astype(jnp.float32)
        return jnp.broadcast_to(note[0:1] + note[1:2] + note[2:3], (8, LANES))

    row = pltpu.roll(of(2), EDGE, 1)
    row = jnp.where(lane < EDGE, pltpu.roll(of(1), (EDGE - STEP) % LANES, 1), row)
    return jnp.where(lane >= EDGE + STEP, pltpu.roll(of(3), EDGE + STEP, 1), row)


def migrate(right, migration, columns, gains, store):
    for chunk in range(LX * LY // CHUNK):
        raw = lax.dot_general(
            migration[chunk * CHUNK : (chunk + 1) * CHUNK, :],
            right,
            (((1,), (1,)), ((), ())),
            preferred_element_type=jnp.float32,
        )
        for piece in range(CHUNK // LY):
            x = chunk * (CHUNK // LY) + piece
            row = x * LY
            gain = columns[row % LANES : row % LANES + LY, row // LANES : row // LANES + 1]
            image = (raw[piece * LY : (piece + 1) * LY] * jnp.broadcast_to(gain, (LY, LANES))) * gains
            store(x, image.astype(jnp.bfloat16).astype(jnp.float32))


def own_kernels(choice, own, migration, column_gain, kernels):
    gap = jnp.zeros((SEGMENT - KZ, migration.shape[1]), jnp.bfloat16)
    rows = []
    for j in range(PACKED):
        pieces = [own[b, EDGE + j * KZ : EDGE + (j + 1) * KZ, :] for b in range(own.shape[0])]
        rows += [jnp.concatenate(pieces, axis=1), gap]
    lane = lax.broadcasted_iota(jnp.int32, (8, LANES), 1)
    note = own[choice[2], :EDGE, :].astype(jnp.float32)
    row = jnp.broadcast_to(note[0:1] + note[1:2] + note[2:3], (8, LANES))
    gains = row
    for j in range(1, PACKED):
        gains = jnp.where(lane >= j * SEGMENT, pltpu.roll(row, j * KZ, 1), gains)
    for x in range(LX):
        for by in range(BY + 1):
            kernels[x * KROWS + by * 16 : x * KROWS + by * 16 + 8, :] = jnp.zeros((8, LANES))

    def store(x, image):
        for by in range(BY):
            row = x * KROWS + 8 + by * 16
            kernels[row : row + 8, :] = image[by * KY : (by + 1) * KY]

    migrate(
        jnp.concatenate(rows), migration, jnp.transpose(column_gain[...]), gains[:1], store
    )


def track(
    choice,
    shift,
    kept,
    received,
    migration,
    column_gain,
    kernels,
    shift_cells,
    scores,
    displacement,
    volume,
    sums,
    turned,
):
    keep = choice[0] == 1
    zero = jnp.zeros((NY, LANES), jnp.float32)
    for x in list(range(MARGIN)) + list(range(LX + MARGIN, NX)):
        volume[x * NY : (x + 1) * NY, :] = zero
    for x in range(LX):
        base = (x + MARGIN) * NY
        volume[base : base + EDGE, :] = zero[:EDGE]
        volume[base + EDGE + LY : base + NY, :] = zero[:EDGE]

    def store(x, image):
        base = (x + MARGIN) * NY + EDGE
        volume[base : base + LY, :] = image

    pieces = [jnp.where(keep, kept[b], received[b]) for b in range(kept.shape[0])]
    spare = jnp.zeros((LANES - WINDOW, migration.shape[1]), jnp.bfloat16)
    right = jnp.concatenate([jnp.concatenate(pieces, axis=1), spare])
    columns = jnp.transpose(column_gain[...])
    migrate(right, migration, columns, depth_row(choice, kept)[:1], store)

    place = lax.broadcasted_iota(jnp.int32, (8, LANES), 1)
    place = (place + 8) % LANES // SEGMENT
    segment = [place == j for j in range(PACKED)]
    row_number = lax.broadcasted_iota(jnp.int32, (8, LANES), 0)

    def group(g, carry):
        bx = g // BY
        by = g % BY
        starts = []
        turns = []
        for j in range(PACKED):
            first = bx * KX + MARGIN + shift[0, 0, bx, j, by]
            second = by * KY + EDGE + shift[1, 0, bx, j, by]
            starts.append(first * NY + second)
            turns.append((j * KZ - EDGE + 2 * LANES - shift[2, 0, bx, j, by]) % LANES)

        def gather(offset, stride):
            value = None
            for j in range(PACKED):
                start = starts[j] + offset
                if stride == 1:
                    rows = volume[pl.ds(start, 8), :]
                else:
                    rows = volume[pl.ds(start, 8, stride=stride), :]
                rows = pltpu.roll(rows, turns[j], 1)
                value = rows if value is None else jnp.where(segment[j], rows, value)
            return value

        base = bx * KX * KROWS + by * 16 + 8
        window = [gather((x - 1) * NY, 1) for x in range(KX + 2)]
        square = [value * value for value in window]
        middle = square[2]
        for x in range(3, KX):
            middle = middle + square[x]
        pair_low = square[0] + square[1]
        pair_high = square[KX] + square[KX + 1]
        center = middle + (square[1] + square[KX])
        cross = [None] * 7
        power = None

        def add(index, value):
            cross[index] = value if cross[index] is None else cross[index] + value

        for x in range(KX):
            row = base + x * KROWS
            kernel = kernels[pl.ds(row, 8), :]
            add(0, kernel * window[x + 1])
            add(1, kernel * window[x])
            add(2, kernel * window[x + 2])
            add(3, kernels[pl.ds(row + 1, 8), :] * window[x + 1])
            add(4, kernels[pl.ds(row - 1, 8), :] * window[x + 1])
            add(5, pltpu.roll(kernel, LANES - 1, 1) * window[x + 1])
            add(6, pltpu.roll(kernel, 1, 1) * window[x + 1])
            power = kernel * kernel if power is None else power + kernel * kernel
        before = gather(-1, NY)
        after = gather(KY, NY)
        add(3, kernels[pl.ds(base, 8, stride=KROWS), :] * before)
        add(4, kernels[pl.ds(base + KY - 1, 8, stride=KROWS), :] * after)
        low = jnp.where(row_number < KY - 1, center, 0.0) + before * before
        high = jnp.where(row_number > 0, center, 0.0) + after * after
        held = cross[:5] + [center, middle + pair_low, middle + pair_high]
        held += [low, high, power, cross[5], cross[6]]
        for index, value in enumerate(held):
            sums[index, pl.ds(g * 8, 8), :] = value
        return carry

    lax.fori_loop(0, GROUPS, group, 0)

    def rows_of(index):
        parts = []
        for bx in range(BX):
            value = None
            for y in range(KY):
                rows = sums[index, pl.ds(bx * BY * 8 + y, BY, stride=8), :]
                value = rows if value is None else value + rows
            parts.append(value)
        return parts

    row_of_block = lax.broadcasted_iota(jnp.int32, (8, LANES), 0)

    def totals(block, offsets):
        value = jnp.transpose(jnp.concatenate([part for index in block for part in rows_of(index)]))
        turned[0:8, :] = value[LANES - 8 :]
        turned[8 : LANES + 8, :] = value
        turned[LANES + 8 : LANES + 16, :] = value[:8]
        result = []
        for offset in offsets:
            total = None
            for j in range(PACKED):
                row = 8 + j * SEGMENT + offset
                value = turned[row : row + 8, :] + turned[row + 8 : row + 16, :]
                value = jnp.broadcast_to(jnp.sum(value, axis=0, keepdims=True), (8, LANES))
                total = value if total is None else jnp.where(row_of_block >= j, value, total)
            result.append(total)
        return result

    def lanes_of(value, place):
        return value if place == 0 else pltpu.roll(value, LANES - place * GROUPS, 1)

    (first,) = totals((0, 1, 2, 3), (0,))
    second, second_low, second_high = totals((4, 5, 6, 7), (0, -1, 1))
    third, third_low, third_high = totals((8, 9, 10, 11), (0, -1, 1))
    (fourth,) = totals((12, 12, 12, 12), (1,))
    cross = [lanes_of(first, place) for place in range(4)]
    cross += [second, lanes_of(third_low, 3), fourth]
    powers = [lanes_of(second, place) for place in (1, 2, 3)]
    powers += [third, lanes_of(third, 1), lanes_of(second_low, 1), lanes_of(second_high, 1)]
    kernel_power = lanes_of(third, 2) * (1.0 / CELLS) + EPSILON
    result = []
    for index in range(7):
        mean = cross[index] * (1.0 / CELLS)
        window_power = powers[index] * (1.0 / CELLS) + EPSILON
        result.append(math.sqrt(CELLS) * mean / jnp.sqrt(kernel_power * window_power))
    moves = []
    for axis in range(3):
        lower = result[1 + 2 * axis]
        upper = result[2 + 2 * axis]
        curvature = jnp.maximum(2.0 * result[0] - lower - upper, 1.0)
        moves.append((upper - lower) / (2.0 * curvature))
    for bx in range(BX):
        for index in range(7):
            value = pltpu.roll(result[index], (LANES - bx * BY) % LANES, 1)
            scores[index, 0, bx] = value[:PACKED, :BY]
        for axis in range(3):
            value = pltpu.roll(moves[axis], (LANES - bx * BY) % LANES, 1)
            cells = shift_cells[axis, 0, bx].astype(jnp.float32)
            displacement[axis, 0, bx] = cells + value[:PACKED, :BY]


def on_chip(count):
    return [pl.BlockSpec(memory_space=pltpu.VMEM)] * count


def per_device(element_data, migration, column_gain, depth_gain, coarse_shift, reference_frame):
    elements_here, frames_here, depth = element_data.shape
    depth_here = depth_gain.shape[0]
    slabs = lax.axis_size("slab")
    frames = lax.axis_size("frame")
    elements = elements_here * slabs
    assert frames_here == 1 and depth_here == STEP
    chosen = reference_frame[0]
    frame = lax.axis_index("frame")
    slab = lax.axis_index("slab")
    own_data = element_data.reshape(elements_here, depth)

    if elements_here == LANES:
        windows = pl.pallas_call(
            window_rows,
            in_specs=on_chip(2),
            out_specs=on_chip(1)[0],
            out_shape=jax.ShapeDtypeStruct((slabs, WINDOW, LANES), jnp.bfloat16),
            scratch_shapes=[pltpu.VMEM((EDGE, LANES), jnp.float32)],
            name="window_rows",
        )(own_data, depth_gain.reshape(1, STEP))
        own = lax.all_to_all(windows, "slab", split_axis=0, concat_axis=0, tiled=True)
        places = [(slab - 1) % slabs, slab, (slab + 1) % slabs]
    else:
        turned = jnp.pad(own_data.T, ((EDGE, EDGE), (0, 0)))
        windows = jnp.stack([turned[i * STEP : i * STEP + WINDOW] for i in range(slabs)])
        own = lax.all_to_all(windows, "slab", split_axis=0, concat_axis=0, tiled=True)
        own = own.transpose(1, 0, 2).reshape(WINDOW, elements // LANES, LANES).transpose(1, 0, 2)
        ring = [(i, (i + 1) % slabs) for i in range(slabs)]
        left = lax.ppermute(depth_gain, "slab", ring)
        right = lax.ppermute(depth_gain, "slab", [(j, i) for i, j in ring])
        high = lambda value: lax.reduce_precision(value, 8, 7)
        for place, value in enumerate((left, depth_gain, right)):
            middle = high(value - high(value))
            note = jnp.stack([high(value), middle, value - high(value) - middle])
            own = own.at[place, :3, :STEP].set(note.astype(jnp.bfloat16))
        places = [0, 1, 2]

    kept = own
    received = own
    bit = 1
    while bit < frames:
        if bit > 1:
            mine = (chosen ^ frame) & (bit // 2) == 0
            kept = jnp.where(mine, kept, received)
        received = lax.ppermute(kept, "frame", [(i, i ^ bit) for i in range(frames)])
        bit *= 2
    keep = ((chosen ^ frame) & (frames // 2) == 0).astype(jnp.int32)
    choice = jnp.stack([keep] + [jnp.asarray(place, jnp.int32) for place in places])

    gain_table = column_gain.reshape(-1, LANES)
    scalars = pl.BlockSpec(memory_space=pltpu.SMEM)
    kernels = pl.pallas_call(
        own_kernels,
        in_specs=[scalars] + on_chip(3),
        out_specs=on_chip(1)[0],
        out_shape=jax.ShapeDtypeStruct((LX * KROWS, LANES), jnp.float32),
        name="own_kernels",
    )(choice, own, migration, gain_table)

    turn = (0, 1, 2, 4, 3)
    shifts = coarse_shift.transpose(turn)
    shapes = [jax.ShapeDtypeStruct((n,) + shifts.shape[1:], jnp.float32) for n in (7, 3)]
    scores, displacement = pl.pallas_call(
        track,
        in_specs=[scalars, scalars] + on_chip(6),
        out_specs=on_chip(2),
        out_shape=shapes,
        scratch_shapes=[
            pltpu.VMEM((NX * NY, LANES), jnp.float32),
            pltpu.VMEM((13, GROUPS * 8, LANES), jnp.float32),
            pltpu.VMEM((LANES + 16, LANES), jnp.float32),
        ],
        name="track",
    )(choice, shifts, kept, received, migration, gain_table, kernels, shifts)
    return scores.transpose(turn), displacement.transpose(turn)


def solution(mesh):
    blocks = P(None, "frame", None, None, "slab")
    placed = (P("slab", "frame", None), P(), P(), P("slab"), blocks, P())
    return jax.shard_map(
        per_device, mesh=mesh, in_specs=placed, out_specs=(blocks, blocks), check_vma=False
    )
```

time: 46.3 us -> 38.1 us (0.82)
  blocking collectives: 0 us -> 15.2 us
  waiting for transfers between devices: 11.2 us -> 0.79 us
  local copies, waits for them, and re-layouts: 8.81 us -> 0.68 us
  starting transfers between devices: 8.87 us -> 1.59 us
  Pallas kernels: 10.5 us -> 17.7 us
  other arithmetic: 5.14 us -> 0.58 us
    all_to_all x0 -> x1, blocking collectives: none -> 15.2 us  [per_device(): lax.all_to_all(windows, 'slab', split_axis=0, concat_axis=0, tiled=True)]
    all_to_all x1 -> x0, starting transfers between devices: 7.28 us -> none  [per_device(): lax.all_to_all(windows, 'slab', split_axis=0, concat_axis=0, tiled=True)]
    pallas_call x1 -> x3, Pallas kernels: 10.5 us -> 17.7 us  [the longest x1 11.1 us: per_device(): pl.pallas_call(track, in_specs=[scalars, scalars] + on_chip(6), out_specs...]
    all_to_all x1 -> x0, waiting for transfers between devices: 5.8 us -> none  [per_device(): lax.all_to_all(windows, 'slab', split_axis=0, concat_axis=0, tiled=True)]
    ppermute x2, waiting for transfers between devices: 5.43 us -> 0.79 us  [per_device(): lax.ppermute(kept, 'frame', [(i, i ^ bit) for i in range(frames)])]
    unnamed x7 -> x0, other arithmetic: 4.32 us -> none
    pallas_call x2 -> x0, local copies, waits for them, and re-layouts: 3.29 us -> none  [per_device(): pl.pallas_call(track, grid=(parts,), in_specs=[pl.BlockSpec(memory_space=...]
    unnamed x9 -> x6, local copies, waits for them, and re-layouts: 3.19 us -> 0.68 us
  transfers between devices with their start and end apart: 3 -> 2, of which waited for: 3 -> 1; matrix products, arithmetic and copies ran while one was open for 6% -> 1% of each run, Pallas kernels for 0% -> 13%
where the time goes in v2:
time: 38.1 us; the launch traced here: 37.8 us
  Pallas kernels  17.7 us (46%)
  blocking collectives  15.2 us (40%)
  starting transfers between devices  1.59 us (4%)
  between operations  1.31 us (3%)
  waiting for transfers between devices  0.79 us (2%)
  local copies, waits for them, and re-layouts  0.68 us (2%)
  other arithmetic  0.58 us (2%)
    all_to_all x1, blocking collectives, per_device(): lax.all_to_all(windows, 'slab', split_axis=0, concat_axis=0, tiled=True)  15.2 us
    pallas_call x1, Pallas kernels, per_device(): pl.pallas_call(track, in_specs=[scalars, scalars] + on_chip(6), out_specs...  11.1 us
    pallas_call x1, Pallas kernels, per_device(): pl.pallas_call(own_kernels, in_specs=[scalars] + on_chip(3), out_specs=on...  4.9 us
    pallas_call x1, Pallas kernels, per_device(): pl.pallas_call(window_rows, in_specs=on_chip(2), out_specs=on_chip(1)[0],...  1.67 us
    ppermute x2, starting transfers between devices, per_device(): lax.ppermute(kept, 'frame', [(i, i ^ bit) for i in range(frames)])  1.59 us
    ppermute x2, waiting for transfers between devices, per_device(): lax.ppermute(kept, 'frame', [(i, i ^ bit) for i in range(frames)])  0.79 us
  transfers between devices with their start and end apart: 2, of which 1 were waited for; matrix products, arithmetic and copies ran while one was open for 1% of the time, Pallas kernels for 13%

profile of v2, /device:TPU:0, one launch (start us, length us, event | category | flops | bytes accessed | tf_op | source)
XLA Modules:
  0.0 37.8 jit_solution(10098647085579139407)
XLA Ops:
  0.6 1.7 %window_rows.1 = bf16[8,96,128]{2,1,0:T(8,128)(2,1)} custom-call(bf16[128,512]{1,0:T(8,128)(2,1)} %bitcast.12, f32[1,64]{1,0:T(1,128)} %bitcast.17), custom_call_target="tpu_custom_call" | custom-call | tf_op jit(solution)/shard_map/window_rows/pallas_call | solution.py:305
  2.3 15.2 %all_to_all.5.own = bf16[8,96,128]{2,1,0:T(8,128)(2,1)S(1)} all-to-all(bf16[8,96,128]{2,1,0:T(8,128)(2,1)} %window_rows.1), channel_id=1, replica_groups=mesh['frame'=4,'slab'=8] {'slab'}, dimensions={0} | all-to-all | bytes 393216 | tf_op jit(solution)/shard_map/all_to_all | solution.py:313
  17.5 0.0 copy-start
  17.5 0.0 collective-permute-start
  18.2 0.8 %collective-permute-done = bf16[8,96,128]{2,1,0:T(8,128)(2,1)S(1)} collective-permute-done((bf16[8,96,128]{2,1,0:T(8,128)(2,1)S(1)}, bf16[8,96,128]{2,1,0:T(8,128)(2,1)S(1)}, u32[]{:S(2)}, u32[]{:S(2)}) %collective-permute-start) | collective-permute-done | bytes 196640 | tf_op jit(solution)/shard_map/ppermute | solution.py:337
  19.0 0.0 copy-start.1
  19.0 1.6 %collective-permute-start.1 = (bf16[8,96,128]{2,1,0:T(8,128)(2,1)S(1)}, bf16[8,96,128]{2,1,0:T(8,128)(2,1)S(1)}, u32[]{:S(2)}, u32[]{:S(2)}) collective-permute-start(bf16[8,96,128]{2,1,0:T(8,128)(2,1)S(1)} %broadcast_select_fusion.kept), channel_id=1, source_target_pairs={{0,16},{8,24},{16,0},{24,8},{1,17},{9,25},{17,1},{25,9},{2,18},{10... | collective-permute-start | bytes 589832 | tf_op jit(solution)/shard_map/ppermute | solution.py:337
  20.6 0.6 %pad_add_fusion.choice = s32[4]{0:T(128)} fusion(s32[1]{0:T(128)} %bitcast.4, s32[1]{0:T(128)} %bitcast.3, s32[1]{0:T(128)} %bitcast.2, s32[1]{0:T(128)} %bitcast.1), kind=kLoop, calls=%fused_computation.1 | loop fusion | flops 12 | bytes 32 | tf_op jit(solution)/shard_map/stack | solution.py:340
  21.1 0.0 copy-done
  21.1 4.9 %own_kernels.1.kernels = f32[4608,128]{1,0:T(8,128)} custom-call(s32[4]{0:T(128)} %pad_add_fusion.choice, bf16[8,96,128]{2,1,0:T(8,128)(2,1)} %copy-done, bf16[2048,1024]{1,0:T(8,128)(2,1)} %migration.3, f32[16,128]{1,0:T(8,128)} %bitcast.15), custom_call_target="tpu_custom_call" | custom-call | tf_op jit(solution)/shard_map/own_kernels/pallas_call | solution.py:344
  26.0 0.0 collective-permute-done.1.received
  26.1 0.0 copy-start.2
  26.1 0.0 copy-done.1
  26.1 0.7 %copy-done.2 = bf16[8,96,128]{2,1,0:T(8,128)(2,1)} copy-done((bf16[8,96,128]{2,1,0:T(8,128)(2,1)}, bf16[8,96,128]{2,1,0:T(8,128)(2,1)S(1)}, u32[]{:S(2)}) %copy-start.2) | copy-done | bytes 196632
  26.7 11.1 %track.1 = (f32[7,1,4,4,8]{4,3,2,1,0:T(4,128)}, f32[3,1,4,4,8]{4,3,2,1,0:T(4,128)}) custom-call(s32[4]{0:T(128)} %pad_add_fusion.choice, s32[3,1,4,4,8]{4,3,2,1,0:T(4,128)} %bitcast.13, bf16[8,96,128]{2,1,0:T(8,128)(2,1)} %copy-done.1, bf16[8,96,128]{2,1,0:T(8,128)(2,1)} %copy-done.2, bf16[2048,1024]{1,0:T(8,128)(2,1)} %migration.3, f32[16,128]{1,0:T(8,128)} %bitcast.16, ...), custom_call_target="tpu_custom_call" | custom-call | tf_op jit(solution)/shard_map/track/pallas_call | solution.py:355
  (1 shorter events, 0.0 us)
Async XLA Ops:
  17.5 3.6 %copy-start = (bf16[8,96,128]{2,1,0:T(8,128)(2,1)}, bf16[8,96,128]{2,1,0:T(8,128)(2,1)S(1)}, u32[]{:S(2)}) copy-start(bf16[8,96,128]{2,1,0:T(8,128)(2,1)S(1)} %all_to_all.5.own) | copy-start | bytes 589828
  17.5 1.4 %collective-permute-start = (bf16[8,96,128]{2,1,0:T(8,128)(2,1)S(1)}, bf16[8,96,128]{2,1,0:T(8,128)(2,1)S(1)}, u32[]{:S(2)}, u32[]{:S(2)}) collective-permute-start(bf16[8,96,128]{2,1,0:T(8,128)(2,1)S(1)} %all_to_all.5.own), channel_id=1, source_target_pairs={{0,8},{8,0},{16,24},{24,16},{1,9},{9,1},{17,25},{25,17},{2,10},{10... | collective-permute-start | bytes 589832 | tf_op jit(solution)/shard_map/ppermute | solution.py:337
  19.0 7.1 %copy-start.1 = (bf16[8,96,128]{2,1,0:T(8,128)(2,1)}, bf16[8,96,128]{2,1,0:T(8,128)(2,1)S(1)}, u32[]{:S(2)}) copy-start(bf16[8,96,128]{2,1,0:T(8,128)(2,1)S(1)} %broadcast_select_fusion.kept) | copy-start | bytes 589828
  19.0 7.0 %collective-permute-start.1 = (bf16[8,96,128]{2,1,0:T(8,128)(2,1)S(1)}, bf16[8,96,128]{2,1,0:T(8,128)(2,1)S(1)}, u32[]{:S(2)}, u32[]{:S(2)}) collective-permute-start(bf16[8,96,128]{2,1,0:T(8,128)(2,1)S(1)} %broadcast_select_fusion.kept), channel_id=1, source_target_pairs={{0,16},{8,24},{16,0},{24,8},{1,17},{9,25},{17,1},{25,9},{2,18},{10... | collective-permute-start | bytes 589832 | tf_op jit(solution)/shard_map/ppermute | solution.py:337
  26.1 0.7 %copy-start.2 = (bf16[8,96,128]{2,1,0:T(8,128)(2,1)}, bf16[8,96,128]{2,1,0:T(8,128)(2,1)S(1)}, u32[]{:S(2)}) copy-start(bf16[8,96,128]{2,1,0:T(8,128)(2,1)S(1)} %collective-permute-done.1.received) | copy-start | bytes 589828

commit v3 on v2

--- a/solution.py
+++ b/solution.py
@@ -27,10 +27,14 @@
 BY = LY // KY
 GROUPS = BX * BY
 NX = LX + 2 * MARGIN
-NY = LY + 2 * EDGE
-KROWS = 8 + 2 * LY + 8
+NY = 89
+KROWS = 145
+SPREAD = LX * KROWS + 7
+VOLUME = NX * NY + 6
+SUMS = 9
 CELLS = KX * KY * KZ
 CHUNK = 256
+UNROLL = 32
 
 
 def pieces_of(value):
@@ -96,7 +100,9 @@
             store(x, image.astype(jnp.bfloat16).astype(jnp.float32))
 
 
-def own_kernels(choice, own, migration, column_gain, kernels):
+def own_kernels(
+    choice, own, migration, column_gain, kernels, deeper, shallower, edges, powers
+):
     gap = jnp.zeros((SEGMENT - KZ, migration.shape[1]), jnp.bfloat16)
     rows = []
     for j in range(PACKED):
@@ -115,11 +121,24 @@
     def store(x, image):
         for by in range(BY):
             row = x * KROWS + 8 + by * 16
-            kernels[row : row + 8, :] = image[by * KY : (by + 1) * KY]
+            kernel = image[by * KY : (by + 1) * KY]
+            kernels[row : row + 8, :] = kernel
+            row = x * LY + by * KY
+            shallower[row : row + 8, :] = pltpu.roll(kernel, LANES - 1, 1)
+            deeper[row : row + 8, :] = pltpu.roll(kernel, 1, 1)
 
     migrate(
         jnp.concatenate(rows), migration, jnp.transpose(column_gain[...]), gains[:1], store
     )
+    for g in range(GROUPS):
+        base = g // BY * KX * KROWS + g % BY * 16 + 8
+        power = None
+        for x in range(KX):
+            kernel = kernels[base + x * KROWS : base + x * KROWS + 8, :]
+            power = kernel * kernel if power is None else power + kernel * kernel
+        powers[g * SUMS : g * SUMS + 8, :] = power
+        for index, row in enumerate((base, base + KY - 1)):
+            edges[index, g * 8 : g * 8 + 8, :] = kernels[pl.ds(row, 8, stride=KROWS), :]
 
 
 def track(
@@ -130,6 +149,10 @@
     migration,
     column_gain,
     kernels,
+    deeper,
+    shallower,
+    edges,
+    kernel_powers,
     shift_cells,
     scores,
     displacement,
@@ -141,13 +164,12 @@
     zero = jnp.zeros((NY, LANES), jnp.float32)
     for x in list(range(MARGIN)) + list(range(LX + MARGIN, NX)):
         volume[x * NY : (x + 1) * NY, :] = zero
-    for x in range(LX):
-        base = (x + MARGIN) * NY
-        volume[base : base + EDGE, :] = zero[:EDGE]
-        volume[base + EDGE + LY : base + NY, :] = zero[:EDGE]
+    for x in range(MARGIN, LX + MARGIN):
+        volume[x * NY : x * NY + MARGIN, :] = zero[:MARGIN]
+        volume[x * NY + MARGIN + LY : (x + 1) * NY, :] = zero[: NY - MARGIN - LY]
 
     def store(x, image):
-        base = (x + MARGIN) * NY + EDGE
+        base = (x + MARGIN) * NY + MARGIN
         volume[base : base + LY, :] = image
 
     pieces = [jnp.where(keep, kept[b], received[b]) for b in range(kept.shape[0])]
@@ -156,36 +178,40 @@
     columns = jnp.transpose(column_gain[...])
     migrate(right, migration, columns, depth_row(choice, kept)[:1], store)
 
-    place = lax.broadcasted_iota(jnp.int32, (8, LANES), 1)
-    place = (place + 8) % LANES // SEGMENT
-    segment = [place == j for j in range(PACKED)]
+    place = lax.broadcasted_iota(jnp.int32, (16, LANES), 1)
+    segment = [((place + 8) & (LANES - 1)) // SEGMENT == j for j in range(PACKED)]
     row_number = lax.broadcasted_iota(jnp.int32, (8, LANES), 0)
 
     def group(g, carry):
         bx = g // BY
-        by = g % BY
+        by = g & (BY - 1)
         starts = []
         turns = []
         for j in range(PACKED):
             first = bx * KX + MARGIN + shift[0, 0, bx, j, by]
-            second = by * KY + EDGE + shift[1, 0, bx, j, by]
+            second = by * KY + MARGIN + shift[1, 0, bx, j, by]
             starts.append(first * NY + second)
-            turns.append((j * KZ - EDGE + 2 * LANES - shift[2, 0, bx, j, by]) % LANES)
-
-        def gather(offset, stride):
+            turns.append((j * KZ - EDGE + LANES - shift[2, 0, bx, j, by]) & (LANES - 1))
+
+        def gather(offsets, stride=None):
             value = None
             for j in range(PACKED):
-                start = starts[j] + offset
-                if stride == 1:
-                    rows = volume[pl.ds(start, 8), :]
-                else:
-                    rows = volume[pl.ds(start, 8, stride=stride), :]
+                pair = []
+                for offset in offsets:
+                    if stride is None:
+                        pair.append(volume[pl.ds(starts[j] + offset, 8), :])
+                    else:
+                        pair.append(volume[pl.ds(starts[j] + offset, 8, stride=stride), :])
+                rows = jnp.concatenate(pair).astype(jnp.bfloat16)
                 rows = pltpu.roll(rows, turns[j], 1)
                 value = rows if value is None else jnp.where(segment[j], rows, value)
-            return value
-
-        base = bx * KX * KROWS + by * 16 + 8
-        window = [gather((x - 1) * NY, 1) for x in range(KX + 2)]
+            value = value.astype(jnp.float32)
+            return [value[:8], value[8:]]
+
+        window = []
+        for x in range(-1, KX, 2):
+            window += gather((x * NY, (x + 1) * NY))
+        before, after = gather((-1, KY), NY)
         square = [value * value for value in window]
         middle = square[2]
         for x in range(3, KX):
@@ -194,11 +220,12 @@
         pair_high = square[KX] + square[KX + 1]
         center = middle + (square[1] + square[KX])
         cross = [None] * 7
-        power = None
 
         def add(index, value):
             cross[index] = value if cross[index] is None else cross[index] + value
 
+        base = bx * KX * KROWS + by * 16 + 8
+        flat = bx * KX * LY + by * KY
         for x in range(KX):
             row = base + x * KROWS
             kernel = kernels[pl.ds(row, 8), :]
@@ -207,29 +234,29 @@
             add(2, kernel * window[x + 2])
             add(3, kernels[pl.ds(row + 1, 8), :] * window[x + 1])
             add(4, kernels[pl.ds(row - 1, 8), :] * window[x + 1])
-            add(5, pltpu.roll(kernel, LANES - 1, 1) * window[x + 1])
-            add(6, pltpu.roll(kernel, 1, 1) * window[x + 1])
-            power = kernel * kernel if power is None else power + kernel * kernel
-        before = gather(-1, NY)
-        after = gather(KY, NY)
-        add(3, kernels[pl.ds(base, 8, stride=KROWS), :] * before)
-        add(4, kernels[pl.ds(base + KY - 1, 8, stride=KROWS), :] * after)
+            aligned = pl.ds(pl.multiple_of(flat + x * LY, 8), 8)
+            add(5, shallower[aligned, :] * window[x + 1])
+            add(6, deeper[aligned, :] * window[x + 1])
+        rows = pl.ds(pl.multiple_of(g * 8, 8), 8)
+        add(3, edges[0, rows, :] * before)
+        add(4, edges[1, rows, :] * after)
         low = jnp.where(row_number < KY - 1, center, 0.0) + before * before
         high = jnp.where(row_number > 0, center, 0.0) + after * after
         held = cross[:5] + [center, middle + pair_low, middle + pair_high]
-        held += [low, high, power, cross[5], cross[6]]
+        held += [low, high, cross[5], cross[6]]
         for index, value in enumerate(held):
-            sums[index, pl.ds(g * 8, 8), :] = value
+            sums[index, pl.ds(g * SUMS, 8), :] = value
         return carry
 
-    lax.fori_loop(0, GROUPS, group, 0)
+    lax.fori_loop(0, GROUPS, group, 0, unroll=UNROLL)
 
     def rows_of(index):
         parts = []
         for bx in range(BX):
             value = None
             for y in range(KY):
-                rows = sums[index, pl.ds(bx * BY * 8 + y, BY, stride=8), :]
+                place = pl.ds(bx * BY * SUMS + y, BY, stride=SUMS)
+                rows = sums[index, place, :] if index < 12 else kernel_powers[place, :]
                 value = rows if value is None else value + rows
             parts.append(value)
         return parts
@@ -258,12 +285,12 @@
     (first,) = totals((0, 1, 2, 3), (0,))
     second, second_low, second_high = totals((4, 5, 6, 7), (0, -1, 1))
     third, third_low, third_high = totals((8, 9, 10, 11), (0, -1, 1))
-    (fourth,) = totals((12, 12, 12, 12), (1,))
+    (fourth,) = totals((12, 12, 12, 12), (0,))
     cross = [lanes_of(first, place) for place in range(4)]
-    cross += [second, lanes_of(third_low, 3), fourth]
+    cross += [second, lanes_of(third_low, 2), lanes_of(third_high, 3)]
     powers = [lanes_of(second, place) for place in (1, 2, 3)]
     powers += [third, lanes_of(third, 1), lanes_of(second_low, 1), lanes_of(second_high, 1)]
-    kernel_power = lanes_of(third, 2) * (1.0 / CELLS) + EPSILON
+    kernel_power = fourth * (1.0 / CELLS) + EPSILON
     result = []
     for index in range(7):
         mean = cross[index] * (1.0 / CELLS)
@@ -289,6 +316,10 @@
     return [pl.BlockSpec(memory_space=pltpu.VMEM)] * count
 
 
+def pinned(array):
+    return pltpu.with_memory_space_constraint(array, pltpu.VMEM)
+
+
 def per_device(element_data, migration, column_gain, depth_gain, coarse_shift, reference_frame):
     elements_here, frames_here, depth = element_data.shape
     depth_here = depth_gain.shape[0]
@@ -308,6 +339,7 @@
             out_specs=on_chip(1)[0],
             out_shape=jax.ShapeDtypeStruct((slabs, WINDOW, LANES), jnp.bfloat16),
             scratch_shapes=[pltpu.VMEM((EDGE, LANES), jnp.float32)],
+            compiler_params=pltpu.CompilerParams(vmem_limit_bytes=4 << 20),
             name="window_rows",
         )(own_data, depth_gain.reshape(1, STEP))
         own = lax.all_to_all(windows, "slab", split_axis=0, concat_axis=0, tiled=True)
@@ -341,29 +373,42 @@
 
     gain_table = column_gain.reshape(-1, LANES)
     scalars = pl.BlockSpec(memory_space=pltpu.SMEM)
-    kernels = pl.pallas_call(
+    own_shapes = [(SPREAD, LANES), (LX * LY, LANES), (LX * LY, LANES)]
+    own_shapes += [(2, GROUPS * 8, LANES), (GROUPS * SUMS, LANES)]
+    kernel_arrays = pl.pallas_call(
         own_kernels,
         in_specs=[scalars] + on_chip(3),
-        out_specs=on_chip(1)[0],
-        out_shape=jax.ShapeDtypeStruct((LX * KROWS, LANES), jnp.float32),
+        out_specs=on_chip(5),
+        out_shape=[pltpu.VMEM(shape, jnp.float32) for shape in own_shapes],
+        compiler_params=pltpu.CompilerParams(vmem_limit_bytes=16 << 20),
         name="own_kernels",
-    )(choice, own, migration, gain_table)
+    )(choice, pinned(own), pinned(migration), gain_table)
 
     turn = (0, 1, 2, 4, 3)
     shifts = coarse_shift.transpose(turn)
     shapes = [jax.ShapeDtypeStruct((n,) + shifts.shape[1:], jnp.float32) for n in (7, 3)]
     scores, displacement = pl.pallas_call(
         track,
-        in_specs=[scalars, scalars] + on_chip(6),
+        in_specs=[scalars, scalars] + on_chip(10),
         out_specs=on_chip(2),
         out_shape=shapes,
         scratch_shapes=[
-            pltpu.VMEM((NX * NY, LANES), jnp.float32),
-            pltpu.VMEM((13, GROUPS * 8, LANES), jnp.float32),
+            pltpu.VMEM((VOLUME, LANES), jnp.float32),
+            pltpu.VMEM((12, GROUPS * SUMS, LANES), jnp.float32),
             pltpu.VMEM((LANES + 16, LANES), jnp.float32),
         ],
+        compiler_params=pltpu.CompilerParams(vmem_limit_bytes=24 << 20),
         name="track",
-    )(choice, shifts, kept, received, migration, gain_table, kernels, shifts)
+    )(
+        choice,
+        shifts,
+        pinned(kept),
+        pinned(received),
+        pinned(migration),
+        gain_table,
+        *[pinned(array) for array in kernel_arrays],
+        shifts,
+    )
     return scores.transpose(turn), displacement.transpose(turn)
 
 

time: 38.1 us -> 30.5 us (0.80)
  Pallas kernels: 17.7 us -> 6.44 us
  local copies, waits for them, and re-layouts: 0.68 us -> 4.45 us
  other arithmetic: 0.58 us -> 0.1 us
  waiting for transfers between devices: 0.79 us -> 1.23 us
    pallas_call x1, Pallas kernels: 11.1 us -> 4.35 us  [per_device(): pl.pallas_call(track, in_specs=[scalars, scalars] + on_chip(10), out_spec...]
    unnamed x6 -> x14, local copies, waits for them, and re-layouts: 0.68 us -> 4.45 us
    pallas_call x1, Pallas kernels: 4.9 us -> 2.01 us  [per_device(): pl.pallas_call(own_kernels, in_specs=[scalars] + on_chip(3), out_specs=on...]
    pallas_call x1, Pallas kernels: 1.67 us -> 0.09 us  [per_device(): pl.pallas_call(window_rows, in_specs=on_chip(2), out_specs=on_chip(1)[0],...]
    another operation x1, other arithmetic: 0.55 us -> 0.08 us  [per_device(): jnp.stack([keep] + [jnp.asarray(place, jnp.int32) for place in places])]
    ppermute x2, waiting for transfers between devices: 0.79 us -> 1.23 us  [per_device(): lax.ppermute(kept, 'frame', [(i, i ^ bit) for i in range(frames)])]
  transfers between devices with their start and end apart: 2 -> 2, of which waited for: 1 -> 2; matrix products, arithmetic and copies ran while one was open for 1% -> 0% of each run, Pallas kernels for 13% -> 7%
where the time goes in v3:
time: 30.5 us; the launch traced here: 30.2 us
  blocking collectives  15 us (49%)
  Pallas kernels  6.44 us (21%)
  local copies, waits for them, and re-layouts  4.45 us (15%)
  starting transfers between devices  1.59 us (5%)
  between operations  1.32 us (4%)
  waiting for transfers between devices  1.23 us (4%)
    all_to_all x1, blocking collectives, per_device(): lax.all_to_all(windows, 'slab', split_axis=0, concat_axis=0, tiled=True)  15 us
    unnamed x14, local copies, waits for them, and re-layouts  4.45 us
    pallas_call x1, Pallas kernels, per_device(): pl.pallas_call(track, in_specs=[scalars, scalars] + on_chip(10), out_spec...  4.35 us
    pallas_call x1, Pallas kernels, per_device(): pl.pallas_call(own_kernels, in_specs=[scalars] + on_chip(3), out_specs=on...  2.01 us
    ppermute x2, starting transfers between devices, per_device(): lax.ppermute(kept, 'frame', [(i, i ^ bit) for i in range(frames)])  1.59 us
    ppermute x2, waiting for transfers between devices, per_device(): lax.ppermute(kept, 'frame', [(i, i ^ bit) for i in range(frames)])  1.23 us
  transfers between devices with their start and end apart: 2, of which 2 were waited for; matrix products, arithmetic and copies ran while one was open for 0% of the time, Pallas kernels for 7%

profile of v3, /device:TPU:0, one launch (start us, length us, event | category | flops | bytes accessed | tf_op | source)
XLA Modules:
  0.0 30.2 jit_solution(11229455016642974077)
XLA Ops:
  0.6 0.0 copy-start.2
  0.6 0.9 %copy-done.2 = bf16[128,1,512]{2,0,1:T(8,128)(2,1)S(1)} copy-done((bf16[128,1,512]{2,0,1:T(8,128)(2,1)S(1)}, bf16[128,1,512]{2,0,1:T(8,128)(2,1)}, u32[]{:S(2)}) %copy-start.2) | copy-done | bytes 131096
  1.5 0.0 copy-start.6
  1.5 0.7 %copy-done.6 = f32[64]{0:T(128)S(1)} copy-done((f32[64]{0:T(128)S(1)}, f32[64]{0:T(128)}, u32[]{:S(2)}) %copy-start.6) | copy-done | bytes 280
  2.2 0.0 copy-start.3
  2.2 0.0 copy-start.5
  2.2 0.1 window_rows.1
  2.3 15.0 %all_to_all.5.own = bf16[8,96,128]{2,1,0:T(8,128)(2,1)S(1)} all-to-all(bf16[8,96,128]{2,1,0:T(8,128)(2,1)S(1)} %window_rows.1), channel_id=1, replica_groups=mesh['frame'=4,'slab'=8] {'slab'}, dimensions={0} | all-to-all | bytes 393216 | tf_op jit(solution)/shard_map/all_to_all | solution.py:345
  17.3 0.0 collective-permute-start
  18.0 0.8 %collective-permute-done = bf16[8,96,128]{2,1,0:T(8,128)(2,1)S(1)} collective-permute-done((bf16[8,96,128]{2,1,0:T(8,128)(2,1)S(1)}, bf16[8,96,128]{2,1,0:T(8,128)(2,1)S(1)}, u32[]{:S(2)}, u32[]{:S(2)}) %collective-permute-start) | collective-permute-done | bytes 196640 | tf_op jit(solution)/shard_map/ppermute | solution.py:369
  18.8 1.6 %collective-permute-start.1 = (bf16[8,96,128]{2,1,0:T(8,128)(2,1)S(1)}, bf16[8,96,128]{2,1,0:T(8,128)(2,1)S(1)}, u32[]{:S(2)}, u32[]{:S(2)}) collective-permute-start(bf16[8,96,128]{2,1,0:T(8,128)(2,1)S(1)} %broadcast_select_fusion.kept), channel_id=1, source_target_pairs={{0,16},{8,24},{16,0},{24,8},{1,17},{9,25},{17,1},{25,9},{2,18},{10... | collective-permute-start | bytes 589832 | tf_op jit(solution)/shard_map/ppermute | solution.py:369
  20.4 0.1 pad_add_fusion.choice
  20.5 0.0 copy-start
  20.5 2.2 %copy-done = bf16[2048,1024]{1,0:T(8,128)(2,1)S(1)} copy-done((bf16[2048,1024]{1,0:T(8,128)(2,1)S(1)}, bf16[2048,1024]{1,0:T(8,128)(2,1)}, u32[]{:S(2)}) %copy-start) | copy-done | bytes 4194328
  22.6 0.0 copy-start.4
  22.6 0.7 %copy-done.4 = f32[2048]{0:T(1024)S(1)} copy-done((f32[2048]{0:T(1024)S(1)}, f32[2048]{0:T(1024)}, u32[]{:S(2)}) %copy-start.4) | copy-done | bytes 8216
  23.3 0.0 copy-start.1
  23.3 2.0 %own_kernels.1 = (f32[4647,128]{1,0:T(8,128)S(1)}, f32[2048,128]{1,0:T(8,128)S(1)}, f32[2048,128]{1,0:T(8,128)S(1)}, f32[2,256,128]{2,1,0:T(8,128)S(1)}, f32[288,128]{1,0:T(8,128)S(1)}) custom-call(s32[4]{0:T(128)S(1)} %pad_add_fusion.choice, bf16[8,96,128]{2,1,0:T(8,128)(2,1)S(1)} %all_to_all.5.own, bf16[2048,1024]{1,0:T(8,128)(2,1)S(1)} %copy-done, ...), custom_call_target="tpu_custom_call" | custom-call | tf_op jit(solution)/shard_map/own_kernels/pallas_call | solution.py:378
  25.4 0.4 %collective-permute-done.1.received = bf16[8,96,128]{2,1,0:T(8,128)(2,1)S(1)} collective-permute-done((bf16[8,96,128]{2,1,0:T(8,128)(2,1)S(1)}, bf16[8,96,128]{2,1,0:T(8,128)(2,1)S(1)}, u32[]{:S(2)}, u32[]{:S(2)}) %collective-permute-start.1) | collective-permute-done | bytes 196640 | tf_op jit(solution)/shard_map/ppermute | solution.py:369
  25.8 0.0 copy-done.3
  25.8 0.0 copy-done.5
  25.8 0.0 copy-done.1
  25.8 4.3 %track.1 = (f32[7,1,4,4,8]{4,3,2,1,0:T(4,128)}, f32[3,1,4,4,8]{4,3,2,1,0:T(4,128)}) custom-call(s32[4]{0:T(128)S(1)} %pad_add_fusion.choice, s32[3,1,4,4,8]{4,3,2,1,0:T(4,128)S(1)} %bitcast.13, bf16[8,96,128]{2,1,0:T(8,128)(2,1)S(1)} %broadcast_select_fusion.kept, bf16[8,96,128]{2,1,0:T(8,128)(2,1)S(1)} %collective-permute-done.1.received, ...), custom_call_target="tpu_custom_call" | custom-call | tf_op jit(solution)/shard_map/track/pallas_call | solution.py:390
  (1 shorter events, 0.0 us)
Async XLA Ops:
  0.6 0.9 %copy-start.2 = (bf16[128,1,512]{2,0,1:T(8,128)(2,1)S(1)}, bf16[128,1,512]{2,0,1:T(8,128)(2,1)}, u32[]{:S(2)}) copy-start(bf16[128,1,512]{2,0,1:T(8,128)(2,1)} %param.6) | copy-start | bytes 393220
  1.5 0.7 %copy-start.6 = (f32[64]{0:T(128)S(1)}, f32[64]{0:T(128)}, u32[]{:S(2)}) copy-start(f32[64]{0:T(128)} %param.9) | copy-start | bytes 772
  2.2 23.6 %copy-start.3 = (s32[3,1,4,8,4]{3,4,2,1,0:T(4,128)S(1)}, s32[3,1,4,8,4]{3,4,2,1,0:T(4,128)}, u32[]{:S(2)}) copy-start(s32[3,1,4,8,4]{3,4,2,1,0:T(4,128)} %param.10) | copy-start | bytes 4612
  2.2 23.6 %copy-start.5 = (f32[2048]{0:T(1024)S(1)}, f32[2048]{0:T(1024)}, u32[]{:S(2)}) copy-start(f32[2048]{0:T(1024)} %param.8) | copy-start | bytes 24580
  17.3 1.4 %collective-permute-start = (bf16[8,96,128]{2,1,0:T(8,128)(2,1)S(1)}, bf16[8,96,128]{2,1,0:T(8,128)(2,1)S(1)}, u32[]{:S(2)}, u32[]{:S(2)}) collective-permute-start(bf16[8,96,128]{2,1,0:T(8,128)(2,1)S(1)} %all_to_all.5.own), channel_id=1, source_target_pairs={{0,8},{8,0},{16,24},{24,16},{1,9},{9,1},{17,25},{25,17},{2,10},{10... | collective-permute-start | bytes 589832 | tf_op jit(solution)/shard_map/ppermute | solution.py:369
  18.8 7.0 %collective-permute-start.1 = (bf16[8,96,128]{2,1,0:T(8,128)(2,1)S(1)}, bf16[8,96,128]{2,1,0:T(8,128)(2,1)S(1)}, u32[]{:S(2)}, u32[]{:S(2)}) collective-permute-start(bf16[8,96,128]{2,1,0:T(8,128)(2,1)S(1)} %broadcast_select_fusion.kept), channel_id=1, source_target_pairs={{0,16},{8,24},{16,0},{24,8},{1,17},{9,25},{17,1},{25,9},{2,18},{10... | collective-permute-start | bytes 589832 | tf_op jit(solution)/shard_map/ppermute | solution.py:369
  20.5 2.2 %copy-start = (bf16[2048,1024]{1,0:T(8,128)(2,1)S(1)}, bf16[2048,1024]{1,0:T(8,128)(2,1)}, u32[]{:S(2)}) copy-start(bf16[2048,1024]{1,0:T(8,128)(2,1)} %migration.3) | copy-start | bytes 12582916
  22.6 0.7 %copy-start.4 = (f32[2048]{0:T(1024)S(1)}, f32[2048]{0:T(1024)}, u32[]{:S(2)}) copy-start(f32[2048]{0:T(1024)} %param.8) | copy-start | bytes 24580
  23.3 2.5 %copy-start.1 = (bf16[2048,1024]{1,0:T(8,128)(2,1)S(1)}, bf16[2048,1024]{1,0:T(8,128)(2,1)}, u32[]{:S(2)}) copy-start(bf16[2048,1024]{1,0:T(8,128)(2,1)} %migration.3) | copy-start | bytes 12582916

commit v4 on v3

--- a/solution.py
+++ b/solution.py
@@ -33,8 +33,8 @@
 VOLUME = NX * NY + 6
 SUMS = 9
 CELLS = KX * KY * KZ
-CHUNK = 256
-UNROLL = 32
+STRIP = 4
+LATE = False
 
 
 def pieces_of(value):
@@ -43,9 +43,17 @@
     return high, middle, value - high - middle
 
 
-def window_rows(element_data, depth_gain, windows, row):
+def window_rows(element_data, depth_gain, windows, held, gain, row, arrived):
+    columns = element_data.shape[1] // LANES
+    copies = [pltpu.make_async_copy(depth_gain, gain, arrived.at[columns])]
+    for column in range(columns):
+        part = element_data.at[:, column * LANES : (column + 1) * LANES]
+        copies.append(pltpu.make_async_copy(part, held.at[column], arrived.at[column]))
+    for copy in copies:
+        copy.start()
     row[...] = jnp.zeros(row.shape, jnp.float32)
-    for index, piece in enumerate(pieces_of(depth_gain[...])):
+    copies[0].wait()
+    for index, piece in enumerate(pieces_of(gain[...])):
         row[index : index + 1, :STEP] = piece
     note = row[...].astype(jnp.bfloat16)
     slabs = windows.shape[0]
@@ -60,8 +68,9 @@
 
     put(0, 0, empty)
     put(slabs - 1, EDGE + STEP, empty)
-    for column in range(element_data.shape[1] // LANES):
-        turned = jnp.transpose(element_data[:, column * LANES : (column + 1) * LANES])
+    for column in range(columns):
+        copies[1 + column].wait()
+        turned = jnp.transpose(held[column])
         for unit in range(LANES // EDGE):
             slab, place = divmod(column * LANES + unit * EDGE, STEP)
             rows = turned[unit * EDGE : (unit + 1) * EDGE]
@@ -84,20 +93,18 @@
     return jnp.where(lane >= EDGE + STEP, pltpu.roll(of(3), EDGE + STEP, 1), row)
 
 
-def migrate(right, migration, columns, gains, store):
-    for chunk in range(LX * LY // CHUNK):
-        raw = lax.dot_general(
-            migration[chunk * CHUNK : (chunk + 1) * CHUNK, :],
-            right,
-            (((1,), (1,)), ((), ())),
-            preferred_element_type=jnp.float32,
-        )
-        for piece in range(CHUNK // LY):
-            x = chunk * (CHUNK // LY) + piece
-            row = x * LY
-            gain = columns[row % LANES : row % LANES + LY, row // LANES : row // LANES + 1]
-            image = (raw[piece * LY : (piece + 1) * LY] * jnp.broadcast_to(gain, (LY, LANES))) * gains
-            store(x, image.astype(jnp.bfloat16).astype(jnp.float32))
+def migrate(right, migration, columns, gains, store, begin, end):
+    raw = lax.dot_general(
+        migration[begin * LY : end * LY, :],
+        right,
+        (((1,), (1,)), ((), ())),
+        preferred_element_type=jnp.float32,
+    )
+    for x in range(begin, end):
+        row = x * LY
+        gain = columns[row % LANES : row % LANES + LY, row // LANES : row // LANES + 1]
+        image = raw[(x - begin) * LY : (x - begin + 1) * LY] * jnp.broadcast_to(gain, (LY, LANES))
+        store(x, (image * gains).astype(jnp.bfloat16).astype(jnp.float32))
 
 
 def own_kernels(
@@ -109,7 +116,7 @@
         pieces = [own[b, EDGE + j * KZ : EDGE + (j + 1) * KZ, :] for b in range(own.shape[0])]
         rows += [jnp.concatenate(pieces, axis=1), gap]
     lane = lax.broadcasted_iota(jnp.int32, (8, LANES), 1)
-    note = own[choice[2], :EDGE, :].astype(jnp.float32)
+    note = own[choice[1], :EDGE, :].astype(jnp.float32)
     row = jnp.broadcast_to(note[0:1] + note[1:2] + note[2:3], (8, LANES))
     gains = row
     for j in range(1, PACKED):
@@ -127,9 +134,10 @@
             shallower[row : row + 8, :] = pltpu.roll(kernel, LANES - 1, 1)
             deeper[row : row + 8, :] = pltpu.roll(kernel, 1, 1)
 
-    migrate(
-        jnp.concatenate(rows), migration, jnp.transpose(column_gain[...]), gains[:1], store
-    )
+    right = jnp.concatenate(rows)
+    columns = jnp.transpose(column_gain[...])
+    for x in range(0, LX, STRIP):
+        migrate(right, migration, columns, gains[:1], store, x, x + STRIP)
     for g in range(GROUPS):
         base = g // BY * KX * KROWS + g % BY * 16 + 8
         power = None
@@ -143,7 +151,7 @@
 
 def track(
     choice,
-    shift,
+    shift_table,
     kept,
     received,
     migration,
@@ -159,7 +167,11 @@
     volume,
     sums,
     turned,
+    shift,
+    arrived,
 ):
+    positions = pltpu.make_async_copy(shift_table, shift, arrived)
+    positions.start()
     keep = choice[0] == 1
     zero = jnp.zeros((NY, LANES), jnp.float32)
     for x in list(range(MARGIN)) + list(range(LX + MARGIN, NX)):
@@ -176,15 +188,17 @@
     spare = jnp.zeros((LANES - WINDOW, migration.shape[1]), jnp.bfloat16)
     right = jnp.concatenate([jnp.concatenate(pieces, axis=1), spare])
     columns = jnp.transpose(column_gain[...])
-    migrate(right, migration, columns, depth_row(choice, kept)[:1], store)
+    gains = depth_row(choice, kept)[:1]
+
+    def strip(begin, end):
+        migrate(right, migration, columns, gains, store, begin, end)
 
     place = lax.broadcasted_iota(jnp.int32, (16, LANES), 1)
     segment = [((place + 8) & (LANES - 1)) // SEGMENT == j for j in range(PACKED)]
     row_number = lax.broadcasted_iota(jnp.int32, (8, LANES), 0)
 
-    def group(g, carry):
-        bx = g // BY
-        by = g & (BY - 1)
+    def group(bx, by):
+        g = bx * BY + by
         starts = []
         turns = []
         for j in range(PACKED):
@@ -234,10 +248,10 @@
             add(2, kernel * window[x + 2])
             add(3, kernels[pl.ds(row + 1, 8), :] * window[x + 1])
             add(4, kernels[pl.ds(row - 1, 8), :] * window[x + 1])
-            aligned = pl.ds(pl.multiple_of(flat + x * LY, 8), 8)
+            aligned = pl.ds(flat + x * LY, 8)
             add(5, shallower[aligned, :] * window[x + 1])
             add(6, deeper[aligned, :] * window[x + 1])
-        rows = pl.ds(pl.multiple_of(g * 8, 8), 8)
+        rows = pl.ds(g * 8, 8)
         add(3, edges[0, rows, :] * before)
         add(4, edges[1, rows, :] * after)
         low = jnp.where(row_number < KY - 1, center, 0.0) + before * before
@@ -246,9 +260,16 @@
         held += [low, high, cross[5], cross[6]]
         for index, value in enumerate(held):
             sums[index, pl.ds(g * SUMS, 8), :] = value
-        return carry
-
-    lax.fori_loop(0, GROUPS, group, 0, unroll=UNROLL)
+
+    strips = [(x, min(x + STRIP, LX)) for x in range(0, LX, STRIP)]
+    for bx in range(BX):
+        reach = min(KX * bx + KX + CMAX, LX - 1) if LATE else LX - 1
+        while strips and strips[0][0] <= reach:
+            strip(*strips.pop(0))
+        if bx == 0:
+            positions.wait()
+        for by in range(BY):
+            group(bx, by)
 
     def rows_of(index):
         parts = []
@@ -320,6 +341,10 @@
     return pltpu.with_memory_space_constraint(array, pltpu.VMEM)
 
 
+def in_hbm(array):
+    return pltpu.with_memory_space_constraint(array, pltpu.HBM)
+
+
 def per_device(element_data, migration, column_gain, depth_gain, coarse_shift, reference_frame):
     elements_here, frames_here, depth = element_data.shape
     depth_here = depth_gain.shape[0]
@@ -335,13 +360,18 @@
     if elements_here == LANES:
         windows = pl.pallas_call(
             window_rows,
-            in_specs=on_chip(2),
+            in_specs=[pl.BlockSpec(memory_space=pltpu.HBM)] * 2,
             out_specs=on_chip(1)[0],
             out_shape=jax.ShapeDtypeStruct((slabs, WINDOW, LANES), jnp.bfloat16),
-            scratch_shapes=[pltpu.VMEM((EDGE, LANES), jnp.float32)],
+            scratch_shapes=[
+                pltpu.VMEM((depth // LANES, LANES, LANES), jnp.bfloat16),
+                pltpu.VMEM((1, STEP), jnp.float32),
+                pltpu.VMEM((EDGE, LANES), jnp.float32),
+                pltpu.SemaphoreType.DMA((depth // LANES + 1,)),
+            ],
             compiler_params=pltpu.CompilerParams(vmem_limit_bytes=4 << 20),
             name="window_rows",
-        )(own_data, depth_gain.reshape(1, STEP))
+        )(in_hbm(own_data), in_hbm(depth_gain.reshape(1, STEP)))
         own = lax.all_to_all(windows, "slab", split_axis=0, concat_axis=0, tiled=True)
         places = [(slab - 1) % slabs, slab, (slab + 1) % slabs]
     else:
@@ -359,18 +389,7 @@
             own = own.at[place, :3, :STEP].set(note.astype(jnp.bfloat16))
         places = [0, 1, 2]
 
-    kept = own
-    received = own
-    bit = 1
-    while bit < frames:
-        if bit > 1:
-            mine = (chosen ^ frame) & (bit // 2) == 0
-            kept = jnp.where(mine, kept, received)
-        received = lax.ppermute(kept, "frame", [(i, i ^ bit) for i in range(frames)])
-        bit *= 2
-    keep = ((chosen ^ frame) & (frames // 2) == 0).astype(jnp.int32)
-    choice = jnp.stack([keep] + [jnp.asarray(place, jnp.int32) for place in places])
-
+    places = [jnp.asarray(place, jnp.int32) for place in places]
     gain_table = column_gain.reshape(-1, LANES)
     scalars = pl.BlockSpec(memory_space=pltpu.SMEM)
     own_shapes = [(SPREAD, LANES), (LX * LY, LANES), (LX * LY, LANES)]
@@ -382,26 +401,40 @@
         out_shape=[pltpu.VMEM(shape, jnp.float32) for shape in own_shapes],
         compiler_params=pltpu.CompilerParams(vmem_limit_bytes=16 << 20),
         name="own_kernels",
-    )(choice, pinned(own), pinned(migration), gain_table)
+    )(jnp.stack(places), pinned(own), pinned(migration), gain_table)
+
+    kept = own
+    received = own
+    bit = 1
+    while bit < frames:
+        if bit > 1:
+            mine = (chosen ^ frame) & (bit // 2) == 0
+            kept = jnp.where(mine, kept, received)
+        received = lax.ppermute(kept, "frame", [(i, i ^ bit) for i in range(frames)])
+        bit *= 2
+    keep = ((chosen ^ frame) & (frames // 2) == 0).astype(jnp.int32)
+    choice = jnp.stack([keep] + places)
 
     turn = (0, 1, 2, 4, 3)
     shifts = coarse_shift.transpose(turn)
     shapes = [jax.ShapeDtypeStruct((n,) + shifts.shape[1:], jnp.float32) for n in (7, 3)]
     scores, displacement = pl.pallas_call(
         track,
-        in_specs=[scalars, scalars] + on_chip(10),
+        in_specs=[scalars, pl.BlockSpec(memory_space=pltpu.HBM)] + on_chip(10),
         out_specs=on_chip(2),
         out_shape=shapes,
         scratch_shapes=[
             pltpu.VMEM((VOLUME, LANES), jnp.float32),
             pltpu.VMEM((12, GROUPS * SUMS, LANES), jnp.float32),
             pltpu.VMEM((LANES + 16, LANES), jnp.float32),
+            pltpu.SMEM(shifts.shape, jnp.int32),
+            pltpu.SemaphoreType.DMA,
         ],
         compiler_params=pltpu.CompilerParams(vmem_limit_bytes=24 << 20),
         name="track",
     )(
         choice,
-        shifts,
+        in_hbm(shifts),
         pinned(kept),
         pinned(received),
         pinned(migration),

time: 30.5 us -> 30.9 us (1.013)
  Pallas kernels: 6.44 us -> 8.26 us
  local copies, waits for them, and re-layouts: 4.45 us -> 2.9 us
    pallas_call x2, Pallas kernels: 4.43 us -> 6.26 us  [the longest x1 5.15 us: per_device(): pl.pallas_call(track, in_specs=[scalars, pl.BlockSpec(memory_space=pltpu....]
    unnamed x14 -> x8, local copies, waits for them, and re-layouts: 4.45 us -> 2.9 us
where the time goes in v4:
time: 30.9 us; the launch traced here: 30.4 us
  blocking collectives  15 us (49%)
  Pallas kernels  8.26 us (27%)
  local copies, waits for them, and re-layouts  2.9 us (9%)
  starting transfers between devices  1.59 us (5%)
  between operations  1.33 us (4%)
  waiting for transfers between devices  1.15 us (4%)
    all_to_all x1, blocking collectives, per_device(): lax.all_to_all(windows, 'slab', split_axis=0, concat_axis=0, tiled=True)  15 us
    pallas_call x1, Pallas kernels, per_device(): pl.pallas_call(track, in_specs=[scalars, pl.BlockSpec(memory_space=pltpu....  5.15 us
    unnamed x8, local copies, waits for them, and re-layouts  2.9 us
    pallas_call x1, Pallas kernels, per_device(): pl.pallas_call(own_kernels, in_specs=[scalars] + on_chip(3), out_specs=on...  2 us
    ppermute x2, starting transfers between devices, per_device(): lax.ppermute(kept, 'frame', [(i, i ^ bit) for i in range(frames)])  1.59 us
    ppermute x2, waiting for transfers between devices, per_device(): lax.ppermute(kept, 'frame', [(i, i ^ bit) for i in range(frames)])  1.15 us
    pallas_call x1, Pallas kernels, per_device(): pl.pallas_call(window_rows, in_specs=[pl.BlockSpec(memory_space=pltpu.HBM...  1.11 us
  transfers between devices with their start and end apart: 2, of which 2 were waited for; matrix products, arithmetic and copies ran while one was open for 0% of the time, Pallas kernels for 7%

profile of v4, /device:TPU:0, one launch (start us, length us, event | category | flops | bytes accessed | tf_op | source)
XLA Modules:
  0.0 30.4 jit_solution(17823784145605108536)
XLA Ops:
  0.6 0.0 copy-start.3
  0.6 1.1 %window_rows.1 = bf16[8,96,128]{2,1,0:T(8,128)(2,1)S(1)} custom-call(bf16[128,512]{1,0:T(8,128)(2,1)} %bitcast.14, f32[1,64]{1,0:T(1,128)} %bitcast.17), custom_call_target="tpu_custom_call" | custom-call | tf_op jit(solution)/shard_map/window_rows/pallas_call | solution.py:361
  1.8 15.0 %all_to_all.5.own = bf16[8,96,128]{2,1,0:T(8,128)(2,1)S(1)} all-to-all(bf16[8,96,128]{2,1,0:T(8,128)(2,1)S(1)} %window_rows.1), channel_id=1, replica_groups=mesh['frame'=4,'slab'=8] {'slab'}, dimensions={0} | all-to-all | bytes 393216 | tf_op jit(solution)/shard_map/all_to_all | solution.py:375
  16.8 0.0 collective-permute-start
  17.5 0.8 %collective-permute-done = bf16[8,96,128]{2,1,0:T(8,128)(2,1)S(1)} collective-permute-done((bf16[8,96,128]{2,1,0:T(8,128)(2,1)S(1)}, bf16[8,96,128]{2,1,0:T(8,128)(2,1)S(1)}, u32[]{:S(2)}, u32[]{:S(2)}) %collective-permute-start) | collective-permute-done | bytes 196640 | tf_op jit(solution)/shard_map/ppermute | solution.py:413
  18.3 1.6 %collective-permute-start.1 = (bf16[8,96,128]{2,1,0:T(8,128)(2,1)S(1)}, bf16[8,96,128]{2,1,0:T(8,128)(2,1)S(1)}, u32[]{:S(2)}, u32[]{:S(2)}) collective-permute-start(bf16[8,96,128]{2,1,0:T(8,128)(2,1)S(1)} %broadcast_select_fusion.kept), channel_id=1, source_target_pairs={{0,16},{8,24},{16,0},{24,8},{1,17},{9,25},{17,1},{25,9},{2,18},{10... | collective-permute-start | bytes 589832 | tf_op jit(solution)/shard_map/ppermute | solution.py:413
  19.8 0.1 pad_add_fusion.1.choice
  19.9 0.1 pad_add_fusion.choice
  20.0 0.0 copy-start
  20.0 2.2 %copy-done = bf16[2048,1024]{1,0:T(8,128)(2,1)S(1)} copy-done((bf16[2048,1024]{1,0:T(8,128)(2,1)S(1)}, bf16[2048,1024]{1,0:T(8,128)(2,1)}, u32[]{:S(2)}) %copy-start) | copy-done | bytes 4194328
  22.2 0.0 copy-start.2
  22.2 0.7 %copy-done.2 = f32[2048]{0:T(1024)S(1)} copy-done((f32[2048]{0:T(1024)S(1)}, f32[2048]{0:T(1024)}, u32[]{:S(2)}) %copy-start.2) | copy-done | bytes 8216
  22.9 0.0 copy-start.1
  22.9 2.0 %own_kernels.1 = (f32[4647,128]{1,0:T(8,128)S(1)}, f32[2048,128]{1,0:T(8,128)S(1)}, f32[2048,128]{1,0:T(8,128)S(1)}, f32[2,256,128]{2,1,0:T(8,128)S(1)}, f32[288,128]{1,0:T(8,128)S(1)}) custom-call(s32[3]{0:T(128)S(1)} %pad_add_fusion.1.choice, bf16[8,96,128]{2,1,0:T(8,128)(2,1)S(1)} %all_to_all.5.own, bf16[2048,1024]{1,0:T(8,128)(2,1)S(1)} %copy-done, ...), custom_call_target="tpu_custom_call" | custom-call | tf_op jit(solution)/shard_map/own_kernels/pallas_call | solution.py:397
  24.9 0.4 %collective-permute-done.1.received = bf16[8,96,128]{2,1,0:T(8,128)(2,1)S(1)} collective-permute-done((bf16[8,96,128]{2,1,0:T(8,128)(2,1)S(1)}, bf16[8,96,128]{2,1,0:T(8,128)(2,1)S(1)}, u32[]{:S(2)}, u32[]{:S(2)}) %collective-permute-start.1) | collective-permute-done | bytes 196640 | tf_op jit(solution)/shard_map/ppermute | solution.py:413
  25.3 0.0 copy-done.3
  25.3 0.0 copy-done.1
  25.3 5.2 %track.1 = (f32[7,1,4,4,8]{4,3,2,1,0:T(4,128)}, f32[3,1,4,4,8]{4,3,2,1,0:T(4,128)}) custom-call(s32[4]{0:T(128)S(1)} %pad_add_fusion.choice, s32[3,1,4,4,8]{4,3,2,1,0:T(4,128)} %bitcast.15, bf16[8,96,128]{2,1,0:T(8,128)(2,1)S(1)} %broadcast_select_fusion.kept, bf16[8,96,128]{2,1,0:T(8,128)(2,1)S(1)} %collective-permute-done.1.received, ...), custom_call_target="tpu_custom_call" | custom-call | tf_op jit(solution)/shard_map/track/pallas_call | solution.py:421
  (1 shorter events, 0.0 us)
Async XLA Ops:
  0.6 24.6 %copy-start.3 = (f32[2048]{0:T(1024)S(1)}, f32[2048]{0:T(1024)}, u32[]{:S(2)}) copy-start(f32[2048]{0:T(1024)} %param.8) | copy-start | bytes 24580
  16.8 1.4 %collective-permute-start = (bf16[8,96,128]{2,1,0:T(8,128)(2,1)S(1)}, bf16[8,96,128]{2,1,0:T(8,128)(2,1)S(1)}, u32[]{:S(2)}, u32[]{:S(2)}) collective-permute-start(bf16[8,96,128]{2,1,0:T(8,128)(2,1)S(1)} %all_to_all.5.own), channel_id=1, source_target_pairs={{0,8},{8,0},{16,24},{24,16},{1,9},{9,1},{17,25},{25,17},{2,10},{10... | collective-permute-start | bytes 589832 | tf_op jit(solution)/shard_map/ppermute | solution.py:413
  18.3 7.0 %collective-permute-start.1 = (bf16[8,96,128]{2,1,0:T(8,128)(2,1)S(1)}, bf16[8,96,128]{2,1,0:T(8,128)(2,1)S(1)}, u32[]{:S(2)}, u32[]{:S(2)}) collective-permute-start(bf16[8,96,128]{2,1,0:T(8,128)(2,1)S(1)} %broadcast_select_fusion.kept), channel_id=1, source_target_pairs={{0,16},{8,24},{16,0},{24,8},{1,17},{9,25},{17,1},{25,9},{2,18},{10... | collective-permute-start | bytes 589832 | tf_op jit(solution)/shard_map/ppermute | solution.py:413
  20.0 2.2 %copy-start = (bf16[2048,1024]{1,0:T(8,128)(2,1)S(1)}, bf16[2048,1024]{1,0:T(8,128)(2,1)}, u32[]{:S(2)}) copy-start(bf16[2048,1024]{1,0:T(8,128)(2,1)} %migration.3) | copy-start | bytes 12582916
  22.2 0.7 %copy-start.2 = (f32[2048]{0:T(1024)S(1)}, f32[2048]{0:T(1024)}, u32[]{:S(2)}) copy-start(f32[2048]{0:T(1024)} %param.8) | copy-start | bytes 24580
  22.9 2.4 %copy-start.1 = (bf16[2048,1024]{1,0:T(8,128)(2,1)S(1)}, bf16[2048,1024]{1,0:T(8,128)(2,1)}, u32[]{:S(2)}) copy-start(bf16[2048,1024]{1,0:T(8,128)(2,1)} %migration.3) | copy-start | bytes 12582916

commit v5 on v4

--- a/solution.py
+++ b/solution.py
@@ -43,7 +43,8 @@
     return high, middle, value - high - middle
 
 
-def window_rows(element_data, depth_gain, windows, held, gain, row, arrived):
+def window_rows(slab_number, element_data, depth_gain, windows, held, gain, row, arrived):
+    odd = slab_number[0] & 1
     columns = element_data.shape[1] // LANES
     copies = [pltpu.make_async_copy(depth_gain, gain, arrived.at[columns])]
     for column in range(columns):
@@ -56,7 +57,7 @@
     for index, piece in enumerate(pieces_of(gain[...])):
         row[index : index + 1, :STEP] = piece
     note = row[...].astype(jnp.bfloat16)
-    slabs = windows.shape[0]
+    slabs = windows.shape[0] * windows.shape[1]
     empty = jnp.zeros((EDGE, LANES), jnp.bfloat16)
     spare = lax.broadcasted_iota(jnp.int32, (EDGE, LANES), 0) < 3
 
@@ -64,7 +65,7 @@
         if 0 <= slab < slabs:
             if first == 0:
                 rows = jnp.where(spare, note, rows)
-            windows[slab, first : first + EDGE, :] = rows
+            windows[odd ^ (slab & 1), slab // 2, first : first + EDGE, :] = rows
 
     put(0, 0, empty)
     put(slabs - 1, EDGE + STEP, empty)
@@ -107,13 +108,65 @@
         store(x, (image * gains).astype(jnp.bfloat16).astype(jnp.float32))
 
 
+def block_table(shifts, table, spread):
+    j = lax.broadcasted_iota(jnp.int32, (PACKED, BY), 0)
+    by = lax.broadcasted_iota(jnp.int32, (PACKED, BY), 1)
+    spread[...] = jnp.zeros(spread.shape, jnp.float32)
+    for bx in range(BX):
+        first, second, third = (shifts[axis, 0, bx] for axis in range(3))
+        start = (first + (bx * KX + MARGIN)) * NY + second + by * KY + MARGIN
+        turn = (j * KZ + (LANES - EDGE) - third) & (LANES - 1)
+        for index, value in enumerate((start, turn)):
+            row = index * BX * PACKED + bx * PACKED
+            spread[row : row + PACKED, :BY] = value.astype(jnp.float32)
+    rows = BX * PACKED
+    row = lax.broadcasted_iota(jnp.int32, (rows, LANES), 0)
+    lane = lax.broadcasted_iota(jnp.int32, (rows, LANES), 1)
+    for index in range(2):
+        value = spread[index * rows : (index + 1) * rows, :]
+        value = pltpu.roll(value, 0, 1, stride=BY, stride_axis=0)
+        value = jnp.sum(jnp.where(lane // BY == row, value, 0.0), axis=0, keepdims=True)
+        table[index : index + 1, :] = value.astype(jnp.int32)
+
+
 def own_kernels(
-    choice, own, migration, column_gain, kernels, deeper, shallower, edges, powers
+    choice,
+    own,
+    migration_source,
+    column_gain,
+    shift_source,
+    kernels,
+    deeper,
+    shallower,
+    edges,
+    powers,
+    table,
+    shifts,
+    columns,
+    migration,
+    spread,
+    gain_rows,
+    arrived,
 ):
+    strips = [(x, x + STRIP) for x in range(0, LX, STRIP)]
+    copies = [
+        pltpu.make_async_copy(column_gain, gain_rows, arrived.at[len(strips)]),
+        pltpu.make_async_copy(shift_source, shifts, arrived.at[len(strips) + 1]),
+    ]
+    for index, (begin, end) in enumerate(strips):
+        rows = pl.ds(begin * LY, (end - begin) * LY)
+        copies.append(
+            pltpu.make_async_copy(
+                migration_source.at[rows, :], migration.at[rows, :], arrived.at[index]
+            )
+        )
+    for copy in copies:
+        copy.start()
     gap = jnp.zeros((SEGMENT - KZ, migration.shape[1]), jnp.bfloat16)
     rows = []
     for j in range(PACKED):
-        pieces = [own[b, EDGE + j * KZ : EDGE + (j + 1) * KZ, :] for b in range(own.shape[0])]
+        cells = slice(EDGE + j * KZ, EDGE + (j + 1) * KZ)
+        pieces = [own[b ^ choice[3], cells, :] for b in range(own.shape[0])]
         rows += [jnp.concatenate(pieces, axis=1), gap]
     lane = lax.broadcasted_iota(jnp.int32, (8, LANES), 1)
     note = own[choice[1], :EDGE, :].astype(jnp.float32)
@@ -135,9 +188,13 @@
             deeper[row : row + 8, :] = pltpu.roll(kernel, 1, 1)
 
     right = jnp.concatenate(rows)
-    columns = jnp.transpose(column_gain[...])
-    for x in range(0, LX, STRIP):
-        migrate(right, migration, columns, gains[:1], store, x, x + STRIP)
+    copies[0].wait()
+    columns[...] = jnp.transpose(gain_rows[...])
+    copies[1].wait()
+    block_table(shifts, table, spread)
+    for copy, (begin, end) in zip(copies[2:], strips):
+        copy.wait()
+        migrate(right, migration, columns, gains[:1], store, begin, end)
     for g in range(GROUPS):
         base = g // BY * KX * KROWS + g % BY * 16 + 8
         power = None
@@ -151,26 +208,26 @@
 
 def track(
     choice,
-    shift_table,
     kept,
     received,
-    migration,
-    column_gain,
     kernels,
     deeper,
     shallower,
     edges,
     kernel_powers,
+    table,
     shift_cells,
+    columns,
+    migration,
     scores,
     displacement,
     volume,
     sums,
     turned,
-    shift,
+    block,
     arrived,
 ):
-    positions = pltpu.make_async_copy(shift_table, shift, arrived)
+    positions = pltpu.make_async_copy(table, block, arrived)
     positions.start()
     keep = choice[0] == 1
     zero = jnp.zeros((NY, LANES), jnp.float32)
@@ -184,10 +241,10 @@
         base = (x + MARGIN) * NY + MARGIN
         volume[base : base + LY, :] = image
 
-    pieces = [jnp.where(keep, kept[b], received[b]) for b in range(kept.shape[0])]
+    places = [b ^ choice[4] for b in range(kept.shape[0])]
+    pieces = [jnp.where(keep, kept[place], received[place]) for place in places]
     spare = jnp.zeros((LANES - WINDOW, migration.shape[1]), jnp.bfloat16)
     right = jnp.concatenate([jnp.concatenate(pieces, axis=1), spare])
-    columns = jnp.transpose(column_gain[...])
     gains = depth_row(choice, kept)[:1]
 
     def strip(begin, end):
@@ -199,13 +256,9 @@
 
     def group(bx, by):
         g = bx * BY + by
-        starts = []
-        turns = []
-        for j in range(PACKED):
-            first = bx * KX + MARGIN + shift[0, 0, bx, j, by]
-            second = by * KY + MARGIN + shift[1, 0, bx, j, by]
-            starts.append(first * NY + second)
-            turns.append((j * KZ - EDGE + LANES - shift[2, 0, bx, j, by]) & (LANES - 1))
+        number = [(bx * PACKED + j) * BY + by for j in range(PACKED)]
+        starts = [block[0, n] for n in number]
+        turns = [block[1, n] for n in number]
 
         def gather(offsets, stride=None):
             value = None
@@ -356,13 +409,14 @@
     frame = lax.axis_index("frame")
     slab = lax.axis_index("slab")
     own_data = element_data.reshape(elements_here, depth)
+    scalars = pl.BlockSpec(memory_space=pltpu.SMEM)
 
     if elements_here == LANES:
         windows = pl.pallas_call(
             window_rows,
-            in_specs=[pl.BlockSpec(memory_space=pltpu.HBM)] * 2,
+            in_specs=[scalars] + [pl.BlockSpec(memory_space=pltpu.HBM)] * 2,
             out_specs=on_chip(1)[0],
-            out_shape=jax.ShapeDtypeStruct((slabs, WINDOW, LANES), jnp.bfloat16),
+            out_shape=jax.ShapeDtypeStruct((2, slabs // 2, WINDOW, LANES), jnp.bfloat16),
             scratch_shapes=[
                 pltpu.VMEM((depth // LANES, LANES, LANES), jnp.bfloat16),
                 pltpu.VMEM((1, STEP), jnp.float32),
@@ -371,9 +425,23 @@
             ],
             compiler_params=pltpu.CompilerParams(vmem_limit_bytes=4 << 20),
             name="window_rows",
-        )(in_hbm(own_data), in_hbm(depth_gain.reshape(1, STEP)))
-        own = lax.all_to_all(windows, "slab", split_axis=0, concat_axis=0, tiled=True)
-        places = [(slab - 1) % slabs, slab, (slab + 1) % slabs]
+        )(slab.reshape(1), in_hbm(own_data), in_hbm(depth_gain.reshape(1, STEP)))
+        swap = lambda array, bits: lax.ppermute(
+            array, "slab", [(i, i ^ bits) for i in range(slabs)]
+        )
+        halves = (windows[0], swap(windows[1], 1))
+        own = []
+        for bits in range(slabs // 2):
+            pair = jnp.stack(
+                [
+                    lax.dynamic_index_in_dim(half, slab // 2 ^ bits, 0, keepdims=False)
+                    for half in halves
+                ]
+            )
+            own.append(swap(pair, 2 * bits) if bits else pair)
+        own = jnp.concatenate(own)
+        order = slab
+        places = [(slab + step & slabs - 1) ^ slab for step in (-1, 0, 1)]
     else:
         turned = jnp.pad(own_data.T, ((EDGE, EDGE), (0, 0)))
         windows = jnp.stack([turned[i * STEP : i * STEP + WINDOW] for i in range(slabs)])
@@ -387,21 +455,34 @@
             middle = high(value - high(value))
             note = jnp.stack([high(value), middle, value - high(value) - middle])
             own = own.at[place, :3, :STEP].set(note.astype(jnp.bfloat16))
+        order = 0
         places = [0, 1, 2]
 
-    places = [jnp.asarray(place, jnp.int32) for place in places]
+    places = [jnp.asarray(place, jnp.int32) for place in places + [order]]
     gain_table = column_gain.reshape(-1, LANES)
-    scalars = pl.BlockSpec(memory_space=pltpu.SMEM)
+    turn = (0, 1, 2, 4, 3)
+    shifts = coarse_shift.transpose(turn)
     own_shapes = [(SPREAD, LANES), (LX * LY, LANES), (LX * LY, LANES)]
     own_shapes += [(2, GROUPS * 8, LANES), (GROUPS * SUMS, LANES)]
     kernel_arrays = pl.pallas_call(
         own_kernels,
-        in_specs=[scalars] + on_chip(3),
-        out_specs=on_chip(5),
-        out_shape=[pltpu.VMEM(shape, jnp.float32) for shape in own_shapes],
+        in_specs=[scalars] + on_chip(1) + [pl.BlockSpec(memory_space=pltpu.HBM)] * 3,
+        out_specs=on_chip(9),
+        out_shape=[pltpu.VMEM(shape, jnp.float32) for shape in own_shapes]
+        + [
+            pltpu.VMEM((8, LANES), jnp.int32),
+            pltpu.VMEM(shifts.shape, jnp.int32),
+            pltpu.VMEM((LANES, LX * LY // LANES), jnp.float32),
+            pltpu.VMEM(migration.shape, jnp.bfloat16),
+        ],
+        scratch_shapes=[
+            pltpu.VMEM((2 * BX * PACKED, LANES), jnp.float32),
+            pltpu.VMEM((LX * LY // LANES, LANES), jnp.float32),
+            pltpu.SemaphoreType.DMA((LX // STRIP + 2,)),
+        ],
         compiler_params=pltpu.CompilerParams(vmem_limit_bytes=16 << 20),
         name="own_kernels",
-    )(jnp.stack(places), pinned(own), pinned(migration), gain_table)
+    )(jnp.stack(places), pinned(own), in_hbm(migration), in_hbm(gain_table), in_hbm(shifts))
 
     kept = own
     received = own
@@ -415,32 +496,26 @@
     keep = ((chosen ^ frame) & (frames // 2) == 0).astype(jnp.int32)
     choice = jnp.stack([keep] + places)
 
-    turn = (0, 1, 2, 4, 3)
-    shifts = coarse_shift.transpose(turn)
     shapes = [jax.ShapeDtypeStruct((n,) + shifts.shape[1:], jnp.float32) for n in (7, 3)]
     scores, displacement = pl.pallas_call(
         track,
-        in_specs=[scalars, pl.BlockSpec(memory_space=pltpu.HBM)] + on_chip(10),
+        in_specs=[scalars] + on_chip(11),
         out_specs=on_chip(2),
         out_shape=shapes,
         scratch_shapes=[
             pltpu.VMEM((VOLUME, LANES), jnp.float32),
             pltpu.VMEM((12, GROUPS * SUMS, LANES), jnp.float32),
             pltpu.VMEM((LANES + 16, LANES), jnp.float32),
-            pltpu.SMEM(shifts.shape, jnp.int32),
+            pltpu.SMEM((8, LANES), jnp.int32),
             pltpu.SemaphoreType.DMA,
         ],
         compiler_params=pltpu.CompilerParams(vmem_limit_bytes=24 << 20),
         name="track",
     )(
         choice,
-        in_hbm(shifts),
         pinned(kept),
         pinned(received),
-        pinned(migration),
-        gain_table,
         *[pinned(array) for array in kernel_arrays],
-        shifts,
     )
     return scores.transpose(turn), displacement.transpose(turn)
 

time: 30.9 us -> 31.3 us (1.013)
  blocking collectives: 15 us -> 0 us
  waiting for transfers between devices: 1.15 us -> 9.41 us
  starting transfers between devices: 1.59 us -> 9.25 us
  local copies, waits for them, and re-layouts: 2.9 us -> 0.15 us
  Pallas kernels: 8.26 us -> 10.8 us
    all_to_all x1 -> x0, blocking collectives: 15 us -> none  [per_device(): lax.all_to_all(windows, 'slab', split_axis=0, concat_axis=0, tiled=True)]
    ppermute x0 -> x4, waiting for transfers between devices: none -> 8.64 us  [per_device(): lax.ppermute(array, 'slab', [(i, i ^ bits) for i in range(slabs)])]
    ppermute x0 -> x4, starting transfers between devices: none -> 7.6 us  [per_device(): lax.ppermute(array, 'slab', [(i, i ^ bits) for i in range(slabs)])]
    unnamed x8 -> x3, local copies, waits for them, and re-layouts: 2.9 us -> 0.02 us
    pallas_call x3, Pallas kernels: 8.26 us -> 10.8 us  [the longest x1 5.63 us: per_device(): pl.pallas_call(own_kernels, in_specs=[scalars] + on_chip(1) + [pl.BlockSp...]
    ppermute x2, waiting for transfers between devices: 1.15 us -> 0.78 us  [per_device(): lax.ppermute(kept, 'frame', [(i, i ^ bit) for i in range(frames)])]
  transfers between devices with their start and end apart: 2 -> 6, of which waited for: 2 -> 4; matrix products, arithmetic and copies ran while one was open for 0% -> 1% of each run, Pallas kernels for 7% -> 18%
where the time goes in v5:
time: 31.3 us; the launch traced here: 31.1 us
  Pallas kernels  10.8 us (35%)
  waiting for transfers between devices  9.41 us (30%)
  starting transfers between devices  9.25 us (30%)
  between operations  1.36 us (4%)
    ppermute x4, waiting for transfers between devices, per_device(): lax.ppermute(array, 'slab', [(i, i ^ bits) for i in range(slabs)])  8.64 us
    ppermute x4, starting transfers between devices, per_device(): lax.ppermute(array, 'slab', [(i, i ^ bits) for i in range(slabs)])  7.6 us
    pallas_call x1, Pallas kernels, per_device(): pl.pallas_call(own_kernels, in_specs=[scalars] + on_chip(1) + [pl.BlockSp...  5.63 us
    pallas_call x1, Pallas kernels, per_device(): pl.pallas_call(track, in_specs=[scalars] + on_chip(11), out_specs=on_chip...  4.06 us
    ppermute x2, starting transfers between devices, per_device(): lax.ppermute(kept, 'frame', [(i, i ^ bit) for i in range(frames)])  1.66 us
    pallas_call x1, Pallas kernels, per_device(): pl.pallas_call(window_rows, in_specs=[scalars] + [pl.BlockSpec(memory_spa...  1.11 us
    ppermute x2, waiting for transfers between devices, per_device(): lax.ppermute(kept, 'frame', [(i, i ^ bit) for i in range(frames)])  0.78 us
  transfers between devices with their start and end apart: 6, of which 4 were waited for; matrix products, arithmetic and copies ran while one was open for 1% of the time, Pallas kernels for 18%

profile of v5, /device:TPU:0, one launch (start us, length us, event | category | flops | bytes accessed | tf_op | source)
XLA Modules:
  0.0 31.1 jit_solution(3480207188181404908)
XLA Ops:
  0.6 1.1 %window_rows.1 = bf16[2,4,96,128]{3,2,1,0:T(8,128)(2,1)S(1)} custom-call(s32[1]{0:T(128)} %bitcast.5.slab_number, bf16[128,512]{1,0:T(8,128)(2,1)} %bitcast.23, f32[1,64]{1,0:T(1,128)} %bitcast.26), custom_call_target="tpu_custom_call" | custom-call | tf_op jit(solution)/shard_map/window_rows/pallas_call | solution.py:415
  1.8 3.0 %collective-permute-start = (bf16[4,96,128]{2,1,0:T(8,128)(2,1)S(1)}, bf16[4,96,128]{2,1,0:T(8,128)(2,1)S(1)}, u32[]{:S(2)}, u32[]{:S(2)}) collective-permute-start(bf16[4,96,128]{2,1,0:T(8,128)(2,1)S(1)} %get-tuple-element.24), channel_id=1, source_target_pairs={{0,1},{1,0},{2,3},{3,2},{4,5},{5,4},{6,7},{7,6},{8,9},{9,8},{10,11... | collective-permute-start | bytes 294920 | tf_op jit(solution)/shard_map/ppermute | solution.py:429
  4.8 2.8 %collective-permute-done = bf16[4,96,128]{2,1,0:T(8,128)(2,1)S(1)} collective-permute-done((bf16[4,96,128]{2,1,0:T(8,128)(2,1)S(1)}, bf16[4,96,128]{2,1,0:T(8,128)(2,1)S(1)}, u32[]{:S(2)}, u32[]{:S(2)}) %collective-permute-start) | collective-permute-done | bytes 98336 | tf_op jit(solution)/shard_map/ppermute | solution.py:429
  7.6 2.0 %collective-permute-start.1 = (bf16[2,96,128]{2,1,0:T(8,128)(2,1)S(1)}, bf16[2,96,128]{2,1,0:T(8,128)(2,1)S(1)}, u32[]{:S(2)}, u32[]{:S(2)}) collective-permute-start(bf16[2,96,128]{2,1,0:T(8,128)(2,1)S(1)} %pad_maximum_fusion), channel_id=1, source_target_pairs={{0,2},{1,3},{2,0},{3,1},{4,6},{5,7},{6,4},{7,5},{8,10},{9,11},{10,... | collective-permute-start | bytes 147464 | tf_op jit(solution)/shard_map/ppermute | solution.py:429
  9.6 2.6 %collective-permute-start.2 = (bf16[2,96,128]{2,1,0:T(8,128)(2,1)S(1)}, bf16[2,96,128]{2,1,0:T(8,128)(2,1)S(1)}, u32[]{:S(2)}, u32[]{:S(2)}) collective-permute-start(bf16[2,96,128]{2,1,0:T(8,128)(2,1)S(1)} %pad_maximum_fusion.1), channel_id=1, source_target_pairs={{0,4},{1,5},{2,6},{3,7},{4,0},{5,1},{6,2},{7,3},{8,12},{9,13},{10,... | collective-permute-start | bytes 147464 | tf_op jit(solution)/shard_map/ppermute | solution.py:429
  12.2 0.0 collective-permute-start.3
  12.2 0.0 collective-permute-done.1
  12.2 3.4 %collective-permute-done.2 = bf16[2,96,128]{2,1,0:T(8,128)(2,1)S(1)} collective-permute-done((bf16[2,96,128]{2,1,0:T(8,128)(2,1)S(1)}, bf16[2,96,128]{2,1,0:T(8,128)(2,1)S(1)}, u32[]{:S(2)}, u32[]{:S(2)}) %collective-permute-start.2) | collective-permute-done | bytes 49184 | tf_op jit(solution)/shard_map/ppermute | solution.py:429
  15.7 2.4 %collective-permute-done.3 = bf16[2,96,128]{2,1,0:T(8,128)(2,1)S(1)} collective-permute-done((bf16[2,96,128]{2,1,0:T(8,128)(2,1)S(1)}, bf16[2,96,128]{2,1,0:T(8,128)(2,1)S(1)}, u32[]{:S(2)}, u32[]{:S(2)}) %collective-permute-start.3) | collective-permute-done | bytes 49184 | tf_op jit(solution)/shard_map/ppermute | solution.py:429
  18.1 0.1 collective-permute-start.4
  18.8 0.8 %collective-permute-done.4 = bf16[8,96,128]{2,1,0:T(8,128)(2,1)S(1)} collective-permute-done((bf16[8,96,128]{2,1,0:T(8,128)(2,1)S(1)}, bf16[8,96,128]{2,1,0:T(8,128)(2,1)S(1)}, u32[]{:S(2)}, u32[]{:S(2)}) %collective-permute-start.4) | collective-permute-done | bytes 196640 | tf_op jit(solution)/shard_map/ppermute | solution.py:494
  19.6 1.6 %collective-permute-start.5 = (bf16[8,96,128]{2,1,0:T(8,128)(2,1)S(1)}, bf16[8,96,128]{2,1,0:T(8,128)(2,1)S(1)}, u32[]{:S(2)}, u32[]{:S(2)}) collective-permute-start(bf16[8,96,128]{2,1,0:T(8,128)(2,1)S(1)} %broadcast_select_fusion.kept), channel_id=1, source_target_pairs={{0,16},{8,24},{16,0},{24,8},{1,17},{9,25},{17,1},{25,9},{2,18},{10... | collective-permute-start | bytes 589832 | tf_op jit(solution)/shard_map/ppermute | solution.py:494
  21.2 0.1 stack.51.choice
  21.3 0.1 pad_add_fusion.choice
  21.4 5.6 %own_kernels.1 = (f32[4647,128]{1,0:T(8,128)S(1)}, f32[2048,128]{1,0:T(8,128)S(1)}, f32[2048,128]{1,0:T(8,128)S(1)}, f32[2,256,128]{2,1,0:T(8,128)S(1)}, f32[288...) custom-call(s32[4]{0:T(128)S(1)} %pad_add_fusion.choice, ...), custom_call_target="tpu_custom_call" | custom-call | tf_op jit(solution)/shard_map/own_kernels/pallas_call | solution.py:467
  27.0 0.0 collective-permute-done.5.received
  27.0 4.1 %track.1 = (f32[7,1,4,4,8]{4,3,2,1,0:T(4,128)}, f32[3,1,4,4,8]{4,3,2,1,0:T(4,128)}) custom-call(s32[5]{0:T(128)S(1)} %stack.51.choice, bf16[8,96,128]{2,1,0:T(8,128)(2,1)S(1)} %broadcast_select_fusion.kept, bf16[8,96,128]{2,1,0:T(8,128)(2,1)S(1)} %collective-permute-done.5.received, f32[4647,128]{1,0:T(8,128)S(1)} %get-tuple-element.13.kernels, ...), custom_call_target="tpu_custom_call" | custom-call | tf_op jit(solution)/shard_map/track/pallas_call | solution.py:500
  (11 shorter events, 0.1 us)
Async XLA Ops:
  1.8 5.8 %collective-permute-start = (bf16[4,96,128]{2,1,0:T(8,128)(2,1)S(1)}, bf16[4,96,128]{2,1,0:T(8,128)(2,1)S(1)}, u32[]{:S(2)}, u32[]{:S(2)}) collective-permute-start(bf16[4,96,128]{2,1,0:T(8,128)(2,1)S(1)} %get-tuple-element.24), channel_id=1, source_target_pairs={{0,1},{1,0},{2,3},{3,2},{4,5},{5,4},{6,7},{7,6},{8,9},{9,8},{10,11... | collective-permute-start | bytes 294920 | tf_op jit(solution)/shard_map/ppermute | solution.py:429
  7.6 4.6 %collective-permute-start.1 = (bf16[2,96,128]{2,1,0:T(8,128)(2,1)S(1)}, bf16[2,96,128]{2,1,0:T(8,128)(2,1)S(1)}, u32[]{:S(2)}, u32[]{:S(2)}) collective-permute-start(bf16[2,96,128]{2,1,0:T(8,128)(2,1)S(1)} %pad_maximum_fusion), channel_id=1, source_target_pairs={{0,2},{1,3},{2,0},{3,1},{4,6},{5,7},{6,4},{7,5},{8,10},{9,11},{10,... | collective-permute-start | bytes 147464 | tf_op jit(solution)/shard_map/ppermute | solution.py:429
  9.6 6.0 %collective-permute-start.2 = (bf16[2,96,128]{2,1,0:T(8,128)(2,1)S(1)}, bf16[2,96,128]{2,1,0:T(8,128)(2,1)S(1)}, u32[]{:S(2)}, u32[]{:S(2)}) collective-permute-start(bf16[2,96,128]{2,1,0:T(8,128)(2,1)S(1)} %pad_maximum_fusion.1), channel_id=1, source_target_pairs={{0,4},{1,5},{2,6},{3,7},{4,0},{5,1},{6,2},{7,3},{8,12},{9,13},{10,... | collective-permute-start | bytes 147464 | tf_op jit(solution)/shard_map/ppermute | solution.py:429
  12.2 5.9 %collective-permute-start.3 = (bf16[2,96,128]{2,1,0:T(8,128)(2,1)S(1)}, bf16[2,96,128]{2,1,0:T(8,128)(2,1)S(1)}, u32[]{:S(2)}, u32[]{:S(2)}) collective-permute-start(bf16[2,96,128]{2,1,0:T(8,128)(2,1)S(1)} %pad_maximum_fusion.2), channel_id=1, source_target_pairs={{0,6},{1,7},{2,4},{3,5},{4,2},{5,3},{6,0},{7,1},{8,14},{9,15},{10,... | collective-permute-start | bytes 147464 | tf_op jit(solution)/shard_map/ppermute | solution.py:429
  18.1 1.5 %collective-permute-start.4 = (bf16[8,96,128]{2,1,0:T(8,128)(2,1)S(1)}, bf16[8,96,128]{2,1,0:T(8,128)(2,1)S(1)}, u32[]{:S(2)}, u32[]{:S(2)}) collective-permute-start(bf16[8,96,128]{2,1,0:T(8,128)(2,1)S(1)} %constant_dynamic-update-slice_fusion.own), channel_id=1, source_target_pairs={{0,8},{8,0},{16,24},{24,16},{1,9},{9,1},{17,25},{25,17},{2,10},{10... | collective-permute-start | bytes 589832 | tf_op jit(solution)/shard_map/ppermute | solution.py:494
  19.6 7.4 %collective-permute-start.5 = (bf16[8,96,128]{2,1,0:T(8,128)(2,1)S(1)}, bf16[8,96,128]{2,1,0:T(8,128)(2,1)S(1)}, u32[]{:S(2)}, u32[]{:S(2)}) collective-permute-start(bf16[8,96,128]{2,1,0:T(8,128)(2,1)S(1)} %broadcast_select_fusion.kept), channel_id=1, source_target_pairs={{0,16},{8,24},{16,0},{24,8},{1,17},{9,25},{17,1},{25,9},{2,18},{10... | collective-permute-start | bytes 589832 | tf_op jit(solution)/shard_map/ppermute | solution.py:494

commit v6 on v5

--- a/solution.py
+++ b/solution.py
@@ -34,7 +34,7 @@
 SUMS = 9
 CELLS = KX * KY * KZ
 STRIP = 4
-LATE = False
+LOAD = 16
 
 
 def pieces_of(value):
@@ -43,8 +43,7 @@
     return high, middle, value - high - middle
 
 
-def window_rows(slab_number, element_data, depth_gain, windows, held, gain, row, arrived):
-    odd = slab_number[0] & 1
+def window_rows(element_data, depth_gain, windows, held, gain, row, arrived):
     columns = element_data.shape[1] // LANES
     copies = [pltpu.make_async_copy(depth_gain, gain, arrived.at[columns])]
     for column in range(columns):
@@ -57,7 +56,7 @@
     for index, piece in enumerate(pieces_of(gain[...])):
         row[index : index + 1, :STEP] = piece
     note = row[...].astype(jnp.bfloat16)
-    slabs = windows.shape[0] * windows.shape[1]
+    slabs = windows.shape[0]
     empty = jnp.zeros((EDGE, LANES), jnp.bfloat16)
     spare = lax.broadcasted_iota(jnp.int32, (EDGE, LANES), 0) < 3
 
@@ -65,7 +64,7 @@
         if 0 <= slab < slabs:
             if first == 0:
                 rows = jnp.where(spare, note, rows)
-            windows[odd ^ (slab & 1), slab // 2, first : first + EDGE, :] = rows
+            windows[slab, first : first + EDGE, :] = rows
 
     put(0, 0, empty)
     put(slabs - 1, EDGE + STEP, empty)
@@ -104,7 +103,8 @@
     for x in range(begin, end):
         row = x * LY
         gain = columns[row % LANES : row % LANES + LY, row // LANES : row // LANES + 1]
-        image = raw[(x - begin) * LY : (x - begin + 1) * LY] * jnp.broadcast_to(gain, (LY, LANES))
+        image = raw[(x - begin) * LY : (x - begin + 1) * LY]
+        image = image * jnp.broadcast_to(gain, image.shape)
         store(x, (image * gains).astype(jnp.bfloat16).astype(jnp.float32))
 
 
@@ -148,7 +148,7 @@
     gain_rows,
     arrived,
 ):
-    strips = [(x, x + STRIP) for x in range(0, LX, STRIP)]
+    strips = [(x, x + LOAD) for x in range(0, LX, LOAD)]
     copies = [
         pltpu.make_async_copy(column_gain, gain_rows, arrived.at[len(strips)]),
         pltpu.make_async_copy(shift_source, shifts, arrived.at[len(strips) + 1]),
@@ -166,7 +166,7 @@
     rows = []
     for j in range(PACKED):
         cells = slice(EDGE + j * KZ, EDGE + (j + 1) * KZ)
-        pieces = [own[b ^ choice[3], cells, :] for b in range(own.shape[0])]
+        pieces = [own[b, cells, :] for b in range(own.shape[0])]
         rows += [jnp.concatenate(pieces, axis=1), gap]
     lane = lax.broadcasted_iota(jnp.int32, (8, LANES), 1)
     note = own[choice[1], :EDGE, :].astype(jnp.float32)
@@ -241,17 +241,13 @@
         base = (x + MARGIN) * NY + MARGIN
         volume[base : base + LY, :] = image
 
-    places = [b ^ choice[4] for b in range(kept.shape[0])]
-    pieces = [jnp.where(keep, kept[place], received[place]) for place in places]
+    pieces = [jnp.where(keep, kept[b], received[b]) for b in range(kept.shape[0])]
     spare = jnp.zeros((LANES - WINDOW, migration.shape[1]), jnp.bfloat16)
     right = jnp.concatenate([jnp.concatenate(pieces, axis=1), spare])
     gains = depth_row(choice, kept)[:1]
 
-    def strip(begin, end):
-        migrate(right, migration, columns, gains, store, begin, end)
-
-    place = lax.broadcasted_iota(jnp.int32, (16, LANES), 1)
-    segment = [((place + 8) & (LANES - 1)) // SEGMENT == j for j in range(PACKED)]
+    lane = lax.broadcasted_iota(jnp.int32, (16, LANES), 1)
+    segment = [((lane + 8) & (LANES - 1)) // SEGMENT == j for j in range(PACKED)]
     row_number = lax.broadcasted_iota(jnp.int32, (8, LANES), 0)
 
     def group(bx, by):
@@ -314,13 +310,10 @@
         for index, value in enumerate(held):
             sums[index, pl.ds(g * SUMS, 8), :] = value
 
-    strips = [(x, min(x + STRIP, LX)) for x in range(0, LX, STRIP)]
+    for x in range(0, LX, STRIP):
+        migrate(right, migration, columns, gains, store, x, x + STRIP)
+    positions.wait()
     for bx in range(BX):
-        reach = min(KX * bx + KX + CMAX, LX - 1) if LATE else LX - 1
-        while strips and strips[0][0] <= reach:
-            strip(*strips.pop(0))
-        if bx == 0:
-            positions.wait()
         for by in range(BY):
             group(bx, by)
 
@@ -414,9 +407,9 @@
     if elements_here == LANES:
         windows = pl.pallas_call(
             window_rows,
-            in_specs=[scalars] + [pl.BlockSpec(memory_space=pltpu.HBM)] * 2,
+            in_specs=[pl.BlockSpec(memory_space=pltpu.HBM)] * 2,
             out_specs=on_chip(1)[0],
-            out_shape=jax.ShapeDtypeStruct((2, slabs // 2, WINDOW, LANES), jnp.bfloat16),
+            out_shape=jax.ShapeDtypeStruct((slabs, WINDOW, LANES), jnp.bfloat16),
             scratch_shapes=[
                 pltpu.VMEM((depth // LANES, LANES, LANES), jnp.bfloat16),
                 pltpu.VMEM((1, STEP), jnp.float32),
@@ -425,23 +418,9 @@
             ],
             compiler_params=pltpu.CompilerParams(vmem_limit_bytes=4 << 20),
             name="window_rows",
-        )(slab.reshape(1), in_hbm(own_data), in_hbm(depth_gain.reshape(1, STEP)))
-        swap = lambda array, bits: lax.ppermute(
-            array, "slab", [(i, i ^ bits) for i in range(slabs)]
-        )
-        halves = (windows[0], swap(windows[1], 1))
-        own = []
-        for bits in range(slabs // 2):
-            pair = jnp.stack(
-                [
-                    lax.dynamic_index_in_dim(half, slab // 2 ^ bits, 0, keepdims=False)
-                    for half in halves
-                ]
-            )
-            own.append(swap(pair, 2 * bits) if bits else pair)
-        own = jnp.concatenate(own)
-        order = slab
-        places = [(slab + step & slabs - 1) ^ slab for step in (-1, 0, 1)]
+        )(in_hbm(own_data), in_hbm(depth_gain.reshape(1, STEP)))
+        own = lax.all_to_all(windows, "slab", split_axis=0, concat_axis=0, tiled=True)
+        places = [slab + step & slabs - 1 for step in (-1, 0, 1)]
     else:
         turned = jnp.pad(own_data.T, ((EDGE, EDGE), (0, 0)))
         windows = jnp.stack([turned[i * STEP : i * STEP + WINDOW] for i in range(slabs)])
@@ -455,10 +434,9 @@
             middle = high(value - high(value))
             note = jnp.stack([high(value), middle, value - high(value) - middle])
             own = own.at[place, :3, :STEP].set(note.astype(jnp.bfloat16))
-        order = 0
         places = [0, 1, 2]
 
-    places = [jnp.asarray(place, jnp.int32) for place in places + [order]]
+    places = [jnp.asarray(place, jnp.int32) for place in places]
     gain_table = column_gain.reshape(-1, LANES)
     turn = (0, 1, 2, 4, 3)
     shifts = coarse_shift.transpose(turn)
@@ -478,7 +456,7 @@
         scratch_shapes=[
             pltpu.VMEM((2 * BX * PACKED, LANES), jnp.float32),
             pltpu.VMEM((LX * LY // LANES, LANES), jnp.float32),
-            pltpu.SemaphoreType.DMA((LX // STRIP + 2,)),
+            pltpu.SemaphoreType.DMA((LX // LOAD + 2,)),
         ],
         compiler_params=pltpu.CompilerParams(vmem_limit_bytes=16 << 20),
         name="own_kernels",

time: 31.3 us -> 29.5 us (0.942)
  blocking collectives: 0 us -> 15 us
  waiting for transfers between devices: 9.41 us -> 1.22 us
  starting transfers between devices: 9.25 us -> 1.59 us
  Pallas kernels: 10.8 us -> 9.97 us
    all_to_all x0 -> x1, blocking collectives: none -> 15 us  [per_device(): lax.all_to_all(windows, 'slab', split_axis=0, concat_axis=0, tiled=True)]
    ppermute x4 -> x0, waiting for transfers between devices: 8.64 us -> none  [per_device(): lax.ppermute(array, 'slab', [(i, i ^ bits) for i in range(slabs)])]
    ppermute x4 -> x0, starting transfers between devices: 7.6 us -> none  [per_device(): lax.ppermute(array, 'slab', [(i, i ^ bits) for i in range(slabs)])]
    pallas_call x1, Pallas kernels: 5.63 us -> 4.82 us  [per_device(): pl.pallas_call(own_kernels, in_specs=[scalars] + on_chip(1) + [pl.BlockSp...]
    ppermute x2, waiting for transfers between devices: 0.78 us -> 1.22 us  [per_device(): lax.ppermute(kept, 'frame', [(i, i ^ bit) for i in range(frames)])]
  transfers between devices with their start and end apart: 6 -> 2, of which waited for: 4 -> 2; matrix products, arithmetic and copies ran while one was open for 1% -> 1% of each run, Pallas kernels for 18% -> 16%
where the time goes in v6:
time: 29.5 us; the launch traced here: 29.3 us
  blocking collectives  15 us (51%)
  Pallas kernels  9.97 us (34%)
  starting transfers between devices  1.59 us (5%)
  between operations  1.31 us (4%)
  waiting for transfers between devices  1.22 us (4%)
    all_to_all x1, blocking collectives, per_device(): lax.all_to_all(windows, 'slab', split_axis=0, concat_axis=0, tiled=True)  15 us
    pallas_call x1, Pallas kernels, per_device(): pl.pallas_call(own_kernels, in_specs=[scalars] + on_chip(1) + [pl.BlockSp...  4.82 us
    pallas_call x1, Pallas kernels, per_device(): pl.pallas_call(track, in_specs=[scalars] + on_chip(11), out_specs=on_chip...  4.05 us
    ppermute x2, starting transfers between devices, per_device(): lax.ppermute(kept, 'frame', [(i, i ^ bit) for i in range(frames)])  1.59 us
    ppermute x2, waiting for transfers between devices, per_device(): lax.ppermute(kept, 'frame', [(i, i ^ bit) for i in range(frames)])  1.22 us
    pallas_call x1, Pallas kernels, per_device(): pl.pallas_call(window_rows, in_specs=[pl.BlockSpec(memory_space=pltpu.HBM...  1.11 us
  transfers between devices with their start and end apart: 2, of which 2 were waited for; matrix products, arithmetic and copies ran while one was open for 1% of the time, Pallas kernels for 16%

profile of v6, /device:TPU:0, one launch (start us, length us, event | category | flops | bytes accessed | tf_op | source)
XLA Modules:
  0.0 29.3 jit_solution(17010499672539291026)
XLA Ops:
  0.6 1.1 %window_rows.1 = bf16[8,96,128]{2,1,0:T(8,128)(2,1)S(1)} custom-call(bf16[128,512]{1,0:T(8,128)(2,1)} %bitcast.12, f32[1,64]{1,0:T(1,128)} %bitcast.15), custom_call_target="tpu_custom_call" | custom-call | tf_op jit(solution)/shard_map/window_rows/pallas_call | solution.py:408
  1.7 15.0 %all_to_all.5.own = bf16[8,96,128]{2,1,0:T(8,128)(2,1)S(1)} all-to-all(bf16[8,96,128]{2,1,0:T(8,128)(2,1)S(1)} %window_rows.1), channel_id=1, replica_groups=mesh['frame'=4,'slab'=8] {'slab'}, dimensions={0} | all-to-all | bytes 393216 | tf_op jit(solution)/shard_map/all_to_all | solution.py:422
  16.8 0.0 collective-permute-start
  17.4 0.8 %collective-permute-done = bf16[8,96,128]{2,1,0:T(8,128)(2,1)S(1)} collective-permute-done((bf16[8,96,128]{2,1,0:T(8,128)(2,1)S(1)}, bf16[8,96,128]{2,1,0:T(8,128)(2,1)S(1)}, u32[]{:S(2)}, u32[]{:S(2)}) %collective-permute-start) | collective-permute-done | bytes 196640 | tf_op jit(solution)/shard_map/ppermute | solution.py:472
  18.2 1.6 %collective-permute-start.1 = (bf16[8,96,128]{2,1,0:T(8,128)(2,1)S(1)}, bf16[8,96,128]{2,1,0:T(8,128)(2,1)S(1)}, u32[]{:S(2)}, u32[]{:S(2)}) collective-permute-start(bf16[8,96,128]{2,1,0:T(8,128)(2,1)S(1)} %broadcast_select_fusion.kept), channel_id=1, source_target_pairs={{0,16},{8,24},{16,0},{24,8},{1,17},{9,25},{17,1},{25,9},{2,18},{10... | collective-permute-start | bytes 589832 | tf_op jit(solution)/shard_map/ppermute | solution.py:472
  19.8 0.1 pad_add_fusion.1.choice
  19.9 0.1 pad_add_fusion.choice
  20.0 4.8 %own_kernels.1 = (f32[4647,128]{1,0:T(8,128)S(1)}, f32[2048,128]{1,0:T(8,128)S(1)}, f32[2048,128]{1,0:T(8,128)S(1)}, f32[2,256,128]{2,1,0:T(8,128)S(1)}, f32[288...) custom-call(s32[3]{0:T(128)S(1)} %pad_add_fusion.1.choice, ...), custom_call_target="tpu_custom_call" | custom-call | tf_op jit(solution)/shard_map/own_kernels/pallas_call | solution.py:445
  24.8 0.4 %collective-permute-done.1.received = bf16[8,96,128]{2,1,0:T(8,128)(2,1)S(1)} collective-permute-done((bf16[8,96,128]{2,1,0:T(8,128)(2,1)S(1)}, bf16[8,96,128]{2,1,0:T(8,128)(2,1)S(1)}, u32[]{:S(2)}, u32[]{:S(2)}) %collective-permute-start.1) | collective-permute-done | bytes 196640 | tf_op jit(solution)/shard_map/ppermute | solution.py:472
  25.3 4.0 %track.1 = (f32[7,1,4,4,8]{4,3,2,1,0:T(4,128)}, f32[3,1,4,4,8]{4,3,2,1,0:T(4,128)}) custom-call(s32[4]{0:T(128)S(1)} %pad_add_fusion.choice, bf16[8,96,128]{2,1,0:T(8,128)(2,1)S(1)} %broadcast_select_fusion.kept, bf16[8,96,128]{2,1,0:T(8,128)(2,1)S(1)} %collective-permute-done.1.received, f32[4647,128]{1,0:T(8,128)S(1)} %get-tuple-element.13.kernels, ...), custom_call_target="tpu_custom_call" | custom-call | tf_op jit(solution)/shard_map/track/pallas_call | solution.py:478
  (1 shorter events, 0.0 us)
Async XLA Ops:
  16.8 1.4 %collective-permute-start = (bf16[8,96,128]{2,1,0:T(8,128)(2,1)S(1)}, bf16[8,96,128]{2,1,0:T(8,128)(2,1)S(1)}, u32[]{:S(2)}, u32[]{:S(2)}) collective-permute-start(bf16[8,96,128]{2,1,0:T(8,128)(2,1)S(1)} %all_to_all.5.own), channel_id=1, source_target_pairs={{0,8},{8,0},{16,24},{24,16},{1,9},{9,1},{17,25},{25,17},{2,10},{10... | collective-permute-start | bytes 589832 | tf_op jit(solution)/shard_map/ppermute | solution.py:472
  18.2 7.0 %collective-permute-start.1 = (bf16[8,96,128]{2,1,0:T(8,128)(2,1)S(1)}, bf16[8,96,128]{2,1,0:T(8,128)(2,1)S(1)}, u32[]{:S(2)}, u32[]{:S(2)}) collective-permute-start(bf16[8,96,128]{2,1,0:T(8,128)(2,1)S(1)} %broadcast_select_fusion.kept), channel_id=1, source_target_pairs={{0,16},{8,24},{16,0},{24,8},{1,17},{9,25},{17,1},{25,9},{2,18},{10... | collective-permute-start | bytes 589832 | tf_op jit(solution)/shard_map/ppermute | solution.py:472

commit v7 on v6

--- a/solution.py
+++ b/solution.py
@@ -93,13 +93,16 @@
     return jnp.where(lane >= EDGE + STEP, pltpu.roll(of(3), EDGE + STEP, 1), row)
 
 
-def migrate(right, migration, columns, gains, store, begin, end):
-    raw = lax.dot_general(
-        migration[begin * LY : end * LY, :],
+def migrated(right, migration, begin, end, first=0):
+    return lax.dot_general(
+        migration[begin * LY : end * LY, first : first + right.shape[1]],
         right,
         (((1,), (1,)), ((), ())),
         preferred_element_type=jnp.float32,
     )
+
+
+def finish(raw, columns, gains, store, begin, end):
     for x in range(begin, end):
         row = x * LY
         gain = columns[row % LANES : row % LANES + LY, row // LANES : row // LANES + 1]
@@ -194,7 +197,8 @@
     block_table(shifts, table, spread)
     for copy, (begin, end) in zip(copies[2:], strips):
         copy.wait()
-        migrate(right, migration, columns, gains[:1], store, begin, end)
+        raw = migrated(right, migration, begin, end)
+        finish(raw, columns, gains[:1], store, begin, end)
     for g in range(GROUPS):
         base = g // BY * KX * KROWS + g % BY * 16 + 8
         power = None
@@ -206,10 +210,25 @@
             edges[index, g * 8 : g * 8 + 8, :] = kernels[pl.ds(row, 8, stride=KROWS), :]
 
 
+def reference_samples(choice, kept, received, first):
+    keep = choice[0] == 1
+    blocks = received.shape[0]
+    pieces = [jnp.where(keep, kept[first + b], received[b]) for b in range(blocks)]
+    spare = jnp.zeros((LANES - WINDOW, blocks * LANES), jnp.bfloat16)
+    return jnp.concatenate([jnp.concatenate(pieces, axis=1), spare])
+
+
+def reference_part(choice, kept, received, migration, partial):
+    right = reference_samples(choice, kept, received, 0)
+    for x in range(0, LX, STRIP):
+        partial[x * LY : (x + STRIP) * LY, :] = migrated(right, migration, x, x + STRIP)
+
+
 def track(
     choice,
     kept,
     received,
+    partial,
     kernels,
     deeper,
     shallower,
@@ -229,22 +248,25 @@
 ):
     positions = pltpu.make_async_copy(table, block, arrived)
     positions.start()
-    keep = choice[0] == 1
+
+    def store(x, image):
+        base = (x + MARGIN) * NY + MARGIN
+        volume[base : base + LY, :] = image
+
+    first = kept.shape[0] - received.shape[0]
+    right = reference_samples(choice, kept, received, first)
+    gains = depth_row(choice, kept)[:1]
+    for x in range(0, LX, STRIP):
+        raw = partial[x * LY : (x + STRIP) * LY, :]
+        raw = raw + migrated(right, migration, x, x + STRIP, first * LANES)
+        finish(raw, columns, gains, store, x, x + STRIP)
     zero = jnp.zeros((NY, LANES), jnp.float32)
     for x in list(range(MARGIN)) + list(range(LX + MARGIN, NX)):
         volume[x * NY : (x + 1) * NY, :] = zero
     for x in range(MARGIN, LX + MARGIN):
         volume[x * NY : x * NY + MARGIN, :] = zero[:MARGIN]
         volume[x * NY + MARGIN + LY : (x + 1) * NY, :] = zero[: NY - MARGIN - LY]
-
-    def store(x, image):
-        base = (x + MARGIN) * NY + MARGIN
-        volume[base : base + LY, :] = image
-
-    pieces = [jnp.where(keep, kept[b], received[b]) for b in range(kept.shape[0])]
-    spare = jnp.zeros((LANES - WINDOW, migration.shape[1]), jnp.bfloat16)
-    right = jnp.concatenate([jnp.concatenate(pieces, axis=1), spare])
-    gains = depth_row(choice, kept)[:1]
+    positions.wait()
 
     lane = lax.broadcasted_iota(jnp.int32, (16, LANES), 1)
     segment = [((lane + 8) & (LANES - 1)) // SEGMENT == j for j in range(PACKED)]
@@ -310,9 +332,6 @@
         for index, value in enumerate(held):
             sums[index, pl.ds(g * SUMS, 8), :] = value
 
-    for x in range(0, LX, STRIP):
-        migrate(right, migration, columns, gains, store, x, x + STRIP)
-    positions.wait()
     for bx in range(BX):
         for by in range(BY):
             group(bx, by)
@@ -463,21 +482,34 @@
     )(jnp.stack(places), pinned(own), in_hbm(migration), in_hbm(gain_table), in_hbm(shifts))
 
     kept = own
-    received = own
     bit = 1
-    while bit < frames:
-        if bit > 1:
-            mine = (chosen ^ frame) & (bit // 2) == 0
-            kept = jnp.where(mine, kept, received)
+    while bit < frames // 2:
         received = lax.ppermute(kept, "frame", [(i, i ^ bit) for i in range(frames)])
+        mine = (chosen ^ frame) & bit == 0
+        kept = jnp.where(mine, kept, received)
         bit *= 2
+    half = kept.shape[0] // 2
+    received = [
+        lax.ppermute(part, "frame", [(i, i ^ bit) for i in range(frames)])
+        for part in (kept[:half], kept[half:])
+    ]
     keep = ((chosen ^ frame) & (frames // 2) == 0).astype(jnp.int32)
     choice = jnp.stack([keep] + places)
+
+    *kernel_arrays, staged = kernel_arrays
+    partial = pl.pallas_call(
+        reference_part,
+        in_specs=[scalars] + on_chip(3),
+        out_specs=on_chip(1)[0],
+        out_shape=pltpu.VMEM((LX * LY, LANES), jnp.float32),
+        compiler_params=pltpu.CompilerParams(vmem_limit_bytes=8 << 20),
+        name="reference_part",
+    )(choice, pinned(kept), pinned(received[0]), pinned(staged))
 
     shapes = [jax.ShapeDtypeStruct((n,) + shifts.shape[1:], jnp.float32) for n in (7, 3)]
     scores, displacement = pl.pallas_call(
         track,
-        in_specs=[scalars] + on_chip(11),
+        in_specs=[scalars] + on_chip(12),
         out_specs=on_chip(2),
         out_shape=shapes,
         scratch_shapes=[
@@ -492,8 +524,8 @@
     )(
         choice,
         pinned(kept),
-        pinned(received),
-        *[pinned(array) for array in kernel_arrays],
+        pinned(received[1]),
+        *[pinned(array) for array in [partial, *kernel_arrays, staged]],
     )
     return scores.transpose(turn), displacement.transpose(turn)
 

time: 29.5 us -> 30.3 us (1.027)
  Pallas kernels: 9.97 us -> 10.7 us
  waiting for transfers between devices: 1.22 us -> 0.71 us
  starting transfers between devices: 1.59 us -> 2.09 us
    ppermute x0 -> x2, starting transfers between devices: none -> 2.09 us  [per_device(): lax.ppermute(part, 'frame', [(i, i ^ bit) for i in range(frames)])]
    ppermute x2 -> x1, starting transfers between devices: 1.59 us -> 0.01 us  [per_device(): lax.ppermute(kept, 'frame', [(i, i ^ bit) for i in range(frames)])]
    pallas_call x1 -> x2, Pallas kernels: 4.05 us -> 4.76 us  [the longest x1 3.51 us: per_device(): pl.pallas_call(track, in_specs=[scalars] + on_chip(12), out_specs=on_chip...]
    ppermute x2 -> x1, waiting for transfers between devices: 1.22 us -> 0.7 us  [per_device(): lax.ppermute(kept, 'frame', [(i, i ^ bit) for i in range(frames)])]
  transfers between devices with their start and end apart: 2 -> 3, of which waited for: 2 -> 1; matrix products, arithmetic and copies ran while one was open for 1% -> 1% of each run, Pallas kernels for 16% -> 20%
where the time goes in v7:
time: 30.3 us; the launch traced here: 30.1 us
  blocking collectives  15 us (50%)
  Pallas kernels  10.7 us (35%)
  starting transfers between devices  2.09 us (7%)
  between operations  1.34 us (4%)
  waiting for transfers between devices  0.71 us (2%)
    all_to_all x1, blocking collectives, per_device(): lax.all_to_all(windows, 'slab', split_axis=0, concat_axis=0, tiled=True)  15 us
    pallas_call x1, Pallas kernels, per_device(): pl.pallas_call(own_kernels, in_specs=[scalars] + on_chip(1) + [pl.BlockSp...  4.83 us
    pallas_call x1, Pallas kernels, per_device(): pl.pallas_call(track, in_specs=[scalars] + on_chip(12), out_specs=on_chip...  3.51 us
    ppermute x2, starting transfers between devices, per_device(): lax.ppermute(part, 'frame', [(i, i ^ bit) for i in range(frames)])  2.09 us
    pallas_call x1, Pallas kernels, per_device(): pl.pallas_call(reference_part, in_specs=[scalars] + on_chip(3), out_specs...  1.24 us
    pallas_call x1, Pallas kernels, per_device(): pl.pallas_call(window_rows, in_specs=[pl.BlockSpec(memory_space=pltpu.HBM...  1.11 us
    ppermute x1, waiting for transfers between devices, per_device(): lax.ppermute(kept, 'frame', [(i, i ^ bit) for i in range(frames)])  0.7 us
  transfers between devices with their start and end apart: 3, of which 1 were waited for; matrix products, arithmetic and copies ran while one was open for 1% of the time, Pallas kernels for 20%

profile of v7, /device:TPU:0, one launch (start us, length us, event | category | flops | bytes accessed | tf_op | source)
XLA Modules:
  0.0 30.1 jit_solution(10032448602153508331)
XLA Ops:
  0.6 1.1 %window_rows.1 = bf16[8,96,128]{2,1,0:T(8,128)(2,1)S(1)} custom-call(bf16[128,512]{1,0:T(8,128)(2,1)} %bitcast.12, f32[1,64]{1,0:T(1,128)} %bitcast.15), custom_call_target="tpu_custom_call" | custom-call | tf_op jit(solution)/shard_map/window_rows/pallas_call | solution.py:427
  1.7 15.0 %all_to_all.5.own = bf16[8,96,128]{2,1,0:T(8,128)(2,1)S(1)} all-to-all(bf16[8,96,128]{2,1,0:T(8,128)(2,1)S(1)} %window_rows.1), channel_id=1, replica_groups=mesh['frame'=4,'slab'=8] {'slab'}, dimensions={0} | all-to-all | bytes 393216 | tf_op jit(solution)/shard_map/all_to_all | solution.py:441
  16.8 0.0 collective-permute-start
  17.4 0.1 pad_add_fusion.1.choice
  17.5 0.7 %collective-permute-done = bf16[8,96,128]{2,1,0:T(8,128)(2,1)S(1)} collective-permute-done((bf16[8,96,128]{2,1,0:T(8,128)(2,1)S(1)}, bf16[8,96,128]{2,1,0:T(8,128)(2,1)S(1)}, u32[]{:S(2)}, u32[]{:S(2)}) %collective-permute-start) | collective-permute-done | bytes 196640 | tf_op jit(solution)/shard_map/ppermute | solution.py:487
  18.3 1.6 %collective-permute-start.2 = (bf16[4,96,128]{2,1,0:T(8,128)(2,1)S(1)}, bf16[4,96,128]{2,1,0:T(8,128)(2,1)S(1)}, u32[]{:S(2)}, u32[]{:S(2)}) collective-permute-start(bf16[4,96,128]{2,1,0:T(8,128)(2,1)S(1)} %get-tuple-element.24), channel_id=1, source_target_pairs={{0,16},{8,24},{16,0},{24,8},{1,17},{9,25},{17,1},{25,9},{2,18},{10... | collective-permute-start | bytes 294920 | tf_op jit(solution)/shard_map/ppermute | solution.py:493
  19.9 0.5 %collective-permute-start.1 = (bf16[4,96,128]{2,1,0:T(8,128)(2,1)S(1)}, bf16[4,96,128]{2,1,0:T(8,128)(2,1)S(1)}, u32[]{:S(2)}, u32[]{:S(2)}) collective-permute-start(bf16[4,96,128]{2,1,0:T(8,128)(2,1)S(1)} %get-tuple-element.25), channel_id=1, source_target_pairs={{0,16},{8,24},{16,0},{24,8},{1,17},{9,25},{17,1},{25,9},{2,18},{10... | collective-permute-start | bytes 294920 | tf_op jit(solution)/shard_map/ppermute | solution.py:493
  20.4 0.1 pad_add_fusion.choice
  20.4 4.8 %own_kernels.1 = (f32[4647,128]{1,0:T(8,128)S(1)}, f32[2048,128]{1,0:T(8,128)S(1)}, f32[2048,128]{1,0:T(8,128)S(1)}, f32[2,256,128]{2,1,0:T(8,128)S(1)}, f32[288...) custom-call(s32[3]{0:T(128)S(1)} %pad_add_fusion.1.choice, ...), custom_call_target="tpu_custom_call" | custom-call | tf_op jit(solution)/shard_map/own_kernels/pallas_call | solution.py:464
  25.3 0.0 collective-permute-done.2.received
  25.3 1.2 %reference_part.1.partial = f32[2048,128]{1,0:T(8,128)S(1)} custom-call(s32[4]{0:T(128)S(1)} %pad_add_fusion.choice, bf16[8,96,128]{2,1,0:T(8,128)(2,1)S(1)} %broadcast_select_fusion.kept, bf16[4,96,128]{2,1,0:T(8,128)(2,1)S(1)} %collective-permute-done.2.received, bf16[2048,1024]{1,0:T(8,128)(2,1)S(1)} %get-tuple-element.13.migration), custom_call_target="tpu_custom_call" | custom-call | tf_op jit(solution)/shard_map/reference_part/pallas_call | solution.py:500
  26.5 0.0 collective-permute-done.1.received
  26.5 3.5 %track.1 = (f32[7,1,4,4,8]{4,3,2,1,0:T(4,128)}, f32[3,1,4,4,8]{4,3,2,1,0:T(4,128)}) custom-call(s32[4]{0:T(128)S(1)} %pad_add_fusion.choice, bf16[8,96,128]{2,1,0:T(8,128)(2,1)S(1)} %broadcast_select_fusion.kept, bf16[4,96,128]{2,1,0:T(8,128)(2,1)S(1)} %collective-permute-done.1.received, f32[2048,128]{1,0:T(8,128)S(1)} %reference_part.1.partial, ...), custom_call_target="tpu_custom_call" | custom-call | tf_op jit(solution)/shard_map/track/pallas_call | solution.py:510
  (2 shorter events, 0.0 us)
Async XLA Ops:
  16.8 1.4 %collective-permute-start = (bf16[8,96,128]{2,1,0:T(8,128)(2,1)S(1)}, bf16[8,96,128]{2,1,0:T(8,128)(2,1)S(1)}, u32[]{:S(2)}, u32[]{:S(2)}) collective-permute-start(bf16[8,96,128]{2,1,0:T(8,128)(2,1)S(1)} %all_to_all.5.own), channel_id=1, source_target_pairs={{0,8},{8,0},{16,24},{24,16},{1,9},{9,1},{17,25},{25,17},{2,10},{10... | collective-permute-start | bytes 589832 | tf_op jit(solution)/shard_map/ppermute | solution.py:487
  18.3 7.0 %collective-permute-start.2 = (bf16[4,96,128]{2,1,0:T(8,128)(2,1)S(1)}, bf16[4,96,128]{2,1,0:T(8,128)(2,1)S(1)}, u32[]{:S(2)}, u32[]{:S(2)}) collective-permute-start(bf16[4,96,128]{2,1,0:T(8,128)(2,1)S(1)} %get-tuple-element.24), channel_id=1, source_target_pairs={{0,16},{8,24},{16,0},{24,8},{1,17},{9,25},{17,1},{25,9},{2,18},{10... | collective-permute-start | bytes 294920 | tf_op jit(solution)/shard_map/ppermute | solution.py:493
  19.9 6.7 %collective-permute-start.1 = (bf16[4,96,128]{2,1,0:T(8,128)(2,1)S(1)}, bf16[4,96,128]{2,1,0:T(8,128)(2,1)S(1)}, u32[]{:S(2)}, u32[]{:S(2)}) collective-permute-start(bf16[4,96,128]{2,1,0:T(8,128)(2,1)S(1)} %get-tuple-element.25), channel_id=1, source_target_pairs={{0,16},{8,24},{16,0},{24,8},{1,17},{9,25},{17,1},{25,9},{2,18},{10... | collective-permute-start | bytes 294920 | tf_op jit(solution)/shard_map/ppermute | solution.py:493

commit v8 on v7

--- a/solution.py
+++ b/solution.py
@@ -94,8 +94,10 @@
 
 
 def migrated(right, migration, begin, end, first=0):
+    rows = migration[begin // LOAD]
+    shift = begin // LOAD * LOAD
     return lax.dot_general(
-        migration[begin * LY : end * LY, first : first + right.shape[1]],
+        rows[(begin - shift) * LY : (end - shift) * LY, first : first + right.shape[1]],
         right,
         (((1,), (1,)), ((), ())),
         preferred_element_type=jnp.float32,
@@ -132,9 +134,16 @@
         table[index : index + 1, :] = value.astype(jnp.int32)
 
 
+def migration_part(own, source, part, arrived):
+    copy = pltpu.make_async_copy(source.at[: part.shape[0], :], part, arrived)
+    copy.start()
+    copy.wait()
+
+
 def own_kernels(
     choice,
     own,
+    migration_low,
     migration_source,
     column_gain,
     shift_source,
@@ -146,26 +155,22 @@
     table,
     shifts,
     columns,
-    migration,
+    migration_high,
     spread,
     gain_rows,
     arrived,
 ):
-    strips = [(x, x + LOAD) for x in range(0, LX, LOAD)]
     copies = [
-        pltpu.make_async_copy(column_gain, gain_rows, arrived.at[len(strips)]),
-        pltpu.make_async_copy(shift_source, shifts, arrived.at[len(strips) + 1]),
+        pltpu.make_async_copy(column_gain, gain_rows, arrived.at[0]),
+        pltpu.make_async_copy(shift_source, shifts, arrived.at[1]),
+        pltpu.make_async_copy(
+            migration_source.at[LOAD * LY :, :], migration_high, arrived.at[2]
+        ),
     ]
-    for index, (begin, end) in enumerate(strips):
-        rows = pl.ds(begin * LY, (end - begin) * LY)
-        copies.append(
-            pltpu.make_async_copy(
-                migration_source.at[rows, :], migration.at[rows, :], arrived.at[index]
-            )
-        )
+    migration = (migration_low, migration_high)
     for copy in copies:
         copy.start()
-    gap = jnp.zeros((SEGMENT - KZ, migration.shape[1]), jnp.bfloat16)
+    gap = jnp.zeros((SEGMENT - KZ, migration_low.shape[1]), jnp.bfloat16)
     rows = []
     for j in range(PACKED):
         cells = slice(EDGE + j * KZ, EDGE + (j + 1) * KZ)
@@ -195,10 +200,12 @@
     columns[...] = jnp.transpose(gain_rows[...])
     copies[1].wait()
     block_table(shifts, table, spread)
-    for copy, (begin, end) in zip(copies[2:], strips):
-        copy.wait()
-        raw = migrated(right, migration, begin, end)
-        finish(raw, columns, gains[:1], store, begin, end)
+    for begin in range(0, LX, LOAD):
+        if begin:
+            copies[2].wait()
+        for x in range(begin, begin + LOAD, STRIP):
+            raw = migrated(right, migration, x, x + STRIP)
+            finish(raw, columns, gains[:1], store, x, x + STRIP)
     for g in range(GROUPS):
         base = g // BY * KX * KROWS + g % BY * 16 + 8
         power = None
@@ -218,7 +225,8 @@
     return jnp.concatenate([jnp.concatenate(pieces, axis=1), spare])
 
 
-def reference_part(choice, kept, received, migration, partial):
+def reference_part(choice, kept, received, migration_low, migration_high, partial):
+    migration = (migration_low, migration_high)
     right = reference_samples(choice, kept, received, 0)
     for x in range(0, LX, STRIP):
         partial[x * LY : (x + STRIP) * LY, :] = migrated(right, migration, x, x + STRIP)
@@ -237,7 +245,8 @@
     table,
     shift_cells,
     columns,
-    migration,
+    migration_high,
+    migration_low,
     scores,
     displacement,
     volume,
@@ -253,6 +262,7 @@
         base = (x + MARGIN) * NY + MARGIN
         volume[base : base + LY, :] = image
 
+    migration = (migration_low, migration_high)
     first = kept.shape[0] - received.shape[0]
     right = reference_samples(choice, kept, received, first)
     gains = depth_row(choice, kept)[:1]
@@ -461,26 +471,15 @@
     shifts = coarse_shift.transpose(turn)
     own_shapes = [(SPREAD, LANES), (LX * LY, LANES), (LX * LY, LANES)]
     own_shapes += [(2, GROUPS * 8, LANES), (GROUPS * SUMS, LANES)]
-    kernel_arrays = pl.pallas_call(
-        own_kernels,
-        in_specs=[scalars] + on_chip(1) + [pl.BlockSpec(memory_space=pltpu.HBM)] * 3,
-        out_specs=on_chip(9),
-        out_shape=[pltpu.VMEM(shape, jnp.float32) for shape in own_shapes]
-        + [
-            pltpu.VMEM((8, LANES), jnp.int32),
-            pltpu.VMEM(shifts.shape, jnp.int32),
-            pltpu.VMEM((LANES, LX * LY // LANES), jnp.float32),
-            pltpu.VMEM(migration.shape, jnp.bfloat16),
-        ],
-        scratch_shapes=[
-            pltpu.VMEM((2 * BX * PACKED, LANES), jnp.float32),
-            pltpu.VMEM((LX * LY // LANES, LANES), jnp.float32),
-            pltpu.SemaphoreType.DMA((LX // LOAD + 2,)),
-        ],
-        compiler_params=pltpu.CompilerParams(vmem_limit_bytes=16 << 20),
-        name="own_kernels",
-    )(jnp.stack(places), pinned(own), in_hbm(migration), in_hbm(gain_table), in_hbm(shifts))
-
+    low = pl.pallas_call(
+        migration_part,
+        in_specs=on_chip(1) + [pl.BlockSpec(memory_space=pltpu.HBM)],
+        out_specs=on_chip(1)[0],
+        out_shape=pltpu.VMEM((LOAD * LY, elements), jnp.bfloat16),
+        scratch_shapes=[pltpu.SemaphoreType.DMA],
+        compiler_params=pltpu.CompilerParams(vmem_limit_bytes=4 << 20),
+        name="migration_part",
+    )(pinned(own), in_hbm(migration))
     kept = own
     bit = 1
     while bit < frames // 2:
@@ -488,28 +487,56 @@
         mine = (chosen ^ frame) & bit == 0
         kept = jnp.where(mine, kept, received)
         bit *= 2
+    kept, low = lax.optimization_barrier((kept, low))
     half = kept.shape[0] // 2
     received = [
         lax.ppermute(part, "frame", [(i, i ^ bit) for i in range(frames)])
         for part in (kept[:half], kept[half:])
     ]
+    kernel_arrays = pl.pallas_call(
+        own_kernels,
+        in_specs=[scalars] + on_chip(2) + [pl.BlockSpec(memory_space=pltpu.HBM)] * 3,
+        out_specs=on_chip(9),
+        out_shape=[pltpu.VMEM(shape, jnp.float32) for shape in own_shapes]
+        + [
+            pltpu.VMEM((8, LANES), jnp.int32),
+            pltpu.VMEM(shifts.shape, jnp.int32),
+            pltpu.VMEM((LANES, LX * LY // LANES), jnp.float32),
+            pltpu.VMEM((LX * LY - LOAD * LY, elements), jnp.bfloat16),
+        ],
+        scratch_shapes=[
+            pltpu.VMEM((2 * BX * PACKED, LANES), jnp.float32),
+            pltpu.VMEM((LX * LY // LANES, LANES), jnp.float32),
+            pltpu.SemaphoreType.DMA((3,)),
+        ],
+        compiler_params=pltpu.CompilerParams(vmem_limit_bytes=16 << 20),
+        name="own_kernels",
+    )(
+        jnp.stack(places),
+        pinned(own),
+        pinned(low),
+        in_hbm(migration),
+        in_hbm(gain_table),
+        in_hbm(shifts),
+    )
+
     keep = ((chosen ^ frame) & (frames // 2) == 0).astype(jnp.int32)
     choice = jnp.stack([keep] + places)
 
     *kernel_arrays, staged = kernel_arrays
     partial = pl.pallas_call(
         reference_part,
-        in_specs=[scalars] + on_chip(3),
+        in_specs=[scalars] + on_chip(4),
         out_specs=on_chip(1)[0],
         out_shape=pltpu.VMEM((LX * LY, LANES), jnp.float32),
         compiler_params=pltpu.CompilerParams(vmem_limit_bytes=8 << 20),
         name="reference_part",
-    )(choice, pinned(kept), pinned(received[0]), pinned(staged))
+    )(choice, pinned(kept), pinned(received[0]), pinned(low), pinned(staged))
 
     shapes = [jax.ShapeDtypeStruct((n,) + shifts.shape[1:], jnp.float32) for n in (7, 3)]
     scores, displacement = pl.pallas_call(
         track,
-        in_specs=[scalars] + on_chip(12),
+        in_specs=[scalars] + on_chip(13),
         out_specs=on_chip(2),
         out_shape=shapes,
         scratch_shapes=[
@@ -525,7 +552,7 @@
         choice,
         pinned(kept),
         pinned(received[1]),
-        *[pinned(array) for array in [partial, *kernel_arrays, staged]],
+        *[pinned(array) for array in [partial, *kernel_arrays, staged, low]],
     )
     return scores.transpose(turn), displacement.transpose(turn)
 

time: 30.3 us -> 30.4 us (level)
    ppermute x2, waiting for transfers between devices: 0.01 us -> 0.94 us  [per_device(): lax.ppermute(part, 'frame', [(i, i ^ bit) for i in range(frames)])]
    ppermute x1, waiting for transfers between devices: 0.7 us -> 0.01 us  [per_device(): lax.ppermute(kept, 'frame', [(i, i ^ bit) for i in range(frames)])]
    pallas_call x3 -> x4, Pallas kernels: 9.58 us -> 9.34 us  [the longest x1 3.49 us: per_device(): pl.pallas_call(track, in_specs=[scalars] + on_chip(13), out_specs=on_chip...]
  transfers between devices with their start and end apart: 3 -> 3, of which waited for: 1 -> 2; matrix products, arithmetic and copies ran while one was open for 1% -> 1% of each run, Pallas kernels for 20% -> 19%
where the time goes in v8:
time: 30.4 us; the launch traced here: 30.1 us
  blocking collectives  15 us (49%)
  Pallas kernels  10.4 us (34%)
  starting transfers between devices  2.09 us (7%)
  between operations  1.35 us (4%)
  waiting for transfers between devices  0.95 us (3%)
    all_to_all x1, blocking collectives, per_device(): lax.all_to_all(windows, 'slab', split_axis=0, concat_axis=0, tiled=True)  15 us
    pallas_call x1, Pallas kernels, per_device(): pl.pallas_call(track, in_specs=[scalars] + on_chip(13), out_specs=on_chip...  3.49 us
    pallas_call x1, Pallas kernels, per_device(): pl.pallas_call(own_kernels, in_specs=[scalars] + on_chip(2) + [pl.BlockSp...  3.02 us
    ppermute x2, starting transfers between devices, per_device(): lax.ppermute(part, 'frame', [(i, i ^ bit) for i in range(frames)])  2.09 us
    pallas_call x1, Pallas kernels, per_device(): pl.pallas_call(migration_part, in_specs=on_chip(1) + [pl.BlockSpec(memory...  1.6 us
    pallas_call x1, Pallas kernels, per_device(): pl.pallas_call(reference_part, in_specs=[scalars] + on_chip(4), out_specs...  1.23 us
    pallas_call x1, Pallas kernels, per_device(): pl.pallas_call(window_rows, in_specs=[pl.BlockSpec(memory_space=pltpu.HBM...  1.11 us
    ppermute x2, waiting for transfers between devices, per_device(): lax.ppermute(part, 'frame', [(i, i ^ bit) for i in range(frames)])  0.94 us
  transfers between devices with their start and end apart: 3, of which 2 were waited for; matrix products, arithmetic and copies ran while one was open for 1% of the time, Pallas kernels for 19%

profile of v8, /device:TPU:0, one launch (start us, length us, event | category | flops | bytes accessed | tf_op | source)
XLA Modules:
  0.0 30.1 jit_solution(3397840660563803756)
XLA Ops:
  0.6 1.1 %window_rows.1 = bf16[8,96,128]{2,1,0:T(8,128)(2,1)S(1)} custom-call(bf16[128,512]{1,0:T(8,128)(2,1)} %bitcast.12, f32[1,64]{1,0:T(1,128)} %bitcast.15), custom_call_target="tpu_custom_call" | custom-call | tf_op jit(solution)/shard_map/window_rows/pallas_call | solution.py:437
  1.7 15.0 %all_to_all.5.own = bf16[8,96,128]{2,1,0:T(8,128)(2,1)S(1)} all-to-all(bf16[8,96,128]{2,1,0:T(8,128)(2,1)S(1)} %window_rows.1), channel_id=1, replica_groups=mesh['frame'=4,'slab'=8] {'slab'}, dimensions={0} | all-to-all | bytes 393216 | tf_op jit(solution)/shard_map/all_to_all | solution.py:451
  16.8 0.0 collective-permute-start
  17.4 0.1 pad_add_fusion.1.choice
  17.5 1.6 %migration_part.1.migration_low = bf16[1024,1024]{1,0:T(8,128)(2,1)S(1)} custom-call(bf16[8,96,128]{2,1,0:T(8,128)(2,1)S(1)} %all_to_all.5.own, bf16[2048,1024]{1,0:T(8,128)(2,1)} %migration_source.1), custom_call_target="tpu_custom_call" | custom-call | tf_op jit(solution)/shard_map/migration_part/pallas_call | solution.py:474
  19.1 0.0 collective-permute-done
  19.2 1.6 %collective-permute-start.2 = (bf16[4,96,128]{2,1,0:T(8,128)(2,1)S(1)}, bf16[4,96,128]{2,1,0:T(8,128)(2,1)S(1)}, u32[]{:S(2)}, u32[]{:S(2)}) collective-permute-start(bf16[4,96,128]{2,1,0:T(8,128)(2,1)S(1)} %get-tuple-element.28), channel_id=1, source_target_pairs={{0,16},{8,24},{16,0},{24,8},{1,17},{9,25},{17,1},{25,9},{2,18},{10... | collective-permute-start | bytes 294920 | tf_op jit(solution)/shard_map/ppermute | solution.py:493
  20.8 0.5 %collective-permute-start.1 = (bf16[4,96,128]{2,1,0:T(8,128)(2,1)S(1)}, bf16[4,96,128]{2,1,0:T(8,128)(2,1)S(1)}, u32[]{:S(2)}, u32[]{:S(2)}) collective-permute-start(bf16[4,96,128]{2,1,0:T(8,128)(2,1)S(1)} %get-tuple-element.29), channel_id=1, source_target_pairs={{0,16},{8,24},{16,0},{24,8},{1,17},{9,25},{17,1},{25,9},{2,18},{10... | collective-permute-start | bytes 294920 | tf_op jit(solution)/shard_map/ppermute | solution.py:493
  21.3 0.1 pad_add_fusion.choice
  21.4 3.0 %own_kernels.1 = (f32[4647,128]{1,0:T(8,128)S(1)}, f32[2048,128]{1,0:T(8,128)S(1)}, f32[2048,128]{1,0:T(8,128)S(1)}, f32[2,256,128]{2,1,0:T(8,128)S(1)}, f32[288...) custom-call(s32[3]{0:T(128)S(1)} %pad_add_fusion.1.choice, ...), custom_call_target="tpu_custom_call" | custom-call | tf_op jit(solution)/shard_map/own_kernels/pallas_call | solution.py:496
  24.4 0.5 %collective-permute-done.2.received = bf16[4,96,128]{2,1,0:T(8,128)(2,1)S(1)} collective-permute-done((bf16[4,96,128]{2,1,0:T(8,128)(2,1)S(1)}, bf16[4,96,128]{2,1,0:T(8,128)(2,1)S(1)}, u32[]{:S(2)}, u32[]{:S(2)}) %collective-permute-start.2) | collective-permute-done | bytes 98336 | tf_op jit(solution)/shard_map/ppermute | solution.py:493
  24.9 1.2 %reference_part.1.partial = f32[2048,128]{1,0:T(8,128)S(1)} custom-call(s32[4]{0:T(128)S(1)} %pad_add_fusion.choice, bf16[8,96,128]{2,1,0:T(8,128)(2,1)S(1)} %broadcast_select_fusion.kept, bf16[4,96,128]{2,1,0:T(8,128)(2,1)S(1)} %collective-permute-done.2.received, bf16[1024,1024]{1,0:T(8,128)(2,1)S(1)} %migration_part.1.migration_low, ...), custom_call_target="tpu_custom_call" | custom-call | tf_op jit(solution)/shard_map/reference_part/pallas_call | solution.py:527
  26.2 0.4 %collective-permute-done.1.received = bf16[4,96,128]{2,1,0:T(8,128)(2,1)S(1)} collective-permute-done((bf16[4,96,128]{2,1,0:T(8,128)(2,1)S(1)}, bf16[4,96,128]{2,1,0:T(8,128)(2,1)S(1)}, u32[]{:S(2)}, u32[]{:S(2)}) %collective-permute-start.1) | collective-permute-done | bytes 98336 | tf_op jit(solution)/shard_map/ppermute | solution.py:493
  26.6 3.5 %track.1 = (f32[7,1,4,4,8]{4,3,2,1,0:T(4,128)}, f32[3,1,4,4,8]{4,3,2,1,0:T(4,128)}) custom-call(s32[4]{0:T(128)S(1)} %pad_add_fusion.choice, bf16[8,96,128]{2,1,0:T(8,128)(2,1)S(1)} %broadcast_select_fusion.kept, bf16[4,96,128]{2,1,0:T(8,128)(2,1)S(1)} %collective-permute-done.1.received, f32[2048,128]{1,0:T(8,128)S(1)} %reference_part.1.partial, ...), custom_call_target="tpu_custom_call" | custom-call | tf_op jit(solution)/shard_map/track/pallas_call | solution.py:537
  (2 shorter events, 0.0 us)
Async XLA Ops:
  16.8 2.4 %collective-permute-start = (bf16[8,96,128]{2,1,0:T(8,128)(2,1)S(1)}, bf16[8,96,128]{2,1,0:T(8,128)(2,1)S(1)}, u32[]{:S(2)}, u32[]{:S(2)}) collective-permute-start(bf16[8,96,128]{2,1,0:T(8,128)(2,1)S(1)} %all_to_all.5.own), channel_id=1, source_target_pairs={{0,8},{8,0},{16,24},{24,16},{1,9},{9,1},{17,25},{25,17},{2,10},{10... | collective-permute-start | bytes 589832 | tf_op jit(solution)/shard_map/ppermute | solution.py:486
  19.2 5.7 %collective-permute-start.2 = (bf16[4,96,128]{2,1,0:T(8,128)(2,1)S(1)}, bf16[4,96,128]{2,1,0:T(8,128)(2,1)S(1)}, u32[]{:S(2)}, u32[]{:S(2)}) collective-permute-start(bf16[4,96,128]{2,1,0:T(8,128)(2,1)S(1)} %get-tuple-element.28), channel_id=1, source_target_pairs={{0,16},{8,24},{16,0},{24,8},{1,17},{9,25},{17,1},{25,9},{2,18},{10... | collective-permute-start | bytes 294920 | tf_op jit(solution)/shard_map/ppermute | solution.py:493
  20.8 5.8 %collective-permute-start.1 = (bf16[4,96,128]{2,1,0:T(8,128)(2,1)S(1)}, bf16[4,96,128]{2,1,0:T(8,128)(2,1)S(1)}, u32[]{:S(2)}, u32[]{:S(2)}) collective-permute-start(bf16[4,96,128]{2,1,0:T(8,128)(2,1)S(1)} %get-tuple-element.29), channel_id=1, source_target_pairs={{0,16},{8,24},{16,0},{24,8},{1,17},{9,25},{17,1},{25,9},{2,18},{10... | collective-permute-start | bytes 294920 | tf_op jit(solution)/shard_map/ppermute | solution.py:493

commit v9 on v6

--- a/solution.py
+++ b/solution.py
@@ -230,13 +230,6 @@
     positions = pltpu.make_async_copy(table, block, arrived)
     positions.start()
     keep = choice[0] == 1
-    zero = jnp.zeros((NY, LANES), jnp.float32)
-    for x in list(range(MARGIN)) + list(range(LX + MARGIN, NX)):
-        volume[x * NY : (x + 1) * NY, :] = zero
-    for x in range(MARGIN, LX + MARGIN):
-        volume[x * NY : x * NY + MARGIN, :] = zero[:MARGIN]
-        volume[x * NY + MARGIN + LY : (x + 1) * NY, :] = zero[: NY - MARGIN - LY]
-
     def store(x, image):
         base = (x + MARGIN) * NY + MARGIN
         volume[base : base + LY, :] = image
@@ -312,6 +305,12 @@
 
     for x in range(0, LX, STRIP):
         migrate(right, migration, columns, gains, store, x, x + STRIP)
+    zero = jnp.zeros((NY, LANES), jnp.float32)
+    for x in list(range(MARGIN)) + list(range(LX + MARGIN, NX)):
+        volume[x * NY : (x + 1) * NY, :] = zero
+    for x in range(MARGIN, LX + MARGIN):
+        volume[x * NY : x * NY + MARGIN, :] = zero[:MARGIN]
+        volume[x * NY + MARGIN + LY : (x + 1) * NY, :] = zero[: NY - MARGIN - LY]
     positions.wait()
     for bx in range(BX):
         for by in range(BY):

time: 29.5 us -> 29.5 us (level)
  transfers between devices with their start and end apart: 2 -> 2, of which waited for: 2 -> 2; matrix products, arithmetic and copies ran while one was open for 1% -> 1% of each run, Pallas kernels for 16% -> 17%
where the time goes in v9:
time: 29.5 us; the launch traced here: 29.2 us
  blocking collectives  15 us (51%)
  Pallas kernels  9.91 us (34%)
  starting transfers between devices  1.59 us (5%)
  between operations  1.31 us (4%)
  waiting for transfers between devices  1.22 us (4%)
    all_to_all x1, blocking collectives, per_device(): lax.all_to_all(windows, 'slab', split_axis=0, concat_axis=0, tiled=True)  15 us
    pallas_call x1, Pallas kernels, per_device(): pl.pallas_call(own_kernels, in_specs=[scalars] + on_chip(1) + [pl.BlockSp...  4.82 us
    pallas_call x1, Pallas kernels, per_device(): pl.pallas_call(track, in_specs=[scalars] + on_chip(11), out_specs=on_chip...  3.98 us
    ppermute x2, starting transfers between devices, per_device(): lax.ppermute(kept, 'frame', [(i, i ^ bit) for i in range(frames)])  1.59 us
    ppermute x2, waiting for transfers between devices, per_device(): lax.ppermute(kept, 'frame', [(i, i ^ bit) for i in range(frames)])  1.22 us
    pallas_call x1, Pallas kernels, per_device(): pl.pallas_call(window_rows, in_specs=[pl.BlockSpec(memory_space=pltpu.HBM...  1.11 us
  transfers between devices with their start and end apart: 2, of which 2 were waited for; matrix products, arithmetic and copies ran while one was open for 1% of the time, Pallas kernels for 17%

profile of v9, /device:TPU:0, one launch (start us, length us, event | category | flops | bytes accessed | tf_op | source)
XLA Modules:
  0.0 29.2 jit_solution(14223725456225526542)
XLA Ops:
  0.6 1.1 %window_rows.1 = bf16[8,96,128]{2,1,0:T(8,128)(2,1)S(1)} custom-call(bf16[128,512]{1,0:T(8,128)(2,1)} %bitcast.12, f32[1,64]{1,0:T(1,128)} %bitcast.15), custom_call_target="tpu_custom_call" | custom-call | tf_op jit(solution)/shard_map/window_rows/pallas_call | solution.py:407
  1.7 15.0 %all_to_all.5.own = bf16[8,96,128]{2,1,0:T(8,128)(2,1)S(1)} all-to-all(bf16[8,96,128]{2,1,0:T(8,128)(2,1)S(1)} %window_rows.1), channel_id=1, replica_groups=mesh['frame'=4,'slab'=8] {'slab'}, dimensions={0} | all-to-all | bytes 393216 | tf_op jit(solution)/shard_map/all_to_all | solution.py:421
  16.8 0.0 collective-permute-start
  17.4 0.8 %collective-permute-done = bf16[8,96,128]{2,1,0:T(8,128)(2,1)S(1)} collective-permute-done((bf16[8,96,128]{2,1,0:T(8,128)(2,1)S(1)}, bf16[8,96,128]{2,1,0:T(8,128)(2,1)S(1)}, u32[]{:S(2)}, u32[]{:S(2)}) %collective-permute-start) | collective-permute-done | bytes 196640 | tf_op jit(solution)/shard_map/ppermute | solution.py:471
  18.2 1.6 %collective-permute-start.1 = (bf16[8,96,128]{2,1,0:T(8,128)(2,1)S(1)}, bf16[8,96,128]{2,1,0:T(8,128)(2,1)S(1)}, u32[]{:S(2)}, u32[]{:S(2)}) collective-permute-start(bf16[8,96,128]{2,1,0:T(8,128)(2,1)S(1)} %broadcast_select_fusion.kept), channel_id=1, source_target_pairs={{0,16},{8,24},{16,0},{24,8},{1,17},{9,25},{17,1},{25,9},{2,18},{10... | collective-permute-start | bytes 589832 | tf_op jit(solution)/shard_map/ppermute | solution.py:471
  19.8 0.1 pad_add_fusion.1.choice
  19.9 0.1 pad_add_fusion.choice
  20.0 4.8 %own_kernels.1 = (f32[4647,128]{1,0:T(8,128)S(1)}, f32[2048,128]{1,0:T(8,128)S(1)}, f32[2048,128]{1,0:T(8,128)S(1)}, f32[2,256,128]{2,1,0:T(8,128)S(1)}, f32[288...) custom-call(s32[3]{0:T(128)S(1)} %pad_add_fusion.1.choice, ...), custom_call_target="tpu_custom_call" | custom-call | tf_op jit(solution)/shard_map/own_kernels/pallas_call | solution.py:444
  24.8 0.4 %collective-permute-done.1.received = bf16[8,96,128]{2,1,0:T(8,128)(2,1)S(1)} collective-permute-done((bf16[8,96,128]{2,1,0:T(8,128)(2,1)S(1)}, bf16[8,96,128]{2,1,0:T(8,128)(2,1)S(1)}, u32[]{:S(2)}, u32[]{:S(2)}) %collective-permute-start.1) | collective-permute-done | bytes 196640 | tf_op jit(solution)/shard_map/ppermute | solution.py:471
  25.3 4.0 %track.1 = (f32[7,1,4,4,8]{4,3,2,1,0:T(4,128)}, f32[3,1,4,4,8]{4,3,2,1,0:T(4,128)}) custom-call(s32[4]{0:T(128)S(1)} %pad_add_fusion.choice, bf16[8,96,128]{2,1,0:T(8,128)(2,1)S(1)} %broadcast_select_fusion.kept, bf16[8,96,128]{2,1,0:T(8,128)(2,1)S(1)} %collective-permute-done.1.received, f32[4647,128]{1,0:T(8,128)S(1)} %get-tuple-element.13.kernels, ...), custom_call_target="tpu_custom_call" | custom-call | tf_op jit(solution)/shard_map/track/pallas_call | solution.py:477
  (1 shorter events, 0.0 us)
Async XLA Ops:
  16.8 1.4 %collective-permute-start = (bf16[8,96,128]{2,1,0:T(8,128)(2,1)S(1)}, bf16[8,96,128]{2,1,0:T(8,128)(2,1)S(1)}, u32[]{:S(2)}, u32[]{:S(2)}) collective-permute-start(bf16[8,96,128]{2,1,0:T(8,128)(2,1)S(1)} %all_to_all.5.own), channel_id=1, source_target_pairs={{0,8},{8,0},{16,24},{24,16},{1,9},{9,1},{17,25},{25,17},{2,10},{10... | collective-permute-start | bytes 589832 | tf_op jit(solution)/shard_map/ppermute | solution.py:471
  18.2 7.0 %collective-permute-start.1 = (bf16[8,96,128]{2,1,0:T(8,128)(2,1)S(1)}, bf16[8,96,128]{2,1,0:T(8,128)(2,1)S(1)}, u32[]{:S(2)}, u32[]{:S(2)}) collective-permute-start(bf16[8,96,128]{2,1,0:T(8,128)(2,1)S(1)} %broadcast_select_fusion.kept), channel_id=1, source_target_pairs={{0,16},{8,24},{16,0},{24,8},{1,17},{9,25},{17,1},{25,9},{2,18},{10... | collective-permute-start | bytes 589832 | tf_op jit(solution)/shard_map/ppermute | solution.py:471
